TPU v7x, 32 devices: a whole 2x2x4 slice. The times are simulated.
32 devices in a mesh: dp: 4 (over y, x), fsdp: 8 (over z, core).
Axes of the slice: x: 2, y: 2, z: 4, core: 2. Of those that a mesh axis runs over, the one named last changes fastest.
Arguments:
- frames: bfloat16 [4096, 1024], P(('dp', 'fsdp')), may hold values from -6 to 6
- segments: int32 [4096], P(('dp', 'fsdp')), may hold values from 0 to 3, as said below
- cotangent: bfloat16 [4096, 1024], P(('dp', 'fsdp')), may hold values from -6 to 6
- early_gain: bfloat16 [1024], P(('dp', 'fsdp')), may hold values from 0.5 to 1.5
- early_shift: bfloat16 [1024], P(('dp', 'fsdp')), may hold values from -1.25 to 1.25
- early_up: bfloat16 [1024, 4096], P(('dp', 'fsdp')), may hold values from -0.1875 to 0.1875
- early_lift: bfloat16 [4096], P(('dp', 'fsdp')), may hold values from -1.25 to 1.25
- early_down: bfloat16 [4096, 1024], P(('dp', 'fsdp')), may hold values from -0.09375 to 0.09375
- early_drop: bfloat16 [1024], P(('dp', 'fsdp')), may hold values from -1.25 to 1.25
- mixer_gain: bfloat16 [1024], P(('dp', 'fsdp')), may hold values from 0.5 to 1.5
- mixer_shift: bfloat16 [1024], P(('dp', 'fsdp')), may hold values from -1.25 to 1.25
- mixer_project: bfloat16 [1024, 3072], P(('dp', 'fsdp')), may hold values from -0.1875 to 0.1875
- query_bias: bfloat16 [1024], P(('dp', 'fsdp')), may hold values from -1.25 to 1.25
- value_bias: bfloat16 [1024], P(('dp', 'fsdp')), may hold values from -1.25 to 1.25
- mixer_output: bfloat16 [1024, 1024], P(('dp', 'fsdp')), may hold values from -1.5 to 1.5
- mixer_drop: bfloat16 [1024], P(('dp', 'fsdp')), may hold values from -1.25 to 1.25
- distance_table: bfloat16 [256, 16], P(('dp', 'fsdp')), may hold values from -6 to 6
- filter_gain: bfloat16 [1024], P(('dp', 'fsdp')), may hold values from 0.5 to 1.5
- filter_shift: bfloat16 [1024], P(('dp', 'fsdp')), may hold values from -1.25 to 1.25
- filter_up: bfloat16 [1024, 2048], P(('dp', 'fsdp')), may hold values from -0.1875 to 0.1875
- filter_lift: bfloat16 [2048], P(('dp', 'fsdp')), may hold values from -1.25 to 1.25
- depth_weight: bfloat16 [1024, 31], P(('dp', 'fsdp')), may hold values from -1 to 1
- depth_bias: bfloat16 [1024], P(('dp', 'fsdp')), may hold values from -1.75 to 1.75
- middle_gain: bfloat16 [1024], P(('dp', 'fsdp')), may hold values from 0.5 to 1.5
- middle_shift: bfloat16 [1024], P(('dp', 'fsdp')), may hold values from -1.25 to 1.25
- filter_down: bfloat16 [1024, 1024], P(('dp', 'fsdp')), may hold values from -0.1875 to 0.1875
- filter_drop: bfloat16 [1024], P(('dp', 'fsdp')), may hold values from -1.25 to 1.25
- late_gain: bfloat16 [1024], P(('dp', 'fsdp')), may hold values from 0.5 to 1.5
- late_shift: bfloat16 [1024], P(('dp', 'fsdp')), may hold values from -1.25 to 1.25
- late_up: bfloat16 [1024, 4096], P(('dp', 'fsdp')), may hold values from -0.1875 to 0.1875
- late_lift: bfloat16 [4096], P(('dp', 'fsdp')), may hold values from -1.25 to 1.25
- late_down: bfloat16 [4096, 1024], P(('dp', 'fsdp')), may hold values from -0.09375 to 0.09375
- late_drop: bfloat16 [1024], P(('dp', 'fsdp')), may hold values from -2.5 to 2.5
- final_gain: bfloat16 [1024], P(('dp', 'fsdp')), may hold values from 0.5 to 1.5
- final_shift: bfloat16 [1024], P(('dp', 'fsdp')), may hold values from -1.25 to 1.25
Outputs:
- layer_out: float32 [4096, 1024], P(('dp', 'fsdp'))
- slope_frames: float32 [4096, 1024], P(('dp', 'fsdp'))
- slope_early_gain: float32 [1024], P(('dp', 'fsdp'))
- slope_early_shift: float32 [1024], P(('dp', 'fsdp'))
- slope_early_up: float32 [1024, 4096], P(('dp', 'fsdp'))
- slope_early_lift: float32 [4096], P(('dp', 'fsdp'))
- slope_early_down: float32 [4096, 1024], P(('dp', 'fsdp'))
- slope_early_drop: float32 [1024], P(('dp', 'fsdp'))
- slope_mixer_gain: float32 [1024], P(('dp', 'fsdp'))
- slope_mixer_shift: float32 [1024], P(('dp', 'fsdp'))
- slope_mixer_project: float32 [1024, 3072], P(('dp', 'fsdp'))
- slope_query_bias: float32 [1024], P(('dp', 'fsdp'))
- slope_value_bias: float32 [1024], P(('dp', 'fsdp'))
- slope_mixer_output: float32 [1024, 1024], P(('dp', 'fsdp'))
- slope_mixer_drop: float32 [1024], P(('dp', 'fsdp'))
- slope_distance_table: float32 [256, 16], P(('dp', 'fsdp'))
- slope_filter_gain: float32 [1024], P(('dp', 'fsdp'))
- slope_filter_shift: float32 [1024], P(('dp', 'fsdp'))
- slope_filter_up: float32 [1024, 2048], P(('dp', 'fsdp'))
- slope_filter_lift: float32 [2048], P(('dp', 'fsdp'))
- slope_depth_weight: float32 [1024, 31], P(('dp', 'fsdp'))
- slope_depth_bias: float32 [1024], P(('dp', 'fsdp'))
- slope_middle_gain: float32 [1024], P(('dp', 'fsdp'))
- slope_middle_shift: float32 [1024], P(('dp', 'fsdp'))
- slope_filter_down: float32 [1024, 1024], P(('dp', 'fsdp'))
- slope_filter_drop: float32 [1024], P(('dp', 'fsdp'))
- slope_late_gain: float32 [1024], P(('dp', 'fsdp'))
- slope_late_shift: float32 [1024], P(('dp', 'fsdp'))
- slope_late_up: float32 [1024, 4096], P(('dp', 'fsdp'))
- slope_late_lift: float32 [4096], P(('dp', 'fsdp'))
- slope_late_down: float32 [4096, 1024], P(('dp', 'fsdp'))
- slope_late_drop: float32 [1024], P(('dp', 'fsdp'))
- slope_final_gain: float32 [1024], P(('dp', 'fsdp'))
- slope_final_shift: float32 [1024], P(('dp', 'fsdp'))
Inputs may be any that keep to these rules, and one draw needn't show every extreme that they name: `segments`: within each device's 4096 / 32 frames the numbers start at 0 and never fall; a device holds one utterance (all 0) or four, each one frame or longer; some device holds four.
All inputs are finite; a program needn't handle non-finite values.
Results may differ from a plain program's by a relative error of at most 0.017.
Values may be sent and summed in bfloat16 or wider, within the bound.
A program may use at most 384 MiB of HBM per device.

v0:
```python
import jax
import jax.numpy as jnp
from jax import lax
from jax.sharding import PartitionSpec as P

D = 1024
HEADS = 16
HEAD = 64
KW = 31
NREL = 256


EPSILON = 1e-05
MASKED = -1e30
UTTERANCE_LIMIT = 4


def flat_dot(left_rows, right_rows):
    return jnp.dot(left_rows, right_rows, preferred_element_type=jnp.float32)


def lead_dot(left_rows, right_rows):
    return lax.dot_general(
        left_rows, right_rows, (((0,), (0,)), ((), ())), preferred_element_type=jnp.float32
    )


def back_dot(left_rows, right_rows):
    return lax.dot_general(
        left_rows, right_rows, (((1,), (1,)), ((), ())), preferred_element_type=jnp.float32
    )


def norm_apply(values, norm_gain, norm_shift):
    centered = values - jnp.mean(values, axis=-1, keepdims=True)
    inverse = lax.rsqrt(jnp.mean(centered * centered, axis=-1, keepdims=True) + EPSILON)
    normed_unit = centered * inverse
    return (
        normed_unit * norm_gain.astype(jnp.float32) + norm_shift.astype(jnp.float32),
        normed_unit,
        inverse,
    )


def norm_back(upstream, normed_unit, inverse, norm_gain):
    scaled = upstream * norm_gain.astype(jnp.float32)
    adjusted = scaled - jnp.mean(scaled, axis=-1, keepdims=True)
    adjusted = adjusted - normed_unit * jnp.mean(scaled * normed_unit, axis=-1, keepdims=True)
    return (inverse * adjusted, jnp.sum(upstream * normed_unit, axis=0), jnp.sum(upstream, axis=0))


def swish_back(upstream, before):
    sigmoid_rows = jax.nn.sigmoid(before)
    return upstream * sigmoid_rows * (1.0 + before * (1.0 - sigmoid_rows))


def depthwise(gated_rows, kernel, segment_ids):
    margin = (KW - 1) // 2
    channels = gated_rows.shape[1]
    taps = jnp.transpose(kernel)[:, None, :]
    running = jnp.zeros_like(gated_rows)
    for utterance in range(UTTERANCE_LIMIT):
        inside = (segment_ids == utterance)[:, None]
        masked_rows = jnp.where(inside, gated_rows, 0.0)
        convolved = lax.conv_general_dilated(
            masked_rows[None],
            taps,
            (1,),
            ((margin, margin),),
            dimension_numbers=("NWC", "WIO", "NWC"),
            feature_group_count=channels,
            precision=lax.Precision.HIGHEST,
        )[0]
        running = running + jnp.where(inside, convolved, 0.0)
    return running


def fetch_feed(norm_gain, norm_shift, w_up, up_shift, w_down, down_shift):
    return (
        lax.all_gather(norm_gain, ("dp", "fsdp"), axis=0, tiled=True),
        lax.all_gather(norm_shift, ("dp", "fsdp"), axis=0, tiled=True),
        lax.all_gather(w_up, ("dp", "fsdp"), axis=0, tiled=True),
        lax.all_gather(up_shift, ("dp", "fsdp"), axis=0, tiled=True),
        lax.all_gather(w_down, ("dp", "fsdp"), axis=0, tiled=True),
        lax.all_gather(down_shift, ("dp", "fsdp"), axis=0, tiled=True),
    )


def reduce_feed(norm_gain, norm_shift, w_up, up_shift, w_down, down_shift):
    return (
        lax.psum_scatter(norm_gain, ("dp", "fsdp"), scatter_dimension=0, tiled=True),
        lax.psum_scatter(norm_shift, ("dp", "fsdp"), scatter_dimension=0, tiled=True),
        lax.psum_scatter(w_up, ("dp", "fsdp"), scatter_dimension=0, tiled=True),
        lax.psum_scatter(up_shift, ("dp", "fsdp"), scatter_dimension=0, tiled=True),
        lax.psum_scatter(w_down, ("dp", "fsdp"), scatter_dimension=0, tiled=True),
        lax.psum_scatter(down_shift, ("dp", "fsdp"), scatter_dimension=0, tiled=True),
    )


def fetch_mixer(
    norm_gain, norm_shift, w_project, query_shift, value_shift, w_output, output_shift, table_rows
):
    return (
        lax.all_gather(norm_gain, ("dp", "fsdp"), axis=0, tiled=True),
        lax.all_gather(norm_shift, ("dp", "fsdp"), axis=0, tiled=True),
        lax.all_gather(w_project, ("dp", "fsdp"), axis=0, tiled=True),
        lax.all_gather(query_shift, ("dp", "fsdp"), axis=0, tiled=True),
        lax.all_gather(value_shift, ("dp", "fsdp"), axis=0, tiled=True),
        lax.all_gather(w_output, ("dp", "fsdp"), axis=0, tiled=True),
        lax.all_gather(output_shift, ("dp", "fsdp"), axis=0, tiled=True),
        lax.all_gather(table_rows, ("dp", "fsdp"), axis=0, tiled=True),
    )


def reduce_mixer(
    norm_gain, norm_shift, w_project, query_shift, value_shift, w_output, output_shift, table_rows
):
    return (
        lax.psum_scatter(norm_gain, ("dp", "fsdp"), scatter_dimension=0, tiled=True),
        lax.psum_scatter(norm_shift, ("dp", "fsdp"), scatter_dimension=0, tiled=True),
        lax.psum_scatter(w_project, ("dp", "fsdp"), scatter_dimension=0, tiled=True),
        lax.psum_scatter(query_shift, ("dp", "fsdp"), scatter_dimension=0, tiled=True),
        lax.psum_scatter(value_shift, ("dp", "fsdp"), scatter_dimension=0, tiled=True),
        lax.psum_scatter(w_output, ("dp", "fsdp"), scatter_dimension=0, tiled=True),
        lax.psum_scatter(output_shift, ("dp", "fsdp"), scatter_dimension=0, tiled=True),
        lax.psum_scatter(table_rows, ("dp", "fsdp"), scatter_dimension=0, tiled=True),
    )


def fetch_filter(
    norm_gain,
    norm_shift,
    w_up,
    up_shift,
    depth_taps,
    depth_shift,
    middle_gain,
    middle_shift,
    w_down,
    down_shift,
    last_gain,
    last_shift,
):
    return (
        lax.all_gather(norm_gain, ("dp", "fsdp"), axis=0, tiled=True),
        lax.all_gather(norm_shift, ("dp", "fsdp"), axis=0, tiled=True),
        lax.all_gather(w_up, ("dp", "fsdp"), axis=0, tiled=True),
        lax.all_gather(up_shift, ("dp", "fsdp"), axis=0, tiled=True),
        lax.all_gather(depth_taps, ("dp", "fsdp"), axis=0, tiled=True),
        lax.all_gather(depth_shift, ("dp", "fsdp"), axis=0, tiled=True),
        lax.all_gather(middle_gain, ("dp", "fsdp"), axis=0, tiled=True),
        lax.all_gather(middle_shift, ("dp", "fsdp"), axis=0, tiled=True),
        lax.all_gather(w_down, ("dp", "fsdp"), axis=0, tiled=True),
        lax.all_gather(down_shift, ("dp", "fsdp"), axis=0, tiled=True),
        lax.all_gather(last_gain, ("dp", "fsdp"), axis=0, tiled=True),
        lax.all_gather(last_shift, ("dp", "fsdp"), axis=0, tiled=True),
    )


def reduce_filter(
    norm_gain,
    norm_shift,
    w_up,
    up_shift,
    depth_taps,
    depth_shift,
    middle_gain,
    middle_shift,
    w_down,
    down_shift,
    last_gain,
    last_shift,
):
    return (
        lax.psum_scatter(norm_gain, ("dp", "fsdp"), scatter_dimension=0, tiled=True),
        lax.psum_scatter(norm_shift, ("dp", "fsdp"), scatter_dimension=0, tiled=True),
        lax.psum_scatter(w_up, ("dp", "fsdp"), scatter_dimension=0, tiled=True),
        lax.psum_scatter(up_shift, ("dp", "fsdp"), scatter_dimension=0, tiled=True),
        lax.psum_scatter(depth_taps, ("dp", "fsdp"), scatter_dimension=0, tiled=True),
        lax.psum_scatter(depth_shift, ("dp", "fsdp"), scatter_dimension=0, tiled=True),
        lax.psum_scatter(middle_gain, ("dp", "fsdp"), scatter_dimension=0, tiled=True),
        lax.psum_scatter(middle_shift, ("dp", "fsdp"), scatter_dimension=0, tiled=True),
        lax.psum_scatter(w_down, ("dp", "fsdp"), scatter_dimension=0, tiled=True),
        lax.psum_scatter(down_shift, ("dp", "fsdp"), scatter_dimension=0, tiled=True),
        lax.psum_scatter(last_gain, ("dp", "fsdp"), scatter_dimension=0, tiled=True),
        lax.psum_scatter(last_shift, ("dp", "fsdp"), scatter_dimension=0, tiled=True),
    )


def feed_forward(values, weights):
    normed, normed_unit, inverse = norm_apply(values, weights[0], weights[1])
    hidden = normed.astype(jnp.bfloat16)
    widened = flat_dot(hidden, weights[2]) + weights[3].astype(jnp.float32)
    active = (widened * jax.nn.sigmoid(widened)).astype(jnp.bfloat16)
    result = values + 0.5 * (flat_dot(active, weights[4]) + weights[5].astype(jnp.float32))
    return (result, (normed_unit, inverse, hidden, widened, active))


def feed_backward(upstream, saved, weights):
    normed_unit, inverse, hidden, widened, active = saved
    half_grad = 0.5 * upstream
    half_low = half_grad.astype(jnp.bfloat16)
    down_slope = lead_dot(active, half_low)
    widened_grad = swish_back(back_dot(half_low, weights[4]), widened)
    widened_low = widened_grad.astype(jnp.bfloat16)
    up_slope = lead_dot(hidden, widened_low)
    hidden_grad = back_dot(widened_low, weights[2])
    input_grad, gain_slope, shift_slope = norm_back(hidden_grad, normed_unit, inverse, weights[0])
    slopes = (
        gain_slope,
        shift_slope,
        up_slope,
        jnp.sum(widened_grad, axis=0),
        down_slope,
        jnp.sum(half_grad, axis=0),
    )
    return (upstream + input_grad, slopes)


def bucket_table(frame_count):
    offsets = jnp.arange(2 * frame_count - 1, dtype=jnp.int32) - (frame_count - 1)
    buckets = jnp.clip(offsets, -(NREL // 2), NREL // 2 - 1) + NREL // 2
    return (buckets[:, None] == jnp.arange(NREL, dtype=jnp.int32)[None, :]).astype(jnp.float32)


def relative_bias(table_rows, frame_count):
    diagonals = jnp.dot(
        bucket_table(frame_count),
        table_rows.astype(jnp.float32),
        precision=lax.Precision.HIGHEST,
        preferred_element_type=jnp.float32,
    )
    flipped = jnp.concatenate(
        [jnp.transpose(diagonals[::-1]), jnp.zeros((HEADS, 1), jnp.float32)], axis=1
    )
    spread = jnp.broadcast_to(flipped[:, None, :], (HEADS, frame_count, 2 * frame_count))
    spread = spread.reshape(HEADS, 2 * frame_count * frame_count)
    sheared = spread[:, : frame_count * (2 * frame_count - 1)].reshape(
        HEADS, frame_count, 2 * frame_count - 1
    )
    return sheared[:, :, frame_count - 1 :]


def relative_slope(score_grad, frame_count):
    placed = jnp.pad(score_grad, ((0, 0), (0, 0), (frame_count - 1, 0)))
    flattened = jnp.pad(
        placed.reshape(HEADS, frame_count * (2 * frame_count - 1)), ((0, 0), (0, frame_count))
    )
    columns = jnp.sum(flattened.reshape(HEADS, frame_count, 2 * frame_count), axis=1)
    diagonals = columns[:, 2 * frame_count - 2 :: -1]
    return lax.dot_general(
        bucket_table(frame_count),
        diagonals,
        (((0,), (1,)), ((), ())),
        precision=lax.Precision.HIGHEST,
        preferred_element_type=jnp.float32,
    )


def mixer_scores(query_rows, key_matrix_rows, relative, same_utterance):
    unnormalized_scores = jnp.einsum(
        "jug,fug->ujf", query_rows, key_matrix_rows, preferred_element_type=jnp.float32
    )
    return jnp.where(same_utterance[None], HEAD ** (-0.5) * unnormalized_scores + relative, MASKED)


def mixer_forward(values, segment_ids, weights):
    frame_count = values.shape[0]
    normed, normed_unit, inverse = norm_apply(values, weights[0], weights[1])
    hidden = normed.astype(jnp.bfloat16)
    projected = flat_dot(hidden, weights[2])
    query_rows = (projected[:, :D] + weights[3].astype(jnp.float32)).astype(jnp.bfloat16)
    query_rows = query_rows.reshape(frame_count, HEADS, HEAD)
    key_matrix_rows = projected[:, D : 2 * D].astype(jnp.bfloat16).reshape(frame_count, HEADS, HEAD)
    value_matrix_rows = (projected[:, 2 * D :] + weights[4].astype(jnp.float32)).astype(
        jnp.bfloat16
    )
    value_matrix_rows = value_matrix_rows.reshape(frame_count, HEADS, HEAD)
    relative = relative_bias(weights[7], frame_count)
    same_utterance = segment_ids[:, None] == segment_ids[None, :]
    scores = mixer_scores(query_rows, key_matrix_rows, relative, same_utterance)
    row_peak = jnp.max(scores, axis=-1, keepdims=True)
    powered = jnp.exp(scores - row_peak)
    row_total = jnp.sum(powered, axis=-1, keepdims=True)
    log_total = row_peak + jnp.log(row_total)
    softmax_rows = (powered / row_total).astype(jnp.bfloat16)
    attention_blend = jnp.einsum(
        "ief,fiv->eiv", softmax_rows, value_matrix_rows, preferred_element_type=jnp.float32
    )
    attention_blend = attention_blend.reshape(frame_count, D).astype(jnp.bfloat16)
    result = values + (flat_dot(attention_blend, weights[5]) + weights[6].astype(jnp.float32))
    return (
        result,
        (
            normed_unit,
            inverse,
            hidden,
            query_rows,
            key_matrix_rows,
            value_matrix_rows,
            log_total,
            attention_blend,
            relative,
            same_utterance,
        ),
    )


def mixer_backward(upstream, saved, weights):
    (
        normed_unit,
        inverse,
        hidden,
        query_rows,
        key_matrix_rows,
        value_matrix_rows,
        log_total,
        attention_blend,
        relative,
        same_utterance,
    ) = saved
    frame_count = upstream.shape[0]
    upstream_low = upstream.astype(jnp.bfloat16)
    output_slope = lead_dot(attention_blend, upstream_low)
    attention_blend_gradient = (
        back_dot(upstream_low, weights[5]).astype(jnp.bfloat16).reshape(frame_count, HEADS, HEAD)
    )
    scores = mixer_scores(query_rows, key_matrix_rows, relative, same_utterance)
    soft_full = jnp.exp(scores - log_total)
    value_grad = jnp.einsum(
        "ybr,byq->ryq",
        soft_full.astype(jnp.bfloat16),
        attention_blend_gradient,
        preferred_element_type=jnp.float32,
    ).reshape(frame_count, D)
    soft_grad = jnp.einsum(
        "jug,fug->ujf",
        attention_blend_gradient,
        value_matrix_rows,
        preferred_element_type=jnp.float32,
    )
    score_grad = soft_full * (soft_grad - jnp.sum(soft_full * soft_grad, axis=-1, keepdims=True))
    table_slope = relative_slope(score_grad, frame_count)
    score_reduced_precision = (HEAD ** (-0.5) * score_grad).astype(jnp.bfloat16)
    query_grad = jnp.einsum(
        "ief,fiv->eiv", score_reduced_precision, key_matrix_rows, preferred_element_type=jnp.float32
    ).reshape(frame_count, D)
    key_grad = jnp.einsum(
        "ybr,byq->ryq", score_reduced_precision, query_rows, preferred_element_type=jnp.float32
    ).reshape(frame_count, D)
    projected_low = jnp.concatenate([query_grad, key_grad, value_grad], axis=1).astype(jnp.bfloat16)
    project_slope = lead_dot(hidden, projected_low)
    hidden_grad = back_dot(projected_low, weights[2])
    input_grad, gain_slope, shift_slope = norm_back(hidden_grad, normed_unit, inverse, weights[0])
    slopes = (
        gain_slope,
        shift_slope,
        project_slope,
        jnp.sum(query_grad, axis=0),
        jnp.sum(value_grad, axis=0),
        output_slope,
        jnp.sum(upstream, axis=0),
        table_slope,
    )
    return (upstream + input_grad, slopes)


def filter_forward(values, segment_ids, weights):
    normed, normed_unit, inverse = norm_apply(values, weights[0], weights[1])
    hidden = normed.astype(jnp.bfloat16)
    widened = flat_dot(hidden, weights[2]) + weights[3].astype(jnp.float32)
    gated_rows = widened[:, :D] * jax.nn.sigmoid(widened[:, D:])
    filtered = depthwise(gated_rows, weights[4].astype(jnp.float32), segment_ids) + weights[
        5
    ].astype(jnp.float32)
    middle, middle_unit, middle_inverse = norm_apply(filtered, weights[6], weights[7])
    swished = (middle * jax.nn.sigmoid(middle)).astype(jnp.bfloat16)
    result = values + (flat_dot(swished, weights[8]) + weights[9].astype(jnp.float32))
    return (
        result,
        (
            normed_unit,
            inverse,
            hidden,
            widened,
            gated_rows,
            middle_unit,
            middle_inverse,
            middle,
            swished,
        ),
    )


def filter_backward(upstream, saved, weights, segment_ids):
    (
        normed_unit,
        inverse,
        hidden,
        widened,
        gated_rows,
        middle_unit,
        middle_inverse,
        middle,
        swished,
    ) = saved
    upstream_low = upstream.astype(jnp.bfloat16)
    down_slope = lead_dot(swished, upstream_low)
    middle_grad = swish_back(back_dot(upstream_low, weights[8]), middle)
    filtered_grad, middle_gain_slope, middle_shift_slope = norm_back(
        middle_grad, middle_unit, middle_inverse, weights[6]
    )

    def local_filter(local_rows, local_kernel):
        return depthwise(local_rows, local_kernel, segment_ids)

    unused, pullback = jax.vjp(local_filter, gated_rows, weights[4].astype(jnp.float32))
    gated_grad, kernel_slope = pullback(filtered_grad)
    opened = jax.nn.sigmoid(widened[:, D:])
    widened_grad = jnp.concatenate(
        [gated_grad * opened, gated_grad * widened[:, :D] * opened * (1.0 - opened)], axis=1
    )
    widened_low = widened_grad.astype(jnp.bfloat16)
    up_slope = lead_dot(hidden, widened_low)
    hidden_grad = back_dot(widened_low, weights[2])
    input_grad, gain_slope, shift_slope = norm_back(hidden_grad, normed_unit, inverse, weights[0])
    slopes = (
        gain_slope,
        shift_slope,
        up_slope,
        jnp.sum(widened_grad, axis=0),
        kernel_slope,
        jnp.sum(filtered_grad, axis=0),
        middle_gain_slope,
        middle_shift_slope,
        down_slope,
        jnp.sum(upstream, axis=0),
    )
    return (upstream + input_grad, slopes)


def body(
    frames,
    segments,
    cotangent,
    early_gain,
    early_shift,
    early_up,
    early_lift,
    early_down,
    early_drop,
    mixer_gain,
    mixer_shift,
    mixer_project,
    query_bias,
    value_bias,
    mixer_output,
    mixer_drop,
    distance_table,
    filter_gain,
    filter_shift,
    filter_up,
    filter_lift,
    depth_weight,
    depth_bias,
    middle_gain,
    middle_shift,
    filter_down,
    filter_drop,
    late_gain,
    late_shift,
    late_up,
    late_lift,
    late_down,
    late_drop,
    final_gain,
    final_shift,
):
    start_rows = frames.astype(jnp.float32)
    final_upstream = cotangent.astype(jnp.float32)
    early_full = fetch_feed(early_gain, early_shift, early_up, early_lift, early_down, early_drop)
    first_rows, early_kept = feed_forward(start_rows, early_full)
    mixer_full = fetch_mixer(
        mixer_gain,
        mixer_shift,
        mixer_project,
        query_bias,
        value_bias,
        mixer_output,
        mixer_drop,
        distance_table,
    )
    second_rows, mixer_kept = mixer_forward(first_rows, segments, mixer_full)
    filter_full = fetch_filter(
        filter_gain,
        filter_shift,
        filter_up,
        filter_lift,
        depth_weight,
        depth_bias,
        middle_gain,
        middle_shift,
        filter_down,
        filter_drop,
        final_gain,
        final_shift,
    )
    third_rows, filter_kept = filter_forward(second_rows, segments, filter_full)
    late_full = fetch_feed(late_gain, late_shift, late_up, late_lift, late_down, late_drop)
    fourth_rows, late_kept = feed_forward(third_rows, late_full)
    layer_out, final_unit, final_inverse = norm_apply(fourth_rows, filter_full[10], filter_full[11])
    final_stats = (final_unit, final_inverse)
    upstream, final_gain_slope, final_shift_slope = norm_back(
        final_upstream, final_stats[0], final_stats[1], filter_full[10]
    )
    upstream, late_slopes = feed_backward(upstream, late_kept, late_full)
    late_summed = reduce_feed(
        late_slopes[0],
        late_slopes[1],
        late_slopes[2],
        late_slopes[3],
        late_slopes[4],
        late_slopes[5],
    )
    upstream, filter_grads = filter_backward(upstream, filter_kept, filter_full, segments)
    filter_summed = reduce_filter(
        filter_grads[0],
        filter_grads[1],
        filter_grads[2],
        filter_grads[3],
        filter_grads[4],
        filter_grads[5],
        filter_grads[6],
        filter_grads[7],
        filter_grads[8],
        filter_grads[9],
        final_gain_slope,
        final_shift_slope,
    )
    upstream, mixer_grads = mixer_backward(upstream, mixer_kept, mixer_full)
    mixer_summed = reduce_mixer(
        mixer_grads[0],
        mixer_grads[1],
        mixer_grads[2],
        mixer_grads[3],
        mixer_grads[4],
        mixer_grads[5],
        mixer_grads[6],
        mixer_grads[7],
    )
    upstream, early_slopes = feed_backward(upstream, early_kept, early_full)
    early_summed = reduce_feed(
        early_slopes[0],
        early_slopes[1],
        early_slopes[2],
        early_slopes[3],
        early_slopes[4],
        early_slopes[5],
    )
    return (
        layer_out,
        upstream,
        early_summed[0],
        early_summed[1],
        early_summed[2],
        early_summed[3],
        early_summed[4],
        early_summed[5],
        mixer_summed[0],
        mixer_summed[1],
        mixer_summed[2],
        mixer_summed[3],
        mixer_summed[4],
        mixer_summed[5],
        mixer_summed[6],
        mixer_summed[7],
        filter_summed[0],
        filter_summed[1],
        filter_summed[2],
        filter_summed[3],
        filter_summed[4],
        filter_summed[5],
        filter_summed[6],
        filter_summed[7],
        filter_summed[8],
        filter_summed[9],
        late_summed[0],
        late_summed[1],
        late_summed[2],
        late_summed[3],
        late_summed[4],
        late_summed[5],
        filter_summed[10],
        filter_summed[11],
    )


def solution(mesh):
    in_specs = (
        P(("dp", "fsdp"), None),
        P(("dp", "fsdp")),
        P(("dp", "fsdp"), None),
        P(("dp", "fsdp")),
        P(("dp", "fsdp")),
        P(("dp", "fsdp"), None),
        P(("dp", "fsdp")),
        P(("dp", "fsdp"), None),
        P(("dp", "fsdp")),
        P(("dp", "fsdp")),
        P(("dp", "fsdp")),
        P(("dp", "fsdp"), None),
        P(("dp", "fsdp")),
        P(("dp", "fsdp")),
        P(("dp", "fsdp"), None),
        P(("dp", "fsdp")),
        P(("dp", "fsdp"), None),
        P(("dp", "fsdp")),
        P(("dp", "fsdp")),
        P(("dp", "fsdp"), None),
        P(("dp", "fsdp")),
        P(("dp", "fsdp"), None),
        P(("dp", "fsdp")),
        P(("dp", "fsdp")),
        P(("dp", "fsdp")),
        P(("dp", "fsdp"), None),
        P(("dp", "fsdp")),
        P(("dp", "fsdp")),
        P(("dp", "fsdp")),
        P(("dp", "fsdp"), None),
        P(("dp", "fsdp")),
        P(("dp", "fsdp"), None),
        P(("dp", "fsdp")),
        P(("dp", "fsdp")),
        P(("dp", "fsdp")),
    )
    out_specs = (
        P(("dp", "fsdp"), None),
        P(("dp", "fsdp"), None),
        P(("dp", "fsdp")),
        P(("dp", "fsdp")),
        P(("dp", "fsdp"), None),
        P(("dp", "fsdp")),
        P(("dp", "fsdp"), None),
        P(("dp", "fsdp")),
        P(("dp", "fsdp")),
        P(("dp", "fsdp")),
        P(("dp", "fsdp"), None),
        P(("dp", "fsdp")),
        P(("dp", "fsdp")),
        P(("dp", "fsdp"), None),
        P(("dp", "fsdp")),
        P(("dp", "fsdp"), None),
        P(("dp", "fsdp")),
        P(("dp", "fsdp")),
        P(("dp", "fsdp"), None),
        P(("dp", "fsdp")),
        P(("dp", "fsdp"), None),
        P(("dp", "fsdp")),
        P(("dp", "fsdp")),
        P(("dp", "fsdp")),
        P(("dp", "fsdp"), None),
        P(("dp", "fsdp")),
        P(("dp", "fsdp")),
        P(("dp", "fsdp")),
        P(("dp", "fsdp"), None),
        P(("dp", "fsdp")),
        P(("dp", "fsdp"), None),
        P(("dp", "fsdp")),
        P(("dp", "fsdp")),
        P(("dp", "fsdp")),
    )
    return jax.shard_map(body, mesh=mesh, in_specs=in_specs, out_specs=out_specs, check_vma=False)
```

profile of v0, /device:TPU:0, one launch (start us, length us, event | category | flops | bytes accessed | tf_op | source)
XLA Modules:
  0.0 2340.5 jit_solution(7746826713431541402)
XLA Ops:
  29.5 44.3 %all-reduce.47 = (bf16[1024]{0:T(1024)(128)(2,1)S(1)}, bf16[1024]{0:T(1024)(128)(2,1)S(1)}, bf16[1024]{0:T(1024)(128)(2,1)S(1)}, bf16[1024]{0:T(1024)(128)(2,1)S...) all-reduce(bf16[1024]{0:T(1024)(128)(2,1)S(1)} %dynamic-update-slic, ...), channel_id=1, replica_groups=mesh['dp'=4,'fsdp'=8] {'dp','fsdp'}, use_global_device_ids=true, to_apply=%add.5 | all-reduce | flops 21504 | bytes 86016
  79.3 40.8 %all-gather = bf16[32,1,128]{2,1,0:T(2,128)(2,1)S(1)} all-gather(bf16[1,1,128]{2,1,0:T(2,128)(2,1)} %bitcast.170), channel_id=1, replica_groups=mesh['dp'=4,'fsdp'=8] {'dp','fsdp'}, dimensions={0}, use_global_device_ids=true | all-gather | bytes 8448 | tf_op jit(solution)/shard_map/all_gather | solution.py:83
  120.1 37.5 %all-gather.1 = bf16[32,1,128]{2,1,0:T(2,128)(2,1)S(1)} all-gather(bf16[1,1,128]{2,1,0:T(2,128)(2,1)} %bitcast.171), channel_id=1, replica_groups=mesh['dp'=4,'fsdp'=8] {'dp','fsdp'}, dimensions={0}, use_global_device_ids=true | all-gather | bytes 8448 | tf_op jit(solution)/shard_map/all_gather | solution.py:83
  157.6 39.3 %all_gather.107 = bf16[256,16]{1,0:T(8,128)(2,1)S(1)} all-gather(bf16[8,16]{1,0:T(8,128)(2,1)} %param.51), channel_id=1, replica_groups=mesh['dp'=4,'fsdp'=8] {'dp','fsdp'}, dimensions={0}, use_global_device_ids=true | all-gather | bytes 8448 | tf_op jit(solution)/shard_map/all_gather | solution.py:111
  197.3 39.6 %all_gather.114 = bf16[1024,31]{1,0:T(8,128)(2,1)S(1)} all-gather(bf16[32,31]{1,0:T(8,128)(2,1)S(1)} %copy-done.86), channel_id=1, replica_groups=mesh['dp'=4,'fsdp'=8] {'dp','fsdp'}, dimensions={0}, use_global_device_ids=true | all-gather | bytes 65472 | tf_op jit(solution)/shard_map/all_gather | solution.py:149
  264.8 35.2 %all-gather.17.cloned.1.call-done = bf16[1024,1024]{1,0:T(8,128)(2,1)} async-done(((bf16[32,1024]{1,0:T(8,128)(2,1)}), bf16[1024,1024]{1,0:T(8,128)(2,1)}) %all-gather.17.cloned.1.call-update) | async-done | bytes 2097168 | tf_op jit(solution)/shard_map/all_gather | solution.py:109
  302.5 61.0 %all-gather.19.cloned.1.call-done = bf16[1024,2048]{1,0:T(8,128)(2,1)} async-done(((bf16[32,2048]{1,0:T(8,128)(2,1)}), bf16[1024,2048]{1,0:T(8,128)(2,1)}) %all-gather.19.cloned.1.call-update) | async-done | bytes 4194320 | tf_op jit(solution)/shard_map/all_gather | solution.py:147
  378.4 43.1 %all-gather.21.cloned.1.call-done = bf16[1024,1024]{1,0:T(8,128)(2,1)} async-done(((bf16[32,1024]{1,0:T(8,128)(2,1)}), bf16[1024,1024]{1,0:T(8,128)(2,1)}) %all-gather.21.cloned.1.call-update) | async-done | bytes 2097168 | tf_op jit(solution)/shard_map/all_gather | solution.py:153
  424.0 76.4 %all-gather.23.cloned.1.call-done = bf16[1024,4096]{1,0:T(8,128)(2,1)} async-done(((bf16[32,4096]{1,0:T(8,128)(2,1)}), bf16[1024,4096]{1,0:T(8,128)(2,1)}) %all-gather.23.cloned.1.call-update) | async-done | bytes 8388624 | tf_op jit(solution)/shard_map/all_gather | solution.py:82
  506.5 72.7 %all-gather.25.cloned.1.call-done = bf16[4096,1024]{1,0:T(8,128)(2,1)} async-done(((bf16[128,1024]{1,0:T(8,128)(2,1)}), bf16[4096,1024]{1,0:T(8,128)(2,1)}) %all-gather.25.cloned.1.call-update) | async-done | bytes 8388624 | tf_op jit(solution)/shard_map/all_gather | solution.py:84
  599.0 12.7 fusion.69
  633.3 13.4 convolution_add_fusion.9
  646.8 13.0 convolution_add_fusion.8
  661.1 6.5 multiply_reduce_fusion.4
  676.9 7.3 fusion.139
  684.2 8.1 fusion.30
  692.6 14.1 convolution_add_fusion.7
  723.6 7.4 fusion.58
  732.0 8.1 fusion.98
  741.8 8.1 fusion.97
  751.3 8.2 fusion.54
  760.7 8.2 fusion.49
  771.2 74.7 %all-reduce.50.cloned.1.call-done = (f32[1024]{0:T(1024)}, f32[1024]{0:T(1024)}, f32[4096]{0:T(1024)}, f32[1024]{0:T(1024)}, f32[1024]{0:T(1024)}, /*index=5*/f3...) async-done(((f32[1024]{0:T(1024)}, f32[1024]{0:T(1024)}, ...) | async-done | bytes 135184
  874.8 109.5 %reduce-scatter.28.cloned.1.call-done = f32[32,31]{1,0:T(8,128)} async-done(((f32[1024,31]{1,0:T(8,128)}), f32[32,31]{1,0:T(8,128)}) %reduce-scatter.28.cloned.1.call-update) | async-done | bytes 3984
  984.3 142.3 %reduce-scatter.22.cloned.1.call-done = f32[32,1024]{1,0:T(8,128)} async-done(((f32[1024,1024]{1,0:T(8,128)}), f32[32,1024]{1,0:T(8,128)}) %reduce-scatter.22.cloned.1.call-update) | async-done | bytes 131088 | tf_op jit(solution)/shard_map/reduce_scatter | solution.py:183
  1126.7 144.6 %reduce-scatter.18.cloned.1.call-done = f32[32,1024]{1,0:T(8,128)} async-done(((f32[1024,1024]{1,0:T(8,128)}), f32[32,1024]{1,0:T(8,128)}) %reduce-scatter.18.cloned.1.call-update) | async-done | bytes 131088 | tf_op jit(solution)/shard_map/reduce_scatter | solution.py:124
  1271.3 153.2 %reduce-scatter.20.cloned.1.call-done = f32[32,2048]{1,0:T(8,128)} async-done(((f32[1024,2048]{1,0:T(8,128)}), f32[32,2048]{1,0:T(8,128)}) %reduce-scatter.20.cloned.1.call-update) | async-done | bytes 262160 | tf_op jit(solution)/shard_map/reduce_scatter | solution.py:177
  1424.5 159.4 %reduce-scatter.16.cloned.1.call-done = f32[32,3072]{1,0:T(8,128)} async-done(((f32[1024,3072]{1,0:T(8,128)}), f32[32,3072]{1,0:T(8,128)}) %reduce-scatter.16.cloned.1.call-update) | async-done | bytes 393232 | tf_op jit(solution)/shard_map/reduce_scatter | solution.py:121
  1583.9 188.2 %reduce-scatter.14.cloned.1.call-done = f32[128,1024]{1,0:T(8,128)} async-done(((f32[4096,1024]{1,0:T(8,128)}), f32[128,1024]{1,0:T(8,128)}) %reduce-scatter.14.cloned.1.call-update) | async-done | bytes 524304 | tf_op jit(solution)/shard_map/reduce_scatter | solution.py:95
  1772.1 187.1 %reduce-scatter.26.cloned.1.call-done = f32[128,1024]{1,0:T(8,128)} async-done(((f32[4096,1024]{1,0:T(8,128)}), f32[128,1024]{1,0:T(8,128)}) %reduce-scatter.26.cloned.1.call-update) | async-done | bytes 524304 | tf_op jit(solution)/shard_map/reduce_scatter | solution.py:95
  1959.2 187.1 %reduce-scatter.24.cloned.1.call-done = f32[32,4096]{1,0:T(8,128)} async-done(((f32[1024,4096]{1,0:T(8,128)}), f32[32,4096]{1,0:T(8,128)}) %reduce-scatter.24.cloned.1.call-update) | async-done | bytes 524304 | tf_op jit(solution)/shard_map/reduce_scatter | solution.py:93
  2146.3 187.1 %reduce-scatter.12.cloned.1.call-done = f32[32,4096]{1,0:T(8,128)} async-done(((f32[1024,4096]{1,0:T(8,128)}), f32[32,4096]{1,0:T(8,128)}) %reduce-scatter.12.cloned.1.call-update) | async-done | bytes 524304 | tf_op jit(solution)/shard_map/reduce_scatter | solution.py:93
  (437 shorter events, 186.3 us)
Async XLA Ops:
  7.2 190.1 %copy-start.86 = (bf16[32,31]{1,0:T(8,128)(2,1)S(1)}, bf16[32,31]{1,0:T(8,128)(2,1)}, u32[]{:S(2)}) copy-start(bf16[32,31]{1,0:T(8,128)(2,1)} %param.56) | copy-start | bytes 5956
  7.2 240.4 %all-gather.11.cloned.1.call-start = ((), (), s32[]{:S(2)}) async-start(), calls=%async_computation.9 | async-start | bytes 8650752 | tf_op jit(solution)/shard_map/all_gather | solution.py:82
  8.0 244.5 %all-gather.13.cloned.1.call-start = ((), (), s32[]{:S(2)}) async-start(), calls=%async_computation.10 | async-start | bytes 8650752 | tf_op jit(solution)/shard_map/all_gather | solution.py:84
  8.7 249.6 %all-gather.15.cloned.1.call-start = ((), (), s32[]{:S(2)}) async-start(), calls=%async_computation.11 | async-start | bytes 6488064 | tf_op jit(solution)/shard_map/all_gather | solution.py:106
  9.4 290.6 %all-gather.17.cloned.1.call-start = ((), (), s32[]{:S(2)}) async-start(), calls=%async_computation.12 | async-start | bytes 2162688 | tf_op jit(solution)/shard_map/all_gather | solution.py:109
  10.0 353.4 %all-gather.19.cloned.1.call-start = ((), (), s32[]{:S(2)}) async-start(), calls=%async_computation.13 | async-start | bytes 4325376 | tf_op jit(solution)/shard_map/all_gather | solution.py:147
  10.6 410.9 %all-gather.21.cloned.1.call-start = ((), (), s32[]{:S(2)}) async-start(), calls=%async_computation.14 | async-start | bytes 2162688 | tf_op jit(solution)/shard_map/all_gather | solution.py:153
  11.2 489.2 %all-gather.23.cloned.1.call-start = ((), (), s32[]{:S(2)}) async-start(), calls=%async_computation.15 | async-start | bytes 8650752 | tf_op jit(solution)/shard_map/all_gather | solution.py:82
  11.9 567.2 %all-gather.25.cloned.1.call-start = ((), (), s32[]{:S(2)}) async-start(), calls=%async_computation.16 | async-start | bytes 8650752 | tf_op jit(solution)/shard_map/all_gather | solution.py:84
  12.7 833.2 %all-reduce.50.cloned.1.call-start = ((), (), s32[]{:S(2)}) async-start(), calls=%async_computation.26 | async-start | bytes 499712
  74.5 173.1 %copy-start.51 = (f32[1024]{0:T(1024)}, f32[1024]{0:T(1024)S(1)}, u32[]{:S(2)}) copy-start(f32[1024]{0:T(1024)S(1)} %convert_element_type.160) | copy-start | bytes 12292
  74.5 183.8 %copy-start.55 = (f32[1024]{0:T(1024)}, f32[1024]{0:T(1024)S(1)}, u32[]{:S(2)}) copy-start(f32[1024]{0:T(1024)S(1)} %convert_element_type.166) | copy-start | bytes 12292
  74.5 425.9 %copy-start.53 = (f32[1024]{0:T(1024)}, f32[1024]{0:T(1024)S(1)}, u32[]{:S(2)}) copy-start(f32[1024]{0:T(1024)S(1)} %convert_element_type.187) | copy-start | bytes 12292
  264.8 101.6 %copy-start.32 = (bf16[16,64,128]{2,1,0:T(8,128)(2,1)}, bf16[16,64,128]{2,1,0:T(8,128)(2,1)S(1)}, u32[]{:S(2)}) copy-start(bf16[16,64,128]{2,1,0:T(8,128)(2,1)S(1)} %convolution_convert_fusion.2) | copy-start | bytes 786436
  264.8 98.6 %copy-start.57 = (f32[2048]{0:T(1024)S(1)}, f32[2048]{0:T(1024)}, u32[]{:S(2)}) copy-start(f32[2048]{0:T(1024)} %convert_element_type.180) | copy-start | bytes 24580
  302.2 64.3 %copy-start.64 = (f32[128]{0:T(128)}, f32[128]{0:T(128)S(1)}, u32[]{:S(2)}) copy-start(f32[128]{0:T(128)S(1)} %broadcast_multiply_fusion.15) | copy-start | bytes 1540
  302.4 61.0 %copy-start.84 = (f32[128]{0:T(128)}, f32[128]{0:T(128)S(1)}, u32[]{:S(2)}) copy-start(f32[128]{0:T(128)S(1)} %add_rsqrt_fusion.3) | copy-start | bytes 1540
  302.4 64.1 %copy-start.77 = (pred[128]{0:T(512)(128)(4,1)S(1)}, pred[128]{0:T(512)(128)(4,1)}, u32[]{:S(2)}) copy-start(pred[128]{0:T(512)(128)(4,1)} %get-tuple-element.268) | copy-start | bytes 388
  378.2 219.8 %copy-start.11 = (f32[128,1024]{1,0:T(8,128)}, f32[128,1024]{1,0:T(8,128)S(1)}, u32[]{:S(2)}) copy-start(f32[128,1024]{1,0:T(8,128)S(1)} %get-tuple-element.250) | copy-start | bytes 1572868
  378.2 45.6 %copy-start.88 = (f32[128]{0:T(128)}, f32[128]{0:T(128)S(1)}, u32[]{:S(2)}) copy-start(f32[128]{0:T(128)S(1)} %broadcast_multiply_fusion.14) | copy-start | bytes 1540
  423.8 171.0 %copy-start.1 = (f32[128,1024]{1,0:T(8,128)}, f32[128,1024]{1,0:T(8,128)S(1)}, u32[]{:S(2)}) copy-start(f32[128,1024]{1,0:T(8,128)S(1)} %get-tuple-element.278) | copy-start | bytes 1572868
  500.4 78.7 %copy-start.91 = (f32[1024]{0:T(1024)S(1)}, f32[1024]{0:T(1024)}, u32[]{:S(2)}) copy-start(f32[1024]{0:T(1024)} %convert_element_type.191) | copy-start | bytes 12292
  506.5 79.3 %copy-start.66 = (f32[1024]{0:T(1024)S(1)}, f32[1024]{0:T(1024)}, u32[]{:S(2)}) copy-start(f32[1024]{0:T(1024)} %convert_element_type.193) | copy-start | bytes 12292
  692.4 292.0 %reduce-scatter.28.cloned.1.call-start = ((), (), s32[]{:S(2)}) async-start(), calls=%async_computation.25 | async-start | bytes 540672
  708.6 418.0 %reduce-scatter.22.cloned.1.call-start = ((), (), s32[]{:S(2)}) async-start(), calls=%async_computation.22 | async-start | bytes 4325376 | tf_op jit(solution)/shard_map/reduce_scatter | solution.py:183
  712.8 558.5 %reduce-scatter.18.cloned.1.call-start = ((), (), s32[]{:S(2)}) async-start(), calls=%async_computation.20 | async-start | bytes 4325376 | tf_op jit(solution)/shard_map/reduce_scatter | solution.py:124
  716.6 707.9 %reduce-scatter.20.cloned.1.call-start = ((), (), s32[]{:S(2)}) async-start(), calls=%async_computation.21 | async-start | bytes 8650752 | tf_op jit(solution)/shard_map/reduce_scatter | solution.py:177
  722.6 861.3 %reduce-scatter.16.cloned.1.call-start = ((), (), s32[]{:S(2)}) async-start(), calls=%async_computation.19 | async-start | bytes 12976128 | tf_op jit(solution)/shard_map/reduce_scatter | solution.py:121
  731.0 1041.1 %reduce-scatter.14.cloned.1.call-start = ((), (), s32[]{:S(2)}) async-start(), calls=%async_computation.18 | async-start | bytes 17301504 | tf_op jit(solution)/shard_map/reduce_scatter | solution.py:95
  740.2 1219.0 %reduce-scatter.26.cloned.1.call-start = ((), (), s32[]{:S(2)}) async-start(), calls=%async_computation.24 | async-start | bytes 17301504 | tf_op jit(solution)/shard_map/reduce_scatter | solution.py:95
  750.0 1396.3 %reduce-scatter.24.cloned.1.call-start = ((), (), s32[]{:S(2)}) async-start(), calls=%async_computation.23 | async-start | bytes 17301504 | tf_op jit(solution)/shard_map/reduce_scatter | solution.py:93
  759.5 1573.8 %reduce-scatter.12.cloned.1.call-start = ((), (), s32[]{:S(2)}) async-start(), calls=%async_computation.17 | async-start | bytes 17301504 | tf_op jit(solution)/shard_map/reduce_scatter | solution.py:93
  (88 other events, 616.2 us)
Sparse Core Ops, SparseCore 0:
  11.0 80.8 all-gather.10
  94.9 75.7 all-gather.12
  173.7 67.6 all-gather.14
  244.3 55.7 all-gather.16
  302.9 60.5 all-gather.18
  366.3 55.1 all-gather.20
  424.5 75.9 all-gather.22
  503.4 75.6 all-gather.24
  692.5 153.3 all-reduce.49
  848.5 135.8 reduce-scatter.27
  987.2 139.4 reduce-scatter.21
  1129.4 141.8 reduce-scatter.17
  1274.1 150.3 reduce-scatter.19
  1431.0 152.8 reduce-scatter.15
  1586.6 185.4 reduce-scatter.13
  1774.8 184.3 reduce-scatter.25
  1961.9 184.3 reduce-scatter.23
  2149.0 184.3 reduce-scatter.11
where the time goes:
time: 2350 us; the launch traced here: 2340 us
  waiting for transfers between devices  1830 us (78%)
  blocking collectives  202 us (9%)
  matrix products  197 us (8%)
  local copies, waits for them, and re-layouts  79 us (3%)
    reduce_scatter x2, waiting for transfers between devices, reduce_feed(): lax.psum_scatter(w_down, ('dp', 'fsdp'), scatter_dimension=0, tiled=True)  375 us
    reduce_scatter x2, waiting for transfers between devices, reduce_feed(): lax.psum_scatter(w_up, ('dp', 'fsdp'), scatter_dimension=0, tiled=True)  374 us
    unnamed x20, waiting for transfers between devices  189 us
    reduce_scatter x1, waiting for transfers between devices, reduce_mixer(): lax.psum_scatter(w_project, ('dp', 'fsdp'), scatter_dimension=0, tiled=True)  159 us
    reduce_scatter x1, waiting for transfers between devices, reduce_filter(): lax.psum_scatter(w_up, ('dp', 'fsdp'), scatter_dimension=0, tiled=True)  153 us
    reduce_scatter x1, waiting for transfers between devices, reduce_mixer(): lax.psum_scatter(w_output, ('dp', 'fsdp'), scatter_dimension=0, tiled=True)  145 us
    reduce_scatter x1, waiting for transfers between devices, reduce_filter(): lax.psum_scatter(w_down, ('dp', 'fsdp'), scatter_dimension=0, tiled=True)  142 us
    all_gather x2, blocking collectives, fetch_feed(): lax.all_gather(up_shift, ('dp', 'fsdp'), axis=0, tiled=True)  78.3 us
  transfers between devices with their start and end apart: 18, of which 15 were waited for; matrix products, arithmetic and copies ran while one was open for 7% of the time, Pallas kernels for 0%

commit v1 on v0

--- a/solution.py
+++ b/solution.py
@@ -1,6 +1,10 @@
+import functools
+
 import jax
 import jax.numpy as jnp
 from jax import lax
+from jax.experimental import pallas as pl
+from jax.experimental.pallas import tpu as pltpu
 from jax.sharding import PartitionSpec as P
 
 D = 1024
@@ -13,6 +17,7 @@
 EPSILON = 1e-05
 MASKED = -1e30
 UTTERANCE_LIMIT = 4
+MESH = pl.DeviceIdType.MESH
 
 
 def flat_dot(left_rows, right_rows):
@@ -595,6 +600,998 @@
     )
 
 
+def near(me, n):
+    if n == 4:
+        row, column = me // 2, me % 2
+        flip_row, flip_column = (1 - row) * 2 + column, row * 2 + 1 - column
+        across = (1 - row) * 2 + 1 - column
+        return [(flip_column, flip_column), (flip_row, flip_row), (across, across)]
+    return [((me + step) % n, (me + n - step) % n) for step in range(1, n)]
+
+
+def greet(targets):
+    barrier = pltpu.get_barrier_semaphore()
+    for target in targets:
+        pl.semaphore_signal(barrier, inc=1, device_id={"dp": target}, device_id_type=MESH)
+    pl.semaphore_wait(barrier, len(targets))
+
+
+def greet_all(n, m):
+    me, lane = lax.axis_index("dp"), lax.axis_index("fsdp")
+    barrier = pltpu.get_barrier_semaphore()
+
+    def say(step, carry):
+        target = {"dp": (me + step // m) % n, "fsdp": (lane + step % m) % m}
+        pl.semaphore_signal(barrier, inc=1, device_id=target, device_id_type=MESH)
+        return carry
+
+    lax.fori_loop(1, n * m, say, 0)
+    pl.semaphore_wait(barrier, n * m - 1)
+
+
+def remote(src, dst, send, recv, target):
+    return pltpu.make_async_remote_copy(
+        src_ref=src, dst_ref=dst, send_sem=send, recv_sem=recv, device_id=target, device_id_type=MESH
+    )
+
+
+def columns(start, width):
+    return pl.ds(pl.multiple_of(start * width, width), width)
+
+
+def column_pieces(index, sizes):
+    pieces = []
+    for place, (groups, width) in enumerate(sizes):
+        whole = width * index[2]
+        for group in range(groups):
+            wide = pl.ds(pl.multiple_of(group * whole + index[0] * width, width), width)
+            pieces.append((place, wide, pl.ds(group * width, width)))
+    return pieces
+
+
+def exchange_kernel(n, m, sizes, *refs):
+    count = len(sizes)
+    wides = refs[:count]
+    small, segs = refs[count : count + 2]
+    narrows = refs[count + 2 : 2 * count + 2]
+    small_all, segs_all, local, send, recv, small_send, small_recv = refs[2 * count + 2 :]
+    me, lane = lax.axis_index("dp"), lax.axis_index("fsdp")
+    here = me * m + lane
+    greet_all(n, m)
+    others = near(me, n)
+
+    def to_device(step):
+        target = {"dp": (me + step // m) % n, "fsdp": (lane + step % m) % m}
+        return remote(small, small_all.at[here], small_send.at[step], small_recv.at[step], target)
+
+    def start_small(step, carry):
+        to_device(step).start()
+        return carry
+
+    def wait_small(step, carry):
+        to_device(step).wait()
+        return carry
+
+    copies = []
+    for peer, (target, unused) in enumerate(others):
+        for at, (place, wide, narrow) in enumerate(column_pieces((target, 0, n), sizes)):
+            copies.append(
+                (at, remote(wides[place].at[:, wide], narrows[place].at[me, :, narrow], send.at[peer, at], recv.at[peer, at], {"dp": target}))
+            )
+        copies.append((-1, remote(segs, segs_all.at[me], send.at[peer, at + 1], recv.at[peer, at + 1], {"dp": target})))
+    owns = [pltpu.make_async_copy(small, small_all.at[here], local.at[0]), pltpu.make_async_copy(segs, segs_all.at[me], local.at[1])]
+    for at, (place, wide, narrow) in enumerate(column_pieces((me, 0, n), sizes)):
+        owns.append(pltpu.make_async_copy(wides[place].at[:, wide], narrows[place].at[me, :, narrow], local.at[2 + at]))
+    for order, copy in copies:
+        if order <= 0:
+            copy.start()
+    lax.fori_loop(1, n * m, start_small, 0)
+    for order, copy in copies:
+        if order > 0:
+            copy.start()
+    for copy in owns:
+        copy.start()
+    for copy in owns:
+        copy.wait()
+    for order, copy in copies:
+        copy.wait()
+    lax.fori_loop(1, n * m, wait_small, 0)
+
+
+def exchange(n, m, wides, sizes, small, segs):
+    rows = small.shape[0]
+    total = sum(groups for groups, width in sizes)
+    outs = [jax.ShapeDtypeStruct((n, rows, groups * width), jnp.bfloat16) for groups, width in sizes]
+    outs.append(jax.ShapeDtypeStruct((n * m,) + small.shape, small.dtype))
+    outs.append(jax.ShapeDtypeStruct((n,) + segs.shape, segs.dtype))
+    anywhere = pl.BlockSpec(memory_space=pl.ANY)
+    return pl.pallas_call(
+        functools.partial(exchange_kernel, n, m, sizes),
+        out_shape=outs,
+        in_specs=[anywhere] * (len(wides) + 2),
+        out_specs=[anywhere] * len(outs),
+        scratch_shapes=[
+            pltpu.SemaphoreType.DMA((total + 2,)),
+            pltpu.SemaphoreType.DMA((n - 1, total + 1)),
+            pltpu.SemaphoreType.DMA((n - 1, total + 1)),
+            pltpu.SemaphoreType.DMA((n * m,)),
+            pltpu.SemaphoreType.DMA((n * m,)),
+        ],
+        compiler_params=pltpu.CompilerParams(collective_id=0, has_side_effects=True),
+        name="exchange",
+    )(*wides, small, segs)
+
+
+def giveback_kernel(n, sizes, *refs):
+    count = len(sizes)
+    narrows, wides = refs[:count], refs[count : 2 * count]
+    local, send, recv = refs[2 * count :]
+    me = lax.axis_index("dp")
+    others = near(me, n)
+    greet([target for target, unused in others])
+    copies = []
+    for peer, (target, unused) in enumerate(others):
+        for at, (place, wide, narrow) in enumerate(column_pieces((me, 0, n), sizes)):
+            copies.append(
+                remote(narrows[place].at[target, :, narrow], wides[place].at[:, wide], send.at[peer, at], recv.at[peer, at], {"dp": target})
+            )
+    for at, (place, wide, narrow) in enumerate(column_pieces((me, 0, n), sizes)):
+        copies.append(pltpu.make_async_copy(narrows[place].at[me, :, narrow], wides[place].at[:, wide], local.at[at]))
+    for copy in copies:
+        copy.start()
+    for copy in copies:
+        copy.wait()
+
+
+def giveback(n, narrows, sizes, number):
+    rows = narrows[0].shape[1]
+    total = sum(groups for groups, width in sizes)
+    outs = [jax.ShapeDtypeStruct((rows, groups * width * n), jnp.bfloat16) for groups, width in sizes]
+    anywhere = pl.BlockSpec(memory_space=pl.ANY)
+    return pl.pallas_call(
+        functools.partial(giveback_kernel, n, sizes),
+        out_shape=outs,
+        in_specs=[anywhere] * len(narrows),
+        out_specs=[anywhere] * len(outs),
+        scratch_shapes=[
+            pltpu.SemaphoreType.DMA((total,)),
+            pltpu.SemaphoreType.DMA((n - 1, total)),
+            pltpu.SemaphoreType.DMA((n - 1, total)),
+        ],
+        compiler_params=pltpu.CompilerParams(collective_id=number, has_side_effects=True),
+        name="giveback",
+    )(*narrows)
+
+
+def share_kernel(n, mine, shared, local, send, recv):
+    me = lax.axis_index("dp")
+    others = near(me, n)
+    greet([target for target, unused in others])
+    copies = [pltpu.make_async_copy(mine, shared.at[me], local)]
+    for peer, (target, unused) in enumerate(others):
+        copies.append(remote(mine, shared.at[me], send.at[peer], recv.at[peer], {"dp": target}))
+    for copy in copies:
+        copy.start()
+    for copy in copies:
+        copy.wait()
+
+
+def share(n, mine, number):
+    inside = pl.BlockSpec(memory_space=pltpu.VMEM)
+    return pl.pallas_call(
+        functools.partial(share_kernel, n),
+        out_shape=jax.ShapeDtypeStruct((n,) + mine.shape, mine.dtype),
+        in_specs=[inside],
+        out_specs=inside,
+        scratch_shapes=[
+            pltpu.SemaphoreType.DMA,
+            pltpu.SemaphoreType.DMA((n - 1,)),
+            pltpu.SemaphoreType.DMA((n - 1,)),
+        ],
+        compiler_params=pltpu.CompilerParams(collective_id=number, has_side_effects=True),
+        name="share",
+    )(mine)
+
+
+def collect_kernel(n, m, wide, group, wide_all, group_all, local, send, recv, group_send, group_recv):
+    me, lane = lax.axis_index("dp"), lax.axis_index("fsdp")
+    here = me * m + lane
+    greet_all(n, m)
+
+    def to_device(step):
+        other, beside = (me + step // m) % n, (lane + step % m) % m
+        return remote(
+            wide.at[other * m + beside], wide_all.at[here], send.at[step], recv.at[step], {"dp": other, "fsdp": beside}
+        )
+
+    def to_group(step):
+        beside = (lane + step) % m
+        return remote(group.at[beside], group_all.at[lane], group_send.at[step], group_recv.at[step], {"fsdp": beside})
+
+    def start_wide(step, carry):
+        to_device(step).start()
+        return carry
+
+    def start_group(step, carry):
+        to_group(step).start()
+        return carry
+
+    def wait_wide(step, carry):
+        to_device(step).wait()
+        return carry
+
+    def wait_group(step, carry):
+        to_group(step).wait()
+        return carry
+
+    own = pltpu.make_async_copy(wide.at[here], wide_all.at[here], local.at[0])
+    own_group = pltpu.make_async_copy(group.at[lane], group_all.at[lane], local.at[1])
+    own.start()
+    own_group.start()
+    lax.fori_loop(1, n * m, start_wide, 0)
+    lax.fori_loop(1, m, start_group, 0)
+    own.wait()
+    own_group.wait()
+    lax.fori_loop(1, n * m, wait_wide, 0)
+    lax.fori_loop(1, m, wait_group, 0)
+
+
+def collect(n, m, wide, group, number):
+    inside = pl.BlockSpec(memory_space=pltpu.VMEM)
+    return pl.pallas_call(
+        functools.partial(collect_kernel, n, m),
+        out_shape=[jax.ShapeDtypeStruct(wide.shape, wide.dtype), jax.ShapeDtypeStruct(group.shape, group.dtype)],
+        in_specs=[inside] * 2,
+        out_specs=[inside] * 2,
+        scratch_shapes=[
+            pltpu.SemaphoreType.DMA((2,)),
+            pltpu.SemaphoreType.DMA((n * m,)),
+            pltpu.SemaphoreType.DMA((n * m,)),
+            pltpu.SemaphoreType.DMA((m,)),
+            pltpu.SemaphoreType.DMA((m,)),
+        ],
+        compiler_params=pltpu.CompilerParams(collective_id=number, has_side_effects=True),
+        name="collect",
+    )(wide, group)
+
+
+def unit_of(values):
+    centered = values - jnp.mean(values, axis=-1, keepdims=True)
+    inverse = lax.rsqrt(jnp.mean(centered * centered, axis=-1, keepdims=True) + EPSILON)
+    return centered * inverse, inverse
+
+
+def unit_back(upstream, unit, inverse, gain):
+    scaled = upstream * gain
+    adjusted = scaled - jnp.mean(scaled, axis=-1, keepdims=True)
+    return inverse * (adjusted - unit * jnp.mean(scaled * unit, axis=-1, keepdims=True))
+
+
+def step_first(total, states, vectors):
+    unit, inverse = unit_of(states[0])
+    return [], unit * vectors[0] + vectors[1], []
+
+
+def step_forward(scale, total, states, vectors):
+    values = states[0] + scale * (total + vectors[0])
+    unit, inverse = unit_of(values)
+    return [values], unit * vectors[1] + vectors[2], []
+
+
+def step_turn(total, states, vectors):
+    values = states[0] + 0.5 * (total + vectors[0])
+    upstream = states[1]
+    unit, inverse = unit_of(values)
+    layer_out = unit * vectors[1] + vectors[2]
+    grad = unit_back(upstream, unit, inverse, vectors[1])
+    half = 0.5 * grad
+    return [layer_out, grad], half, [upstream * unit, upstream, half]
+
+
+def step_backward(scale, total, states, vectors):
+    unit, inverse = unit_of(states[1])
+    grad = states[0] + unit_back(total, unit, inverse, vectors[0])
+    sent = scale * grad
+    return [grad], sent, [total * unit, total, sent]
+
+
+def step_last(total, states, vectors):
+    unit, inverse = unit_of(states[1])
+    grad = states[0] + unit_back(total, unit, inverse, vectors[0])
+    return [grad], None, [total * unit, total]
+
+
+PIECES = 4
+BLOCK = 16
+
+
+def boundary_kernel(n, step, shape, *refs):
+    summed, gathered, state_count, out_count, sum_count, vector_count = shape
+    refs = list(refs)
+    take = lambda count: [refs.pop(0) for unused in range(count)]
+    part = take(1)[0] if summed else None
+    states = take(state_count)
+    vectors = take(1)[0]
+    outs = take(out_count)
+    spread = take(1)[0] if gathered else None
+    sums = take(1)[0] if sum_count else None
+    if summed:
+        arrived, own, own_sem, send, recv = take(5)
+    if gathered:
+        held, held_sem, out_send, out_recv = take(4)
+    partials = take(1)[0] if sum_count else None
+    me = lax.axis_index("dp")
+    others = near(me, n)
+    rows = states[0].shape[0]
+    height = rows // PIECES
+    greet([target for target, unused in others])
+    incoming = {}
+    if summed:
+        own_copy = pltpu.make_async_copy(part.at[me], own, own_sem)
+        for piece in range(PIECES):
+            span = pl.ds(piece * height, height)
+            for peer, (target, unused) in enumerate(others):
+                copy = remote(
+                    part.at[target, span], arrived.at[peer, span], send.at[peer, piece], recv.at[peer, piece], {"dp": target}
+                )
+                copy.start()
+                incoming[peer, piece] = copy
+        own_copy.start()
+        own_copy.wait()
+    if sum_count:
+        partials[...] = jnp.zeros_like(partials)
+    outgoing = []
+    rows_of = [vectors[pl.ds(index, 1), :] for index in range(vector_count)]
+    for piece in range(PIECES):
+        if summed:
+            for peer in range(n - 1):
+                incoming[peer, piece].wait_recv()
+
+        def work(block, carry):
+            span = pl.ds(pl.multiple_of(piece * height + block * BLOCK, BLOCK), BLOCK)
+            total = None
+            if summed:
+                total = own[span, :].astype(jnp.float32)
+                for peer in range(n - 1):
+                    total = total + arrived[peer, span, :].astype(jnp.float32)
+            made, sent, terms = step(total, [state[span, :] for state in states], rows_of)
+            for out, value in zip(outs, made):
+                out[span, :] = value
+            if gathered:
+                held[span, :] = sent.astype(jnp.bfloat16)
+            for index, term in enumerate(terms):
+                partials[index] += sum(term[8 * low : 8 * low + 8] for low in range(BLOCK // 8))
+            return carry
+
+        lax.fori_loop(0, height // BLOCK, work, 0)
+        if gathered:
+            span = pl.ds(piece * height, height)
+            for peer, (target, unused) in enumerate(others):
+                copy = remote(
+                    held.at[span], spread.at[me, span], out_send.at[peer, piece], out_recv.at[peer, piece], {"dp": target}
+                )
+                copy.start()
+                outgoing.append(copy)
+    if gathered:
+        keep = pltpu.make_async_copy(held, spread.at[me], held_sem)
+        keep.start()
+    for index in range(sum_count):
+        sums[pl.ds(index, 1), :] = jnp.sum(partials[index], axis=0, keepdims=True)
+    for copy in incoming.values():
+        copy.wait_send()
+    for copy in outgoing:
+        copy.wait()
+    if gathered:
+        keep.wait()
+
+
+def boundary(n, step, part, states, vectors, out_count, sum_count, number, gathered=True):
+    rows, width = states[0].shape
+    summed = part is not None
+    inside = pl.BlockSpec(memory_space=pltpu.VMEM)
+    anywhere = pl.BlockSpec(memory_space=pl.ANY)
+    shape = (summed, gathered, len(states), out_count, sum_count, len(vectors))
+    operands, in_specs, outs, out_specs, scratch = [], [], [], [], []
+    if summed:
+        operands.append(part)
+        in_specs.append(anywhere)
+        scratch += [
+            pltpu.VMEM((n - 1, rows, width), jnp.bfloat16),
+            pltpu.VMEM((rows, width), jnp.bfloat16),
+            pltpu.SemaphoreType.DMA,
+            pltpu.SemaphoreType.DMA((n - 1, PIECES)),
+            pltpu.SemaphoreType.DMA((n - 1, PIECES)),
+        ]
+    operands += list(states) + [jnp.stack(vectors)]
+    in_specs += [inside] * (len(states) + 1)
+    outs += [jax.ShapeDtypeStruct((rows, width), jnp.float32)] * out_count
+    out_specs += [inside] * out_count
+    if gathered:
+        outs.append(jax.ShapeDtypeStruct((n, rows, width), jnp.bfloat16))
+        out_specs.append(anywhere)
+        scratch += [
+            pltpu.VMEM((rows, width), jnp.bfloat16),
+            pltpu.SemaphoreType.DMA,
+            pltpu.SemaphoreType.DMA((n - 1, PIECES)),
+            pltpu.SemaphoreType.DMA((n - 1, PIECES)),
+        ]
+    if sum_count:
+        outs.append(jax.ShapeDtypeStruct((sum_count, width), jnp.float32))
+        out_specs.append(inside)
+        scratch.append(pltpu.VMEM((sum_count, 8, width), jnp.float32))
+    return pl.pallas_call(
+        functools.partial(boundary_kernel, n, step, shape),
+        out_shape=outs,
+        in_specs=in_specs,
+        out_specs=out_specs,
+        scratch_shapes=scratch,
+        compiler_params=pltpu.CompilerParams(collective_id=number, has_side_effects=True),
+        name="boundary",
+    )(*operands)
+
+
+def toeplitz(line, frame_count):
+    wide = jnp.broadcast_to(line, (frame_count, NREL))
+    return pltpu.roll(wide, NREL - frame_count + 1, 1, stride=1, stride_axis=0)[:, :frame_count]
+
+
+def head_scores(packed, head, heads, same, bias):
+    size = heads * HEAD
+    query_rows = packed[:, head * HEAD : (head + 1) * HEAD]
+    key_rows = packed[:, size + head * HEAD : size + (head + 1) * HEAD]
+    value_rows = packed[:, 2 * size + head * HEAD : 2 * size + (head + 1) * HEAD]
+    scores = jnp.where(same, HEAD ** (-0.5) * back_dot(query_rows, key_rows) + bias, MASKED)
+    powered = jnp.exp(scores - jnp.max(scores, axis=-1, keepdims=True))
+    soft = powered / jnp.sum(powered, axis=-1, keepdims=True)
+    return query_rows, key_rows, value_rows, soft
+
+
+def attend_kernel(heads, packed, segment_rows, segment_columns, table, blended, bias):
+    frame_count = packed.shape[1]
+
+    @pl.when(pl.program_id(0) == 0)
+    def _():
+        for head in range(heads):
+            bias[head] = toeplitz(table[pl.ds(head, 1), :], frame_count)
+
+    same = segment_columns[0] == segment_rows[0]
+    block = packed[0]
+    results = []
+    for head in range(heads):
+        unused, unused_too, value_rows, soft = head_scores(block, head, heads, same, bias[head])
+        results.append(flat_dot(soft.astype(jnp.bfloat16), value_rows).astype(jnp.bfloat16))
+    blended[0] = jnp.concatenate(results, axis=1)
+
+
+def attend(packed, segment_rows, segment_columns, table):
+    blocks, frame_count, width = packed.shape
+    heads = table.shape[0]
+    return pl.pallas_call(
+        functools.partial(attend_kernel, heads),
+        grid=(blocks,),
+        out_shape=jax.ShapeDtypeStruct((blocks, frame_count, width // 3), jnp.bfloat16),
+        in_specs=[
+            pl.BlockSpec((1, frame_count, width), lambda i: (i, 0, 0)),
+            pl.BlockSpec((1, 1, frame_count), lambda i: (i, 0, 0)),
+            pl.BlockSpec((1, frame_count, 1), lambda i: (i, 0, 0)),
+            pl.BlockSpec((heads, NREL), lambda i: (0, 0)),
+        ],
+        out_specs=pl.BlockSpec((1, frame_count, width // 3), lambda i: (i, 0, 0)),
+        scratch_shapes=[pltpu.VMEM((heads, frame_count, frame_count), jnp.float32)],
+        name="attend",
+    )(packed, segment_rows, segment_columns, table)
+
+
+def unattend_kernel(heads, packed, upstream, segment_rows, segment_columns, table, grads, sums, slope, bias, gathered):
+    frame_count = packed.shape[1]
+    size = heads * HEAD
+    at = pl.program_id(0)
+
+    @pl.when(at == 0)
+    def _():
+        for head in range(heads):
+            bias[head] = toeplitz(table[pl.ds(head, 1), :], frame_count)
+        gathered[...] = jnp.zeros_like(gathered)
+        sums[...] = jnp.zeros_like(sums)
+
+    same = segment_columns[0] == segment_rows[0]
+    block = packed[0]
+    above = upstream[0]
+    query_grads, key_grads, value_grads = [], [], []
+    for head in range(heads):
+        query_rows, key_rows, value_rows, soft = head_scores(block, head, heads, same, bias[head])
+        blend_grad = above[:, head * HEAD : (head + 1) * HEAD]
+        value_grads.append(lead_dot(soft.astype(jnp.bfloat16), blend_grad))
+        soft_grad = back_dot(blend_grad, value_rows)
+        score_grad = soft * (soft_grad - jnp.sum(soft * soft_grad, axis=-1, keepdims=True))
+        gathered[head] += score_grad
+        low = (HEAD ** (-0.5) * score_grad).astype(jnp.bfloat16)
+        query_grads.append(flat_dot(low, key_rows))
+        key_grads.append(lead_dot(low, query_rows))
+    query_grad = jnp.concatenate(query_grads, axis=1)
+    value_grad = jnp.concatenate(value_grads, axis=1)
+    grads[0, :, 0:size] = query_grad.astype(jnp.bfloat16)
+    grads[0, :, size : 2 * size] = jnp.concatenate(key_grads, axis=1).astype(jnp.bfloat16)
+    grads[0, :, 2 * size :] = value_grad.astype(jnp.bfloat16)
+    sums[0:1, :] += jnp.sum(query_grad, axis=0, keepdims=True)
+    sums[1:2, :] += jnp.sum(value_grad, axis=0, keepdims=True)
+
+    @pl.when(at == pl.num_programs(0) - 1)
+    def _():
+        places = lax.broadcasted_iota(jnp.int32, (frame_count, NREL), 0)
+        for head in range(heads):
+            wide = jnp.concatenate(
+                [gathered[head], jnp.zeros((frame_count, NREL - frame_count), jnp.float32)], axis=1
+            )
+            stride = 1
+            while stride < frame_count:
+                moved = pltpu.roll(wide, NREL - stride, 1)
+                wide = jnp.where((places // stride) % 2 == 1, moved, wide)
+                stride *= 2
+            slope[pl.ds(head, 1), :] = jnp.sum(wide, axis=0, keepdims=True)
+
+
+def unattend(packed, upstream, segment_rows, segment_columns, table):
+    blocks, frame_count, width = packed.shape
+    heads = table.shape[0]
+    return pl.pallas_call(
+        functools.partial(unattend_kernel, heads),
+        grid=(blocks,),
+        out_shape=[
+            jax.ShapeDtypeStruct((blocks, frame_count, width), jnp.bfloat16),
+            jax.ShapeDtypeStruct((2, width // 3), jnp.float32),
+            jax.ShapeDtypeStruct((heads, NREL), jnp.float32),
+        ],
+        in_specs=[
+            pl.BlockSpec((1, frame_count, width), lambda i: (i, 0, 0)),
+            pl.BlockSpec((1, frame_count, width // 3), lambda i: (i, 0, 0)),
+            pl.BlockSpec((1, 1, frame_count), lambda i: (i, 0, 0)),
+            pl.BlockSpec((1, frame_count, 1), lambda i: (i, 0, 0)),
+            pl.BlockSpec((heads, NREL), lambda i: (0, 0)),
+        ],
+        out_specs=[
+            pl.BlockSpec((1, frame_count, width), lambda i: (i, 0, 0)),
+            pl.BlockSpec((2, width // 3), lambda i: (0, 0)),
+            pl.BlockSpec((heads, NREL), lambda i: (0, 0)),
+        ],
+        scratch_shapes=[
+            pltpu.VMEM((heads, frame_count, frame_count), jnp.float32),
+            pltpu.VMEM((heads, frame_count, frame_count), jnp.float32),
+        ],
+        name="unattend",
+    )(packed, upstream, segment_rows, segment_columns, table)
+
+
+MARGIN = 16
+LANES = 128
+
+
+def reach_mask(offset, behind, ahead):
+    if offset < 0:
+        return behind >= -offset
+    return ahead >= offset
+
+
+def convolve_kernel(opened, behind, ahead, taps, bias, gated, filtered, padded):
+    frame_count, channels = gated.shape[1:]
+    gates = opened[0, :, 0:channels] * jax.nn.sigmoid(opened[0, :, channels:])
+    gated[0] = gates
+    padded[pl.ds(0, MARGIN), :] = jnp.zeros((MARGIN, channels), jnp.float32)
+    padded[pl.ds(MARGIN + frame_count, MARGIN), :] = jnp.zeros((MARGIN, channels), jnp.float32)
+    padded[pl.ds(MARGIN, frame_count), :] = gates
+    back = jnp.broadcast_to(behind[0], (frame_count, LANES))
+    front = jnp.broadcast_to(ahead[0], (frame_count, LANES))
+    for low in range(0, channels, LANES):
+        lanes = slice(low, low + LANES)
+        running = jnp.broadcast_to(bias[:, lanes], (frame_count, LANES))
+        for tap in range(KW):
+            offset = tap - (KW - 1) // 2
+            moved = padded[pl.ds(MARGIN + offset, frame_count), lanes]
+            if offset:
+                moved = jnp.where(reach_mask(offset, back, front), moved, 0.0)
+            running = running + moved * taps[pl.ds(tap, 1), lanes]
+        filtered[0, :, lanes] = running
+
+
+def convolve(opened, behind, ahead, taps, bias):
+    blocks, frame_count, width = opened.shape
+    channels = width // 2
+    rows = pl.BlockSpec((1, frame_count, channels), lambda i: (i, 0, 0))
+    places = pl.BlockSpec((1, frame_count, 1), lambda i: (i, 0, 0))
+    return pl.pallas_call(
+        convolve_kernel,
+        grid=(blocks,),
+        out_shape=[jax.ShapeDtypeStruct((blocks, frame_count, channels), jnp.float32)] * 2,
+        in_specs=[
+            pl.BlockSpec((1, frame_count, width), lambda i: (i, 0, 0)),
+            places,
+            places,
+            pl.BlockSpec((KW, channels), lambda i: (0, 0)),
+            pl.BlockSpec((1, channels), lambda i: (0, 0)),
+        ],
+        out_specs=[rows, rows],
+        scratch_shapes=[pltpu.VMEM((frame_count + 2 * MARGIN, channels), jnp.float32)],
+        name="convolve",
+    )(opened, behind, ahead, taps, bias)
+
+
+def unconvolve_kernel(opened, gated, upstream, behind, ahead, taps, grads, lifts, slopes, padded, padded_grad):
+    frame_count, channels = gated.shape[1:]
+
+    @pl.when(pl.program_id(0) == 0)
+    def _():
+        lifts[...] = jnp.zeros_like(lifts)
+        slopes[...] = jnp.zeros_like(slopes)
+
+    for store, value in ((padded, gated[0]), (padded_grad, upstream[0])):
+        store[pl.ds(0, MARGIN), :] = jnp.zeros((MARGIN, channels), jnp.float32)
+        store[pl.ds(MARGIN + frame_count, MARGIN), :] = jnp.zeros((MARGIN, channels), jnp.float32)
+        store[pl.ds(MARGIN, frame_count), :] = value
+    back = jnp.broadcast_to(behind[0], (frame_count, LANES))
+    front = jnp.broadcast_to(ahead[0], (frame_count, LANES))
+    for low in range(0, channels, LANES):
+        lanes = slice(low, low + LANES)
+        above = upstream[0, :, lanes]
+        running = jnp.zeros((frame_count, LANES), jnp.float32)
+        for tap in range(KW):
+            offset = tap - (KW - 1) // 2
+            moved = padded[pl.ds(MARGIN + offset, frame_count), lanes]
+            moved_grad = padded_grad[pl.ds(MARGIN + offset, frame_count), lanes]
+            if offset:
+                mask = reach_mask(offset, back, front)
+                moved = jnp.where(mask, moved, 0.0)
+                moved_grad = jnp.where(mask, moved_grad, 0.0)
+            running = running + moved_grad * taps[pl.ds(KW - 1 - tap, 1), lanes]
+            slopes[pl.ds(tap, 1), lanes] += jnp.sum(moved * above, axis=0, keepdims=True)
+        slopes[pl.ds(KW, 1), lanes] += jnp.sum(above, axis=0, keepdims=True)
+        wide = slice(channels + low, channels + low + LANES)
+        left, gate = opened[0, :, lanes], jax.nn.sigmoid(opened[0, :, wide])
+        left_grad = running * gate
+        gate_grad = running * left * gate * (1.0 - gate)
+        grads[0, :, lanes] = left_grad.astype(jnp.bfloat16)
+        grads[0, :, wide] = gate_grad.astype(jnp.bfloat16)
+        lifts[:, lanes] += jnp.sum(left_grad, axis=0, keepdims=True)
+        lifts[:, wide] += jnp.sum(gate_grad, axis=0, keepdims=True)
+
+
+def unconvolve(opened, gated, upstream, behind, ahead, taps):
+    blocks, frame_count, width = opened.shape
+    channels = width // 2
+    wide = pl.BlockSpec((1, frame_count, width), lambda i: (i, 0, 0))
+    rows = pl.BlockSpec((1, frame_count, channels), lambda i: (i, 0, 0))
+    places = pl.BlockSpec((1, frame_count, 1), lambda i: (i, 0, 0))
+    return pl.pallas_call(
+        unconvolve_kernel,
+        grid=(blocks,),
+        out_shape=[
+            jax.ShapeDtypeStruct((blocks, frame_count, width), jnp.bfloat16),
+            jax.ShapeDtypeStruct((1, width), jnp.float32),
+            jax.ShapeDtypeStruct((KW + 1, channels), jnp.float32),
+        ],
+        in_specs=[wide, rows, rows, places, places, pl.BlockSpec((KW, channels), lambda i: (0, 0))],
+        out_specs=[
+            wide,
+            pl.BlockSpec((1, width), lambda i: (0, 0)),
+            pl.BlockSpec((KW + 1, channels), lambda i: (0, 0)),
+        ],
+        scratch_shapes=[pltpu.VMEM((frame_count + 2 * MARGIN, channels), jnp.float32)] * 2,
+        name="unconvolve",
+    )(opened, gated, upstream, behind, ahead, taps)
+
+
+def gather_rows(value):
+    return lax.all_gather(value, "fsdp", axis=0, tiled=True)
+
+
+def gather_split(value):
+    full = lax.all_gather(value, "fsdp", axis=1, tiled=True)
+    return full.reshape(-1, full.shape[-1])
+
+
+def scatter_rows(value):
+    return lax.psum_scatter(value.astype(jnp.bfloat16), "fsdp", scatter_dimension=0, tiled=True)
+
+
+def scatter_split(value, n):
+    value = value.astype(jnp.bfloat16).reshape(n, value.shape[0] // n, value.shape[1])
+    return lax.psum_scatter(value, "fsdp", scatter_dimension=1, tiled=True)
+
+
+def flat(value):
+    return value.reshape(-1, value.shape[-1])
+
+
+def split_body(
+    n,
+    m,
+    frames,
+    segments,
+    cotangent,
+    early_gain,
+    early_shift,
+    early_up,
+    early_lift,
+    early_down,
+    early_drop,
+    mixer_gain,
+    mixer_shift,
+    mixer_project,
+    query_bias,
+    value_bias,
+    mixer_output,
+    mixer_drop,
+    distance_table,
+    filter_gain,
+    filter_shift,
+    filter_up,
+    filter_lift,
+    depth_weight,
+    depth_bias,
+    middle_gain,
+    middle_shift,
+    filter_down,
+    filter_drop,
+    late_gain,
+    late_shift,
+    late_up,
+    late_lift,
+    late_down,
+    late_drop,
+    final_gain,
+    final_shift,
+):
+    me = lax.axis_index("dp")
+    frame_count = frames.shape[0]
+    rows = early_gain.shape[0]
+    hidden = early_up.shape[1] // n
+    inner = D // n
+    heads = HEADS // n
+    start_rows = frames.astype(jnp.float32)
+    final_upstream = cotangent.astype(jnp.float32)
+    singles = [
+        early_gain, early_shift, early_drop, mixer_gain, mixer_shift, query_bias, value_bias, mixer_drop,
+        filter_gain, filter_shift, depth_bias, middle_gain, middle_shift, filter_drop, late_gain, late_shift,
+        late_drop, final_gain, final_shift,
+    ]
+    at_lift = len(singles) + KW
+    spans = hidden * n // D
+    small = jnp.concatenate(
+        [
+            jnp.transpose(jnp.stack(singles)),
+            depth_weight,
+            early_lift.reshape(rows, spans),
+            late_lift.reshape(rows, spans),
+            filter_lift.reshape(rows, 2),
+            distance_table.reshape(rows, -1),
+        ],
+        axis=1,
+    )
+    small = jnp.pad(small, ((0, 0), (0, LANES - small.shape[1])))
+    sizes = [(1, hidden), (1, hidden), (3, inner), (2, inner)]
+    early_up_split, late_up_split, project_split, filter_up_split, small_all, segments_all = exchange(
+        n, m, [early_up, late_up, mixer_project, filter_up], sizes, small, segments.reshape(1, frame_count)
+    )
+    w_early_down = gather_rows(early_down)
+    w_early_up = gather_split(early_up_split)
+    w_project = gather_split(project_split)
+    w_output = gather_rows(mixer_output)
+    w_filter_up = gather_split(filter_up_split)
+    w_filter_down = gather_rows(filter_down)
+    w_late_up = gather_split(late_up_split)
+    w_late_down = gather_rows(late_down)
+
+    listed = small_all.reshape(D, LANES)
+    vectors = jnp.transpose(listed).astype(jnp.float32)
+    own_vectors = lax.dynamic_slice(vectors, (0, me * inner), (LANES, inner))
+
+    def whole(low, count):
+        return listed[:, low : low + count].astype(jnp.float32).reshape(-1)
+
+    early_lifts = lax.dynamic_slice(whole(at_lift, spans), (me * hidden,), (hidden,))
+    late_lifts = lax.dynamic_slice(whole(at_lift + spans, spans), (me * hidden,), (hidden,))
+    filter_lifts = lax.dynamic_slice(
+        whole(at_lift + 2 * spans, 2).reshape(2, D), (0, me * inner), (2, inner)
+    ).reshape(2 * inner)
+    at_table = at_lift + 2 * spans + 2
+    table = whole(at_table, NREL * HEADS // D).reshape(NREL, HEADS)
+    table = jnp.transpose(lax.dynamic_slice(table, (0, me * heads), (NREL, heads)))[:, ::-1]
+    taps = own_vectors[len(singles) : len(singles) + KW]
+    attention_shift = jnp.concatenate([own_vectors[5], jnp.zeros((inner,), jnp.float32), own_vectors[6]])
+    segment_rows = segments_all
+    segment_columns = segments_all.reshape(n, frame_count, 1)
+    places = jnp.arange(frame_count, dtype=jnp.int32)[None, :]
+    lower = (segment_rows < segment_columns).astype(jnp.int32)
+    upto = (segment_rows <= segment_columns).astype(jnp.int32)
+    behind = (places - jnp.sum(lower, axis=-1)).reshape(n, frame_count, 1)
+    ahead = (jnp.sum(upto, axis=-1) - 1 - places).reshape(n, frame_count, 1)
+
+    def blocks(value):
+        return value.reshape(n, frame_count, value.shape[-1])
+
+    def feed(hidden_rows, w_up, lifts, w_down):
+        widened = flat_dot(flat(hidden_rows), w_up) + lifts
+        active = (widened * jax.nn.sigmoid(widened)).astype(jnp.bfloat16)
+        return widened, active, blocks(flat_dot(active, w_down).astype(jnp.bfloat16))
+
+    def feed_back(low, hidden_rows, widened, active, w_up, w_down):
+        low = flat(low)
+        down_slope = scatter_rows(lead_dot(active, low))
+        widened_grad = swish_back(back_dot(low, w_down), widened)
+        widened_low = widened_grad.astype(jnp.bfloat16)
+        up_slope = scatter_split(lead_dot(flat(hidden_rows), widened_low), n)
+        part = blocks(back_dot(widened_low, w_up).astype(jnp.bfloat16))
+        return part, down_slope, up_slope, jnp.sum(widened_grad, axis=0)
+
+    (early_hidden,) = boundary(n, step_first, None, [start_rows], [vectors[0], vectors[1]], 0, 0, 1)
+    early_wide, early_active, part = feed(early_hidden, w_early_up, early_lifts, w_early_down)
+    first_rows, mixer_hidden = boundary(
+        n, functools.partial(step_forward, 0.5), part, [start_rows], [vectors[2], vectors[3], vectors[4]], 1, 0, 2
+    )
+    packed = blocks((flat_dot(flat(mixer_hidden), w_project) + attention_shift).astype(jnp.bfloat16))
+    blended = attend(packed, segment_rows, segment_columns, table)
+    part = blocks(flat_dot(flat(blended), w_output).astype(jnp.bfloat16))
+    second_rows, filter_hidden = boundary(
+        n, functools.partial(step_forward, 1.0), part, [first_rows], [vectors[7], vectors[8], vectors[9]], 1, 0, 3
+    )
+    opened = blocks(flat_dot(flat(filter_hidden), w_filter_up) + filter_lifts)
+    gated, filtered = convolve(opened, behind, ahead, taps, own_vectors[10:11])
+    filtered = flat(filtered)
+    local_mean = jnp.mean(filtered, axis=-1)
+    local_square = jnp.sum((filtered - local_mean[:, None]) ** 2, axis=-1)
+    shared = share(
+        n, jnp.concatenate([local_mean.reshape(n, frame_count), local_square.reshape(n, frame_count)]), 4
+    )
+    means, squares = shared[:, :n], shared[:, n:]
+    middle_mean = jnp.mean(means, axis=0)
+    spread = jnp.sum(squares, axis=0) + inner * jnp.sum((means - middle_mean) ** 2, axis=0)
+    middle_inverse = lax.rsqrt(spread / D + EPSILON).reshape(-1, 1)
+    middle_unit = (filtered - middle_mean.reshape(-1, 1)) * middle_inverse
+    middle = middle_unit * own_vectors[11] + own_vectors[12]
+    swished = (middle * jax.nn.sigmoid(middle)).astype(jnp.bfloat16)
+    part = blocks(flat_dot(swished, w_filter_down).astype(jnp.bfloat16))
+    third_rows, late_hidden = boundary(
+        n, functools.partial(step_forward, 1.0), part, [second_rows], [vectors[13], vectors[14], vectors[15]], 1, 0, 5
+    )
+    late_wide, late_active, part = feed(late_hidden, w_late_up, late_lifts, w_late_down)
+    layer_out, grad, low, turn_sums = boundary(
+        n, step_turn, part, [third_rows, final_upstream], [vectors[16], vectors[17], vectors[18]], 2, 3, 6
+    )
+
+    part, late_down_slope, late_up_slope, late_lift_slope = feed_back(
+        low, late_hidden, late_wide, late_active, w_late_up, w_late_down
+    )
+    grad, low, late_sums = boundary(
+        n, functools.partial(step_backward, 1.0), part, [grad, third_rows], [vectors[14]], 1, 3, 7
+    )
+    low = flat(low)
+    filter_down_slope = scatter_rows(lead_dot(swished, low))
+    middle_grad = swish_back(back_dot(low, w_filter_down), middle)
+    middle_gain_slope = jnp.sum(middle_grad * middle_unit, axis=0)
+    middle_shift_slope = jnp.sum(middle_grad, axis=0)
+    scaled = middle_grad * own_vectors[11]
+    shared = share(
+        n,
+        jnp.concatenate(
+            [
+                jnp.sum(scaled, axis=-1).reshape(n, frame_count),
+                jnp.sum(scaled * middle_unit, axis=-1).reshape(n, frame_count),
+            ]
+        ),
+        8,
+    )
+    totals = jnp.sum(shared, axis=0) / D
+    filtered_grad = middle_inverse * (
+        scaled - totals[:n].reshape(-1, 1) - middle_unit * totals[n:].reshape(-1, 1)
+    )
+    opened_low, filter_lift_slope, depth_slope = unconvolve(
+        opened, gated, blocks(filtered_grad), behind, ahead, taps
+    )
+    opened_low = flat(opened_low)
+    filter_up_slope = scatter_split(lead_dot(flat(filter_hidden), opened_low), n)
+    part = blocks(back_dot(opened_low, w_filter_up).astype(jnp.bfloat16))
+    grad, low, filter_sums = boundary(
+        n, functools.partial(step_backward, 1.0), part, [grad, second_rows], [vectors[8]], 1, 3, 9
+    )
+    low = flat(low)
+    output_slope = scatter_rows(lead_dot(flat(blended), low))
+    blend_grad = blocks(back_dot(low, w_output).astype(jnp.bfloat16))
+    packed_low, shift_sums, table_slope = unattend(packed, blend_grad, segment_rows, segment_columns, table)
+    packed_low = flat(packed_low)
+    project_slope = scatter_split(lead_dot(flat(mixer_hidden), packed_low), n)
+    part = blocks(back_dot(packed_low, w_project).astype(jnp.bfloat16))
+    grad, low, mixer_sums = boundary(
+        n, functools.partial(step_backward, 0.5), part, [grad, first_rows], [vectors[3]], 1, 3, 10
+    )
+    part, early_down_slope, early_up_slope, early_lift_slope = feed_back(
+        low, early_hidden, early_wide, early_active, w_early_up, w_early_down
+    )
+    slope_frames, early_sums = boundary(
+        n, step_last, part, [grad, start_rows], [vectors[0]], 1, 2, 11, gathered=False
+    )
+
+    table_slope = jnp.roll(table_slope[:, ::-1], 1 - NREL // 2, axis=1)
+    table_rows = NREL // (n * m)
+    wide = jnp.concatenate([turn_sums, late_sums, filter_sums, mixer_sums, early_sums])
+    wide_count = wide.shape[0]
+    wide = jnp.transpose(wide.reshape(wide_count, n * m, rows), (1, 0, 2)).reshape(n * m, wide_count * rows)
+    wide = jnp.concatenate(
+        [wide, jnp.transpose(table_slope.reshape(heads, n * m, table_rows), (1, 0, 2)).reshape(n * m, -1)], axis=1
+    )
+    lift_full = lax.dynamic_update_slice(
+        jnp.zeros((2, D), jnp.float32), filter_lift_slope.reshape(2, inner), (0, me * inner)
+    ).reshape(n * m, -1)
+    table_used = wide.shape[1]
+    wide = jnp.concatenate([wide, lift_full], axis=1)
+    wide_used = wide.shape[1]
+    wide = jnp.pad(wide, ((0, 0), (0, -wide_used % LANES))).reshape(n * m, -1, LANES)
+    group = jnp.concatenate(
+        [
+            shift_sums,
+            middle_gain_slope[None],
+            middle_shift_slope[None],
+            depth_slope,
+            jnp.transpose(early_lift_slope.reshape(inner, spans)),
+            jnp.transpose(late_lift_slope.reshape(inner, spans)),
+        ]
+    )
+    group_count = group.shape[0]
+    group = jnp.transpose(group.reshape(group_count, m, rows), (1, 0, 2)).reshape(m, group_count * rows)
+    group_used = group.shape[1]
+    group = jnp.pad(group, ((0, 0), (0, -group_used % LANES))).reshape(m, -1, LANES)
+    wide_all, group_all = collect(n, m, wide, group, 12)
+    tables = wide_all.reshape(n, m, -1)[:, :, wide_count * rows : table_used]
+    wide = jnp.sum(wide_all, axis=0).reshape(-1)
+    lift_total = wide[table_used:wide_used]
+    wide = wide[: wide_count * rows].reshape(wide_count, rows)
+    tables = jnp.transpose(jnp.sum(tables, axis=1).reshape(HEADS, table_rows))
+    group = jnp.sum(group_all, axis=0).reshape(-1)[:group_used].reshape(group_count, rows)
+    late_up_wide, project_wide, filter_up_wide = giveback(
+        n, [late_up_slope, project_slope, filter_up_slope], sizes[1:], 13
+    )
+    (early_up_wide,) = giveback(n, [early_up_slope], sizes[:1], 14)
+
+    def final(value):
+        return value.astype(jnp.float32)
+
+    lift_slopes = KW + 5
+    return (
+        layer_out,
+        slope_frames,
+        wide[12],
+        wide[13],
+        final(early_up_wide),
+        jnp.transpose(group[lift_slopes : lift_slopes + spans]).reshape(-1),
+        final(early_down_slope),
+        wide[11],
+        wide[9],
+        wide[10],
+        final(project_wide),
+        group[0],
+        group[1],
+        final(output_slope),
+        wide[8],
+        tables,
+        wide[6],
+        wide[7],
+        final(filter_up_wide),
+        lift_total,
+        jnp.transpose(group[4 : 4 + KW]),
+        group[4 + KW],
+        group[2],
+        group[3],
+        final(filter_down_slope),
+        wide[5],
+        wide[3],
+        wide[4],
+        final(late_up_wide),
+        jnp.transpose(group[lift_slopes + spans : lift_slopes + 2 * spans]).reshape(-1),
+        final(late_down_slope),
+        wide[2],
+        wide[0],
+        wide[1],
+    )
+
+
 def solution(mesh):
     in_specs = (
         P(("dp", "fsdp"), None),
@@ -669,4 +1666,6 @@
         P(("dp", "fsdp")),
         P(("dp", "fsdp")),
     )
-    return jax.shard_map(body, mesh=mesh, in_specs=in_specs, out_specs=out_specs, check_vma=False)
+    n, m = mesh.shape["dp"], mesh.shape["fsdp"]
+    run = functools.partial(split_body, n, m) if n == 4 and D // (n * m) == 32 else body
+    return jax.shard_map(run, mesh=mesh, in_specs=in_specs, out_specs=out_specs, check_vma=False)

time: 2350 us -> 627 us (0.27)
  waiting for transfers between devices: 1830 us -> 127 us
  Pallas kernels: 0 us -> 296 us
  blocking collectives: 202 us -> 33 us
  matrix products: 197 us -> 77.8 us
  local copies, waits for them, and re-layouts: 79 us -> 42.5 us
    reduce_scatter x8, waiting for transfers between devices: 1350 us -> 124 us  [the longest x4 65.2 us: scatter_split(): return lax.psum_scatter(value, 'fsdp', scatter_dimension=1, tiled=True)]
    pallas_call x0 -> x19, Pallas kernels: none -> 296 us  [the longest x9 202 us: boundary(): pl.pallas_call(functools.partial(boundary_kernel, n, step, shape), out_sh...]
    all_gather x8 -> x6, waiting for transfers between devices: 288 us -> 0.11 us  [the longest x4 0.08 us: gather_split(): full = lax.all_gather(value, 'fsdp', axis=1, tiled=True)]
    unnamed x20 -> x14, waiting for transfers between devices: 189 us -> 3.1 us
    all_gather x4 -> x2, blocking collectives: 157 us -> 33 us  [gather_rows(): return lax.all_gather(value, 'fsdp', axis=0, tiled=True)]
    conv_general_dilated x12 -> x0, matrix products: 72.4 us -> none  [depthwise(): lax.conv_general_dilated(masked_rows[None], taps, (1,), ((margin, margin)...]
    unnamed x273 -> x77, local copies, waits for them, and re-layouts: 62.5 us -> 7.05 us
    unnamed x1 -> x0, blocking collectives: 44.3 us -> none
  transfers between devices with their start and end apart: 18 -> 14, of which waited for: 15 -> 4; matrix products, arithmetic and copies ran while one was open for 7% -> 17% of each run, Pallas kernels for 0% -> 35%
where the time goes in v1:
time: 627 us; the launch traced here: 620 us
  Pallas kernels  296 us (47%)
  waiting for transfers between devices  127 us (20%)
  matrix products  77.8 us (12%)
  local copies, waits for them, and re-layouts  42.5 us (7%)
  blocking collectives  33 us (5%)
  other arithmetic  28 us (4%)
  between operations  14.9 us (2%)
    pallas_call x9, Pallas kernels, boundary(): pl.pallas_call(functools.partial(boundary_kernel, n, step, shape), out_sh...  202 us
    reduce_scatter x4, waiting for transfers between devices, scatter_split(): return lax.psum_scatter(value, 'fsdp', scatter_dimension=1, tiled=True)  65.2 us
    reduce_scatter x4, waiting for transfers between devices, scatter_rows(): lax.psum_scatter(value.astype(jnp.bfloat16), 'fsdp', scatter_dimension=0,...  58.4 us
    all_gather x2, blocking collectives, gather_rows(): return lax.all_gather(value, 'fsdp', axis=0, tiled=True)  33 us
    dot_general x8, matrix products, flat_dot(): return jnp.dot(left_rows, right_rows, preferred_element_type=jnp.float32)  27.7 us
    dot_general x8, matrix products, lead_dot(): lax.dot_general(left_rows, right_rows, (((0,), (0,)), ((), ())), preferre...  25.6 us
    dot_general x8, matrix products, back_dot(): lax.dot_general(left_rows, right_rows, (((1,), (1,)), ((), ())), preferre...  24.6 us
    pallas_call x1, Pallas kernels, exchange(): pl.pallas_call(functools.partial(exchange_kernel, n, m, sizes), out_shape...  22.3 us
  transfers between devices with their start and end apart: 14, of which 4 were waited for; matrix products, arithmetic and copies ran while one was open for 17% of the time, Pallas kernels for 35%

profile of v1, /device:TPU:0, one launch (start us, length us, event | category | flops | bytes accessed | tf_op | source)
XLA Modules:
  0.0 620.0 jit_solution(2450018806025538888)
XLA Ops:
  26.2 22.3 %exchange.1 = (bf16[4,32,1024]{2,1,0:T(8,128)(2,1)}, bf16[4,32,1024]{2,1,0:T(8,128)(2,1)}, bf16[4,32,768]{2,1,0:T(8,128)(2,1)}, bf16[4,32,512]{2,1,0:T(8,128)(2,...) custom-call(bf16[32,4096]{1,0:T(8,128)(2,1)} %refs_0_.1, bf16[32,4096]{1,0:T(8,128)(2,1)} %refs_1_.1, ...), custom_call_target="tpu_custom_call" | custom-call | tf_op jit(solution)/shard_map/exchange/pallas_call | solution.py:708
  57.4 17.2 %all_gather.27 = bf16[256,1024]{1,0:T(8,128)(2,1)S(1)} all-gather(bf16[32,1024]{1,0:T(8,128)(2,1)S(1)} %copy-done.10), channel_id=1, replica_groups=mesh['dp'=4,'fsdp'=8] {'fsdp'}, dimensions={0}, use_global_device_ids=true | all-gather | bytes 589824 | tf_op jit(solution)/shard_map/all_gather | solution.py:1283
  74.6 15.8 %all_gather.29 = bf16[256,1024]{1,0:T(8,128)(2,1)} all-gather(bf16[32,1024]{1,0:T(8,128)(2,1)S(1)} %copy-done.11), channel_id=1, replica_groups=mesh['dp'=4,'fsdp'=8] {'fsdp'}, dimensions={0}, use_global_device_ids=true | all-gather | bytes 589824 | tf_op jit(solution)/shard_map/all_gather | solution.py:1283
  95.8 16.8 %boundary.9 = bf16[4,128,1024]{2,1,0:T(8,128)(2,1)} custom-call(f32[128,1024]{1,0:T(8,128)} %convert_element_type.122.refs_0_.refs_1_.refs_2_, f32[2,1024]{1,0:T(2,128)} %stack.88.refs_1_), custom_call_target="tpu_custom_call" | custom-call | tf_op jit(solution)/shard_map/boundary/pallas_call | solution.py:1022
  115.9 4.6 convolution_convert_fusion.10
  120.5 28.4 %boundary.10 = (f32[128,1024]{1,0:T(8,128)}, bf16[4,128,1024]{2,1,0:T(8,128)(2,1)}) custom-call(bf16[4,128,1024]{2,1,0:T(8,128)(2,1)} %bitcast.186, f32[128,1024]{1,0:T(8,128)} %convert_element_type.122.refs_0_.refs_1_.refs_2_, f32[3,1024]{1,0:T(4,128)} %get-tuple-element.233.refs_2_), custom_call_target="tpu_custom_call" | custom-call | tf_op jit(solution)/shard_map/boundary/pallas_call | solution.py:1022
  152.6 8.1 %attend.1 = bf16[4,128,256]{2,1,0:T(8,128)(2,1)} custom-call(bf16[4,128,768]{2,1,0:T(8,128)(2,1)} %bitcast.175, s32[4,1,128]{2,1,0:T(1,128)} %get-tuple-element.78.segment_rows, s32[4,128,1]{2,1,0:T(8,128)} %copy.163.segment_columns, f32[4,256]{1,0:T(4,128)} %rev.4.table), custom_call_target="tpu_custom_call" | custom-call | tf_op jit(solution)/shard_map/attend/pallas_call | solution.py:1069
  163.1 27.2 %boundary.11 = (f32[128,1024]{1,0:T(8,128)}, bf16[4,128,1024]{2,1,0:T(8,128)(2,1)}) custom-call(bf16[4,128,1024]{2,1,0:T(8,128)(2,1)} %bitcast.172, f32[128,1024]{1,0:T(8,128)} %get-tuple-element.79.refs_1_.refs_2_, f32[3,1024]{1,0:T(4,128)} %get-tuple-element.232.refs_2_), custom_call_target="tpu_custom_call" | custom-call | tf_op jit(solution)/shard_map/boundary/pallas_call | solution.py:1022
  193.7 5.0 convolve.1
  201.8 5.9 share.2
  212.0 25.7 %boundary.12 = (f32[128,1024]{1,0:T(8,128)}, bf16[4,128,1024]{2,1,0:T(8,128)(2,1)}) custom-call(bf16[4,128,1024]{2,1,0:T(8,128)(2,1)} %bitcast.185, f32[128,1024]{1,0:T(8,128)} %get-tuple-element.83.refs_1_.refs_2_, f32[3,1024]{1,0:T(4,128)} %get-tuple-element.231.refs_2_), custom_call_target="tpu_custom_call" | custom-call | tf_op jit(solution)/shard_map/boundary/pallas_call | solution.py:1022
  237.8 4.5 fusion.27
  242.3 4.5 convolution_convert_fusion.7
  246.8 24.9 %boundary.13 = (f32[128,1024]{1,0:T(8,128)}, f32[128,1024]{1,0:T(8,128)}, bf16[4,128,1024]{2,1,0:T(8,128)(2,1)}, f32[3,1024]{1,0:T(4,128)}) custom-call(bf16[4,128,1024]{2,1,0:T(8,128)(2,1)} %bitcast.188, f32[128,1024]{1,0:T(8,128)} %get-tuple-element.86.refs_1_.refs_2_, f32[128,1024]{1,0:T(8,128)} %convert_element_type.135.refs_2_, ...), custom_call_target="tpu_custom_call" | custom-call | tf_op jit(solution)/shard_map/boundary/pallas_call | solution.py:1022
  271.7 4.4 fusion.25
  278.4 23.6 %boundary.14 = (f32[128,1024]{1,0:T(8,128)}, bf16[4,128,1024]{2,1,0:T(8,128)(2,1)}, f32[3,1024]{1,0:T(4,128)}) custom-call(bf16[4,128,1024]{2,1,0:T(8,128)(2,1)} %bitcast.190, f32[128,1024]{1,0:T(8,128)} %get-tuple-element.90.refs_1_, f32[128,1024]{1,0:T(8,128)} %get-tuple-element.86.refs_1_.refs_2_, f32[1,1024]{1,0:T(1,128)} %get-tuple-element.229.refs_3_), custom_call_target="tpu_custom_call" | custom-call | tf_op jit(solution)/shard_map/boundary/pallas_call | solution.py:1022
  307.3 5.9 share.3
  315.2 9.0 %unconvolve.1 = (bf16[4,128,512]{2,1,0:T(8,128)(2,1)}, f32[1,512]{1,0:T(1,128)}, f32[32,256]{1,0:T(8,128)}) custom-call(f32[4,128,512]{2,1,0:T(8,128)} %bitcast.174, f32[4,128,256]{2,1,0:T(8,128)} %get-tuple-element.88.gated, f32[4,128,256]{2,1,0:T(8,128)} %bitcast.180, s32[4,128,1]{2,1,0:T(8,128)} %get-tuple-element.273.behind, ...), custom_call_target="tpu_custom_call" | custom-call | tf_op jit(solution)/shard_map/unconvolve/pallas_call | solution.py:1263
  327.0 21.5 %boundary.15 = (f32[128,1024]{1,0:T(8,128)}, bf16[4,128,1024]{2,1,0:T(8,128)(2,1)}, f32[3,1024]{1,0:T(4,128)}) custom-call(bf16[4,128,1024]{2,1,0:T(8,128)(2,1)} %bitcast.191, f32[128,1024]{1,0:T(8,128)} %get-tuple-element.93.refs_1_, f32[128,1024]{1,0:T(8,128)} %get-tuple-element.83.refs_1_.refs_2_, f32[1,1024]{1,0:T(1,128)} %get-tuple-element.228.refs_3_), custom_call_target="tpu_custom_call" | custom-call | tf_op jit(solution)/shard_map/boundary/pallas_call | solution.py:1022
  351.0 12.0 %unattend.1 = (bf16[4,128,768]{2,1,0:T(8,128)(2,1)}, f32[2,256]{1,0:T(2,128)}, f32[4,256]{1,0:T(4,128)}) custom-call(bf16[4,128,768]{2,1,0:T(8,128)(2,1)} %bitcast.176, bf16[4,128,256]{2,1,0:T(8,128)(2,1)} %bitcast.197, s32[4,1,128]{2,1,0:T(1,128)} %get-tuple-element.78.segment_rows, s32[4,128,1]{2,1,0:T(8,128)} %copy.163.segment_columns, f32[4,256]{1,0:T(4,128)} %rev.4.table), custom_call_target="tpu_custom_call" | custom-call | tf_op jit(solution)/shard_map/unattend/pallas_call | solution.py:1137
  367.7 20.4 %boundary.16 = (f32[128,1024]{1,0:T(8,128)}, bf16[4,128,1024]{2,1,0:T(8,128)(2,1)}, f32[3,1024]{1,0:T(4,128)}) custom-call(bf16[4,128,1024]{2,1,0:T(8,128)(2,1)} %bitcast.192, f32[128,1024]{1,0:T(8,128)} %get-tuple-element.96.refs_1_, f32[128,1024]{1,0:T(8,128)} %get-tuple-element.79.refs_1_.refs_2_, f32[1,1024]{1,0:T(1,128)} %get-tuple-element.227.refs_3_), custom_call_target="tpu_custom_call" | custom-call | tf_op jit(solution)/shard_map/boundary/pallas_call | solution.py:1022
  402.4 3.9 convolution_convert_fusion.1
  407.5 4.3 convolution_convert_fusion.2
  413.1 4.3 convolution_convert_fusion
  425.1 13.2 %boundary.17 = (f32[128,1024]{1,0:T(8,128)}, f32[2,1024]{1,0:T(2,128)}) custom-call(bf16[4,128,1024]{2,1,0:T(8,128)(2,1)} %bitcast.189, f32[128,1024]{1,0:T(8,128)} %get-tuple-element.98.refs_1_, f32[128,1024]{1,0:T(8,128)} %convert_element_type.122.refs_0_.refs_1_.refs_2_, f32[1,1024]{1,0:T(1,128)} %get-tuple-element.226.refs_3_), custom_call_target="tpu_custom_call" | custom-call | tf_op jit(solution)/shard_map/boundary/pallas_call | solution.py:1022
  440.3 11.0 %collect.1 = (f32[32,5,128]{2,1,0:T(8,128)}, f32[8,11,128]{2,1,0:T(8,128)}) custom-call(f32[32,5,128]{2,1,0:T(8,128)} %reshape.454.wide, f32[8,11,128]{2,1,0:T(8,128)} %reshape.457.group), custom_call_target="tpu_custom_call" | custom-call | tf_op jit(solution)/shard_map/collect/pallas_call | solution.py:841
  462.1 7.0 %giveback.2 = bf16[32,4096]{1,0:T(8,128)(2,1)} custom-call(bf16[4,32,1024]{2,1,0:T(8,128)(2,1)} %reduce-scatter.9.cloned.1.call-done.refs_0_), custom_call_target="tpu_custom_call" | custom-call | tf_op jit(solution)/shard_map/giveback/pallas_call | solution.py:751
  470.9 28.7 %reduce-scatter.15.cloned.1.call-done.refs_1_ = bf16[4,32,768]{2,1,0:T(8,128)(2,1)} async-done(((bf16[4,256,768]{2,1,0:T(8,128)(2,1)}), bf16[4,32,768]{2,1,0:T(8,128)(2,1)}) %reduce-scatter.15.cloned.1.call-update) | async-done | bytes 196624 | tf_op jit(solution)/shard_map/reduce_scatter | solution.py:1297
  499.6 36.5 %reduce-scatter.13.cloned.1.call-done.refs_0_ = bf16[4,32,1024]{2,1,0:T(8,128)(2,1)} async-done(((bf16[4,256,1024]{2,1,0:T(8,128)(2,1)}), bf16[4,32,1024]{2,1,0:T(8,128)(2,1)}) %reduce-scatter.13.cloned.1.call-update) | async-done | bytes 262160 | tf_op jit(solution)/shard_map/reduce_scatter | solution.py:1297
  536.1 8.5 %giveback.3 = (bf16[32,4096]{1,0:T(8,128)(2,1)}, bf16[32,3072]{1,0:T(8,128)(2,1)}, bf16[32,2048]{1,0:T(8,128)(2,1)}) custom-call(bf16[4,32,1024]{2,1,0:T(8,128)(2,1)} %reduce-scatter.13.cloned.1.call-done.refs_0_, bf16[4,32,768]{2,1,0:T(8,128)(2,1)} %reduce-scatter.15.cloned.1.call-done.refs_1_, bf16[4,32,512]{2,1,0:T(8,128)(2,1)} %reduce-scatter.17.cloned.1.call-done.refs_2_), custom_call_target="tpu_custom_call" | custom-call | tf_op jit(solution)/shard_map/giveback/pallas_call | solution.py:751
  549.7 23.3 %reduce-scatter.11.cloned.1.call-done = bf16[128,1024]{1,0:T(8,128)(2,1)} async-done(((bf16[1024,1024]{1,0:T(8,128)(2,1)}), bf16[128,1024]{1,0:T(8,128)(2,1)}) %reduce-scatter.11.cloned.1.call-update) | async-done | bytes 262160 | tf_op jit(solution)/shard_map/reduce_scatter | solution.py:1292
  574.9 35.0 %reduce-scatter.23.cloned.1.call-done = bf16[128,1024]{1,0:T(8,128)(2,1)} async-done(((bf16[1024,1024]{1,0:T(8,128)(2,1)}), bf16[128,1024]{1,0:T(8,128)(2,1)}) %reduce-scatter.23.cloned.1.call-update) | async-done | bytes 262160 | tf_op jit(solution)/shard_map/reduce_scatter | solution.py:1292
  (255 shorter events, 121.4 us)
Async XLA Ops:
  7.2 105.5 %all-gather.7.cloned.1.call-start = ((), (), s32[]{:S(2)}) async-start(), calls=%async_computation.8 | async-start | bytes 2359296 | tf_op jit(solution)/shard_map/all_gather | solution.py:1287
  48.5 4.4 copy-start.1
  48.5 67.4 %all-gather.9.cloned.1.call-start = ((), (), s32[]{:S(2)}) async-start(), calls=%async_computation.9 | async-start | bytes 2359296 | tf_op jit(solution)/shard_map/all_gather | solution.py:1283
  49.3 99.7 %all-gather.11.cloned.1.call-start = ((), (), s32[]{:S(2)}) async-start(), calls=%async_computation.10 | async-start | bytes 1769472 | tf_op jit(solution)/shard_map/all_gather | solution.py:1287
  50.0 140.3 %all-gather.13.cloned.1.call-start = ((), (), s32[]{:S(2)}) async-start(), calls=%async_computation.11 | async-start | bytes 1179648 | tf_op jit(solution)/shard_map/all_gather | solution.py:1287
  50.6 187.2 %all-gather.15.cloned.1.call-start = ((), (), s32[]{:S(2)}) async-start(), calls=%async_computation.12 | async-start | bytes 2359296 | tf_op jit(solution)/shard_map/all_gather | solution.py:1287
  51.2 191.1 %all-gather.17.cloned.1.call-start = ((), (), s32[]{:S(2)}) async-start(), calls=%async_computation.13 | async-start | bytes 2359296 | tf_op jit(solution)/shard_map/all_gather | solution.py:1283
  51.8 407.3 %reduce-scatter.21.cloned.1.call-start = ((), (), s32[]{:S(2)}) async-start(), calls=%async_computation.20 | async-start | bytes 589824 | tf_op jit(solution)/shard_map/reduce_scatter | solution.py:1292
  53.2 21.4 %copy-start.11 = (bf16[32,1024]{1,0:T(8,128)(2,1)S(1)}, bf16[32,1024]{1,0:T(8,128)(2,1)}, u32[]{:S(2)}) copy-start(bf16[32,1024]{1,0:T(8,128)(2,1)} %param.60) | copy-start | bytes 196612
  56.3 34.1 %copy-start.9 = (bf16[128,1024]{1,0:T(8,128)(2,1)S(1)}, bf16[128,1024]{1,0:T(8,128)(2,1)}, u32[]{:S(2)}) copy-start(bf16[128,1024]{1,0:T(8,128)(2,1)} %param.37) | copy-start | bytes 786436
  56.3 35.0 %copy-start.12 = (s32[4,1,128]{2,1,0:T(1,128)S(1)}, s32[4,1,128]{2,1,0:T(1,128)}, u32[]{:S(2)}) copy-start(s32[4,1,128]{2,1,0:T(1,128)} %get-tuple-element.78.segment_rows) | copy-start | bytes 6148
  115.9 4.7 copy-start.31
  193.7 16.9 %copy-start.5 = (bf16[256,1024]{1,0:T(8,128)(2,1)S(1)}, bf16[256,1024]{1,0:T(8,128)(2,1)}, u32[]{:S(2)}) copy-start(bf16[256,1024]{1,0:T(8,128)(2,1)} %all_gather.29) | copy-start | bytes 1572868
  271.7 4.5 copy-start.23
  278.4 23.6 %copy-start = (f32[4,128,256]{2,1,0:T(8,128)S(1)}, f32[4,128,256]{2,1,0:T(8,128)}, u32[]{:S(2)}) copy-start(f32[4,128,256]{2,1,0:T(8,128)} %get-tuple-element.82) | copy-start | bytes 1572868
  314.0 146.6 %reduce-scatter.19.cloned.1.call-start = ((), (), s32[]{:S(2)}) async-start(), calls=%async_computation.19 | async-start | bytes 589824 | tf_op jit(solution)/shard_map/reduce_scatter | solution.py:1292
  315.1 9.0 %copy-start.24 = (bf16[4,256,512]{2,1,0:T(8,128)(2,1)S(1)}, bf16[4,256,512]{2,1,0:T(8,128)(2,1)}, u32[]{:S(2)}) copy-start(bf16[4,256,512]{2,1,0:T(8,128)(2,1)} %all-gather.13.cloned.1.call-done) | copy-start | bytes 3145732
  348.5 14.5 %copy-start.2 = (bf16[4,128,256]{2,1,0:T(8,128)(2,1)S(1)}, bf16[4,128,256]{2,1,0:T(8,128)(2,1)}, u32[]{:S(2)}) copy-start(bf16[4,128,256]{2,1,0:T(8,128)(2,1)} %attend.1) | copy-start | bytes 786436
  348.5 14.5 %copy-start.3 = (bf16[4,128,1024]{2,1,0:T(8,128)(2,1)S(1)}, bf16[4,128,1024]{2,1,0:T(8,128)(2,1)}, u32[]{:S(2)}) copy-start(bf16[4,128,1024]{2,1,0:T(8,128)(2,1)} %get-tuple-element.94) | copy-start | bytes 3145732
  364.3 97.8 %reduce-scatter.9.cloned.1.call-start = ((), (), s32[]{:S(2)}) async-start(), calls=%async_computation.14 | async-start | bytes 2359296 | tf_op jit(solution)/shard_map/reduce_scatter | solution.py:1297
  367.7 20.4 %copy-start.22 = (bf16[1024,1024]{1,0:T(8,128)(2,1)S(1)}, bf16[1024,1024]{1,0:T(8,128)(2,1)}, u32[]{:S(2)}) copy-start(bf16[1024,1024]{1,0:T(8,128)(2,1)} %all-gather.9.cloned.1.call-done) | copy-start | bytes 6291460
  394.6 76.2 %reduce-scatter.17.cloned.1.call-start = ((), (), s32[]{:S(2)}) async-start(), calls=%async_computation.18 | async-start | bytes 1179648 | tf_op jit(solution)/shard_map/reduce_scatter | solution.py:1297
  398.7 100.9 %reduce-scatter.15.cloned.1.call-start = ((), (), s32[]{:S(2)}) async-start(), calls=%async_computation.17 | async-start | bytes 1769472 | tf_op jit(solution)/shard_map/reduce_scatter | solution.py:1297
  402.3 133.7 %reduce-scatter.13.cloned.1.call-start = ((), (), s32[]{:S(2)}) async-start(), calls=%async_computation.16 | async-start | bytes 2359296 | tf_op jit(solution)/shard_map/reduce_scatter | solution.py:1297
  406.3 166.7 %reduce-scatter.11.cloned.1.call-start = ((), (), s32[]{:S(2)}) async-start(), calls=%async_computation.15 | async-start | bytes 2359296 | tf_op jit(solution)/shard_map/reduce_scatter | solution.py:1292
  411.9 198.0 %reduce-scatter.23.cloned.1.call-start = ((), (), s32[]{:S(2)}) async-start(), calls=%async_computation.21 | async-start | bytes 2359296 | tf_op jit(solution)/shard_map/reduce_scatter | solution.py:1292
  425.1 13.2 %copy-start.14 = (f32[3,1024]{1,0:T(4,128)S(1)}, f32[3,1024]{1,0:T(4,128)}, u32[]{:S(2)}) copy-start(f32[3,1024]{1,0:T(4,128)} %get-tuple-element.100) | copy-start | bytes 36868
  425.1 13.2 %copy-start.15 = (f32[3,1024]{1,0:T(4,128)S(1)}, f32[3,1024]{1,0:T(4,128)}, u32[]{:S(2)}) copy-start(f32[3,1024]{1,0:T(4,128)} %get-tuple-element.101) | copy-start | bytes 36868
  425.1 13.2 %copy-start.16 = (f32[3,1024]{1,0:T(4,128)S(1)}, f32[3,1024]{1,0:T(4,128)}, u32[]{:S(2)}) copy-start(f32[3,1024]{1,0:T(4,128)} %get-tuple-element.102) | copy-start | bytes 36868
  425.1 13.2 %copy-start.17 = (f32[3,1024]{1,0:T(4,128)S(1)}, f32[3,1024]{1,0:T(4,128)}, u32[]{:S(2)}) copy-start(f32[3,1024]{1,0:T(4,128)} %get-tuple-element.103) | copy-start | bytes 36868
  470.9 140.8 %copy-start.6 = (f32[128,1024]{1,0:T(8,128)S(1)}, f32[128,1024]{1,0:T(8,128)}, u32[]{:S(2)}) copy-start(f32[128,1024]{1,0:T(8,128)} %get-tuple-element.312) | copy-start | bytes 1572868
  544.6 67.9 %copy-start.7 = (f32[128,1024]{1,0:T(8,128)S(1)}, f32[128,1024]{1,0:T(8,128)}, u32[]{:S(2)}) copy-start(f32[128,1024]{1,0:T(8,128)} %get-tuple-element.313) | copy-start | bytes 1572868
  (16 other events, 40.6 us)
Sparse Core Ops, SparseCore 0:
  48.7 32.2 all-gather.6
  82.5 28.4 all-gather.8
  112.7 24.6 all-gather.10
  138.8 21.4 all-gather.12
  161.7 28.6 all-gather.14
  191.9 28.5 all-gather.16
  314.1 29.0 reduce-scatter.20
  364.4 28.8 reduce-scatter.18
  395.6 34.2 reduce-scatter.8
  432.0 32.4 reduce-scatter.16
  466.8 32.7 reduce-scatter.14
  501.7 34.3 reduce-scatter.12
  538.3 34.6 reduce-scatter.10
  575.2 34.6 reduce-scatter.22

commit v2 on v1

--- a/solution.py
+++ b/solution.py
@@ -18,6 +18,10 @@
 MASKED = -1e30
 UTTERANCE_LIMIT = 4
 MESH = pl.DeviceIdType.MESH
+PIECES = 4
+BLOCK = 16
+MARGIN = 16
+LANES = 128
 
 
 def flat_dot(left_rows, right_rows):
@@ -639,31 +643,87 @@
     return pl.ds(pl.multiple_of(start * width, width), width)
 
 
-def column_pieces(index, sizes):
+def column_pieces(index, n, sizes):
     pieces = []
     for place, (groups, width) in enumerate(sizes):
-        whole = width * index[2]
         for group in range(groups):
-            wide = pl.ds(pl.multiple_of(group * whole + index[0] * width, width), width)
+            wide = pl.ds(pl.multiple_of((group * n + index) * width, width), width)
             pieces.append((place, wide, pl.ds(group * width, width)))
     return pieces
 
 
-def exchange_kernel(n, m, sizes, *refs):
-    count = len(sizes)
-    wides = refs[:count]
-    small, segs = refs[count : count + 2]
-    narrows = refs[count + 2 : 2 * count + 2]
-    small_all, segs_all, local, send, recv, small_send, small_recv = refs[2 * count + 2 :]
+def row_of(shards, first):
+    rows = shards.shape[0]
+    lines = shards[:, 0, :]
+    lanes = lax.broadcasted_iota(jnp.int32, lines.shape, 1) // 32
+    places = lax.broadcasted_iota(jnp.int32, lines.shape, 0) % 4
+    merged = jnp.zeros_like(lines)
+    for quarter in range(4):
+        shift = (32 * quarter - 32 * first) % LANES
+        moved = pltpu.roll(lines, shift, 1) if shift else lines
+        merged = merged + jnp.where((lanes == quarter) & (places == quarter), moved, 0.0)
+    return [
+        jnp.sum(merged[4 * tile : 4 * tile + 4], axis=0, keepdims=True) for tile in range(rows // 4)
+    ]
+
+
+def pack_small(small, singles, lifts, table):
+    rows = singles[0].shape[0]
+    small[...] = jnp.zeros_like(small)
+    for at, single in enumerate(singles):
+        line, low = at * rows // LANES, at * rows % LANES
+        small[line : line + 1, low : low + rows] = single[...].astype(jnp.float32).reshape(1, rows)
+    for at, lift in enumerate(lifts):
+        line, count = 5 + at, lift.shape[0]
+        small[line : line + 1, 0:count] = lift[...].astype(jnp.float32).reshape(1, count)
+    small[8 : 8 + table.shape[0], 0 : table.shape[1]] = table[...].astype(jnp.float32)
+
+
+def exchange_kernel(n, m, width, inner, *refs):
+    early_up, late_up, project, filter_up, output, filter_down, depth, segs, frames = refs[:9]
+    singles, lifts, table = refs[9:28], refs[28:31], refs[31]
+    early_full, late_split, mixer_split, filter_split, small_all, depth_all, segs_all, spread = refs[32:40]
+    scratch = refs[40:]
+    small, gains, held, local, send, recv, small_send, small_recv = scratch[:8]
+    up_send, up_recv, pass_send, pass_recv, out_send, out_recv, depth_send, depth_recv = scratch[8:]
+    pack_small(small, singles, lifts, table)
     me, lane = lax.axis_index("dp"), lax.axis_index("fsdp")
     here = me * m + lane
+    half = m // 2
+    beside = lane + 1 - 2 * (lane % 2)
+    others = near(me, n)
     greet_all(n, m)
-    others = near(me, n)
 
     def to_device(step):
         target = {"dp": (me + step // m) % n, "fsdp": (lane + step % m) % m}
         return remote(small, small_all.at[here], small_send.at[step], small_recv.at[step], target)
 
+    def to_lane(step):
+        return remote(
+            depth, depth_all.at[lane], depth_send.at[step], depth_recv.at[step], {"fsdp": (lane + step) % m}
+        )
+
+    def start_depth(step, carry):
+        to_lane(step).start()
+        return carry
+
+    def wait_depth(step, carry):
+        to_lane(step).wait()
+        return carry
+
+    def to_column(step):
+        other, above = (me + step // half) % n, (lane + 2 * (step % half)) % m
+        target = {"dp": other, "fsdp": above}
+        return remote(
+            early_up.at[:, columns(other, width)], early_full.at[here], up_send.at[step], up_recv.at[step], target
+        )
+
+    def to_partner(step):
+        source = ((me + n - step // half) % n) * m + (lane + m - 2 * (step % half)) % m
+        return remote(
+            early_full.at[source], early_full.at[source], pass_send.at[step], pass_recv.at[step], {"fsdp": beside}
+        )
+
     def start_small(step, carry):
         to_device(step).start()
         return carry
@@ -672,54 +732,130 @@
         to_device(step).wait()
         return carry
 
+    def start_column(step, carry):
+        to_column(step).start()
+        return carry
+
+    def relay_column(step, carry):
+        to_column(step).wait_recv()
+        to_partner(step).start()
+        return carry
+
+    def wait_column(step, carry):
+        to_column(step).wait_send()
+        to_partner(step).wait()
+        return carry
+
+    def pieces(index):
+        found = [(late_up.at[:, columns(index, width)], late_split.at[me])]
+        for group in range(3):
+            wide = pl.ds(pl.multiple_of(group * inner * n + index * inner, inner), inner)
+            found.append((project.at[:, wide], mixer_split.at[me, :, pl.ds(group * inner, inner)]))
+        for group in range(2):
+            wide = pl.ds(pl.multiple_of(group * inner * n + index * inner, inner), inner)
+            found.append((filter_up.at[:, wide], filter_split.at[me, :, pl.ds(group * inner, inner)]))
+        found.append((segs, segs_all.at[me]))
+        return found
+
+    lax.fori_loop(1, n * m, start_small, 0)
+    own_small = pltpu.make_async_copy(small, small_all.at[here], local.at[0])
+    own_small.start()
+    own_up = pltpu.make_async_copy(early_up.at[:, columns(me, width)], early_full.at[here], local.at[1])
+    own_up.start()
+    lax.fori_loop(1, n * half, start_column, 0)
     copies = []
     for peer, (target, unused) in enumerate(others):
-        for at, (place, wide, narrow) in enumerate(column_pieces((target, 0, n), sizes)):
-            copies.append(
-                (at, remote(wides[place].at[:, wide], narrows[place].at[me, :, narrow], send.at[peer, at], recv.at[peer, at], {"dp": target}))
-            )
-        copies.append((-1, remote(segs, segs_all.at[me], send.at[peer, at + 1], recv.at[peer, at + 1], {"dp": target})))
-    owns = [pltpu.make_async_copy(small, small_all.at[here], local.at[0]), pltpu.make_async_copy(segs, segs_all.at[me], local.at[1])]
-    for at, (place, wide, narrow) in enumerate(column_pieces((me, 0, n), sizes)):
-        owns.append(pltpu.make_async_copy(wides[place].at[:, wide], narrows[place].at[me, :, narrow], local.at[2 + at]))
-    for order, copy in copies:
-        if order <= 0:
-            copy.start()
-    lax.fori_loop(1, n * m, start_small, 0)
-    for order, copy in copies:
-        if order > 0:
-            copy.start()
-    for copy in owns:
+        for at, (src, dst) in enumerate(pieces(target)):
+            copies.append(remote(src, dst, send.at[peer, at], recv.at[peer, at], {"dp": target}))
+    owns = []
+    for src, dst in pieces(me):
+        owns.append((src, dst))
+    for group in range(n):
+        wide = pl.ds(group * inner, inner)
+        owns.append((output.at[:, wide], mixer_split.at[group, :, pl.ds(3 * inner, inner)]))
+        owns.append((filter_down.at[:, wide], filter_split.at[group, :, pl.ds(2 * inner, inner)]))
+    owns = [pltpu.make_async_copy(src, dst, local.at[2 + at]) for at, (src, dst) in enumerate(owns)]
+    owns.append(pltpu.make_async_copy(depth, depth_all.at[lane], local.at[2 + len(owns)]))
+    for copy in copies + owns:
         copy.start()
-    for copy in owns:
+    lax.fori_loop(1, m, start_depth, 0)
+    own_up.wait()
+    to_partner(0).start()
+    own_small.wait()
+    lax.fori_loop(1, n * m, wait_small, 0)
+    for index in range(2):
+        for tile, line in enumerate(row_of(small_all, index)):
+            gains[pl.ds(index, 1), pl.ds(tile * LANES, LANES)] = line
+    gain, shift = gains[0:1, :], gains[1:2, :]
+
+    def work(block, carry):
+        span = pl.ds(pl.multiple_of(block * BLOCK, BLOCK), BLOCK)
+        unit, inverse = unit_of(frames[span, :].astype(jnp.float32))
+        held[span, :] = (unit * gain + shift).astype(jnp.bfloat16)
+        return carry
+
+    lax.fori_loop(0, frames.shape[0] // BLOCK, work, 0)
+    keep = pltpu.make_async_copy(held, spread.at[me], local.at[len(owns) + 2])
+    keep.start()
+    outgoing = []
+    for peer, (target, unused) in enumerate(others):
+        outgoing.append(remote(held, spread.at[me], out_send.at[peer], out_recv.at[peer], {"dp": target}))
+    for copy in outgoing:
+        copy.start()
+    lax.fori_loop(1, n * half, relay_column, 0)
+    for copy in owns + copies + outgoing:
         copy.wait()
-    for order, copy in copies:
-        copy.wait()
-    lax.fori_loop(1, n * m, wait_small, 0)
-
-
-def exchange(n, m, wides, sizes, small, segs):
-    rows = small.shape[0]
-    total = sum(groups for groups, width in sizes)
-    outs = [jax.ShapeDtypeStruct((n, rows, groups * width), jnp.bfloat16) for groups, width in sizes]
-    outs.append(jax.ShapeDtypeStruct((n * m,) + small.shape, small.dtype))
-    outs.append(jax.ShapeDtypeStruct((n,) + segs.shape, segs.dtype))
+    keep.wait()
+    to_partner(0).wait()
+    lax.fori_loop(1, n * half, wait_column, 0)
+    lax.fori_loop(1, m, wait_depth, 0)
+
+
+def exchange(n, m, early_up, late_up, project, filter_up, output, filter_down, depth, segs, frames, singles, lifts, table):
+    rows, width = early_up.shape[0], early_up.shape[1] // n
+    inner = output.shape[1] // n
+    frame_count, deep = frames.shape
+    low = jnp.bfloat16
+    packed = (16, LANES)
+    outs = [
+        jax.ShapeDtypeStruct((n * m, rows, width), low),
+        jax.ShapeDtypeStruct((n, rows, width), low),
+        jax.ShapeDtypeStruct((n, rows, 4 * inner), low),
+        jax.ShapeDtypeStruct((n, rows, 3 * inner), low),
+        jax.ShapeDtypeStruct((n * m,) + packed, jnp.float32),
+        jax.ShapeDtypeStruct((m,) + depth.shape, low),
+        jax.ShapeDtypeStruct((n,) + segs.shape, segs.dtype),
+        jax.ShapeDtypeStruct((n, frame_count, deep), low),
+    ]
     anywhere = pl.BlockSpec(memory_space=pl.ANY)
+    inside = pl.BlockSpec(memory_space=pltpu.VMEM)
+    dma = pltpu.SemaphoreType.DMA
     return pl.pallas_call(
-        functools.partial(exchange_kernel, n, m, sizes),
+        functools.partial(exchange_kernel, n, m, width, inner),
         out_shape=outs,
-        in_specs=[anywhere] * (len(wides) + 2),
-        out_specs=[anywhere] * len(outs),
+        in_specs=[anywhere] * 8 + [inside] * (2 + len(singles) + len(lifts)),
+        out_specs=[anywhere] * 4 + [inside] + [anywhere] * 3,
         scratch_shapes=[
-            pltpu.SemaphoreType.DMA((total + 2,)),
-            pltpu.SemaphoreType.DMA((n - 1, total + 1)),
-            pltpu.SemaphoreType.DMA((n - 1, total + 1)),
-            pltpu.SemaphoreType.DMA((n * m,)),
-            pltpu.SemaphoreType.DMA((n * m,)),
+            pltpu.VMEM(packed, jnp.float32),
+            pltpu.VMEM((2, deep), jnp.float32),
+            pltpu.VMEM((frame_count, deep), low),
+            dma((2 * n + 8 + 3,)),
+            dma((n - 1, 7)),
+            dma((n - 1, 7)),
+            dma((n * m,)),
+            dma((n * m,)),
+            dma((n * m // 2,)),
+            dma((n * m // 2,)),
+            dma((n * m // 2,)),
+            dma((n * m // 2,)),
+            dma((n - 1,)),
+            dma((n - 1,)),
+            dma((m,)),
+            dma((m,)),
         ],
         compiler_params=pltpu.CompilerParams(collective_id=0, has_side_effects=True),
         name="exchange",
-    )(*wides, small, segs)
+    )(early_up, late_up, project, filter_up, output, filter_down, depth, segs, frames, *singles, *lifts, table)
 
 
 def giveback_kernel(n, sizes, *refs):
@@ -731,11 +867,11 @@
     greet([target for target, unused in others])
     copies = []
     for peer, (target, unused) in enumerate(others):
-        for at, (place, wide, narrow) in enumerate(column_pieces((me, 0, n), sizes)):
+        for at, (place, wide, narrow) in enumerate(column_pieces(me, n, sizes)):
             copies.append(
                 remote(narrows[place].at[target, :, narrow], wides[place].at[:, wide], send.at[peer, at], recv.at[peer, at], {"dp": target})
             )
-    for at, (place, wide, narrow) in enumerate(column_pieces((me, 0, n), sizes)):
+    for at, (place, wide, narrow) in enumerate(column_pieces(me, n, sizes)):
         copies.append(pltpu.make_async_copy(narrows[place].at[me, :, narrow], wides[place].at[:, wide], local.at[at]))
     for copy in copies:
         copy.start()
@@ -867,11 +1003,6 @@
     return inverse * (adjusted - unit * jnp.mean(scaled * unit, axis=-1, keepdims=True))
 
 
-def step_first(total, states, vectors):
-    unit, inverse = unit_of(states[0])
-    return [], unit * vectors[0] + vectors[1], []
-
-
 def step_forward(scale, total, states, vectors):
     values = states[0] + scale * (total + vectors[0])
     unit, inverse = unit_of(values)
@@ -899,10 +1030,6 @@
     unit, inverse = unit_of(states[1])
     grad = states[0] + unit_back(total, unit, inverse, vectors[0])
     return [grad], None, [total * unit, total]
-
-
-PIECES = 4
-BLOCK = 16
 
 
 def boundary_kernel(n, step, shape, *refs):
@@ -1162,10 +1289,6 @@
     )(packed, upstream, segment_rows, segment_columns, table)
 
 
-MARGIN = 16
-LANES = 128
-
-
 def reach_mask(offset, behind, ahead):
     if offset < 0:
         return behind >= -offset
@@ -1295,6 +1418,13 @@
 def scatter_split(value, n):
     value = value.astype(jnp.bfloat16).reshape(n, value.shape[0] // n, value.shape[1])
     return lax.psum_scatter(value, "fsdp", scatter_dimension=1, tiled=True)
+
+
+def pair_slopes(up_slope, down_slope, n):
+    inner = down_slope.shape[0]
+    up_slope = up_slope.reshape(n, inner, -1)
+    down_slope = jnp.transpose(down_slope.reshape(inner, n, inner), (1, 0, 2))
+    return jnp.concatenate([up_slope, down_slope], axis=2)
 
 
 def flat(value):
@@ -1353,49 +1483,28 @@
         filter_gain, filter_shift, depth_bias, middle_gain, middle_shift, filter_drop, late_gain, late_shift,
         late_drop, final_gain, final_shift,
     ]
-    at_lift = len(singles) + KW
     spans = hidden * n // D
-    small = jnp.concatenate(
-        [
-            jnp.transpose(jnp.stack(singles)),
-            depth_weight,
-            early_lift.reshape(rows, spans),
-            late_lift.reshape(rows, spans),
-            filter_lift.reshape(rows, 2),
-            distance_table.reshape(rows, -1),
-        ],
-        axis=1,
-    )
-    small = jnp.pad(small, ((0, 0), (0, LANES - small.shape[1])))
-    sizes = [(1, hidden), (1, hidden), (3, inner), (2, inner)]
-    early_up_split, late_up_split, project_split, filter_up_split, small_all, segments_all = exchange(
-        n, m, [early_up, late_up, mixer_project, filter_up], sizes, small, segments.reshape(1, frame_count)
-    )
     w_early_down = gather_rows(early_down)
-    w_early_up = gather_split(early_up_split)
-    w_project = gather_split(project_split)
-    w_output = gather_rows(mixer_output)
-    w_filter_up = gather_split(filter_up_split)
-    w_filter_down = gather_rows(filter_down)
+    w_early_up, late_up_split, mixer_split, filter_split, small_all, depth_all, segments_all, early_hidden = exchange(
+        n, m, early_up, late_up, mixer_project, filter_up, mixer_output, filter_down, depth_weight,
+        segments.reshape(1, frame_count), frames, singles, [early_lift, late_lift, filter_lift], distance_table,
+    )
+    w_early_up = w_early_up.reshape(D, hidden)
+    w_mixer = lax.all_gather(mixer_split, "fsdp", axis=1, tiled=True)
+    w_filter = lax.all_gather(filter_split, "fsdp", axis=1, tiled=True)
     w_late_up = gather_split(late_up_split)
     w_late_down = gather_rows(late_down)
 
-    listed = small_all.reshape(D, LANES)
-    vectors = jnp.transpose(listed).astype(jnp.float32)
-    own_vectors = lax.dynamic_slice(vectors, (0, me * inner), (LANES, inner))
-
-    def whole(low, count):
-        return listed[:, low : low + count].astype(jnp.float32).reshape(-1)
-
-    early_lifts = lax.dynamic_slice(whole(at_lift, spans), (me * hidden,), (hidden,))
-    late_lifts = lax.dynamic_slice(whole(at_lift + spans, spans), (me * hidden,), (hidden,))
-    filter_lifts = lax.dynamic_slice(
-        whole(at_lift + 2 * spans, 2).reshape(2, D), (0, me * inner), (2, inner)
-    ).reshape(2 * inner)
-    at_table = at_lift + 2 * spans + 2
-    table = whole(at_table, NREL * HEADS // D).reshape(NREL, HEADS)
+    lines = -(-len(singles) * rows // LANES)
+    vectors = jnp.transpose(small_all[:, :lines].reshape(n * m, lines, LANES // rows, rows), (1, 2, 0, 3)).reshape(-1, D)
+    own_vectors = lax.dynamic_slice(vectors, (0, me * inner), (vectors.shape[0], inner))
+    own_lifts = lax.dynamic_slice(small_all, (me * m, lines, 0), (m, 2, LANES))
+    early_lifts, late_lifts = own_lifts[:, 0].reshape(-1), own_lifts[:, 1].reshape(-1)
+    filter_lifts = small_all[:, lines + 2, : 2 * D // (n * m)].reshape(2, D)
+    filter_lifts = lax.dynamic_slice(filter_lifts, (0, me * inner), (2, inner)).reshape(2 * inner)
+    table = small_all[:, 8 : 8 + distance_table.shape[0], :HEADS].reshape(NREL, HEADS)
     table = jnp.transpose(lax.dynamic_slice(table, (0, me * heads), (NREL, heads)))[:, ::-1]
-    taps = own_vectors[len(singles) : len(singles) + KW]
+    taps = jnp.transpose(depth_all.reshape(inner, KW)).astype(jnp.float32)
     attention_shift = jnp.concatenate([own_vectors[5], jnp.zeros((inner,), jnp.float32), own_vectors[6]])
     segment_rows = segments_all
     segment_columns = segments_all.reshape(n, frame_count, 1)
@@ -1415,24 +1524,30 @@
 
     def feed_back(low, hidden_rows, widened, active, w_up, w_down):
         low = flat(low)
-        down_slope = scatter_rows(lead_dot(active, low))
+        down_slope = lead_dot(active, low).astype(jnp.bfloat16)
         widened_grad = swish_back(back_dot(low, w_down), widened)
         widened_low = widened_grad.astype(jnp.bfloat16)
-        up_slope = scatter_split(lead_dot(flat(hidden_rows), widened_low), n)
+        up_slope = lead_dot(flat(hidden_rows), widened_low).astype(jnp.bfloat16)
         part = blocks(back_dot(widened_low, w_up).astype(jnp.bfloat16))
+        part, down_slope, up_slope = lax.optimization_barrier((part, down_slope, up_slope))
         return part, down_slope, up_slope, jnp.sum(widened_grad, axis=0)
 
-    (early_hidden,) = boundary(n, step_first, None, [start_rows], [vectors[0], vectors[1]], 0, 0, 1)
     early_wide, early_active, part = feed(early_hidden, w_early_up, early_lifts, w_early_down)
     first_rows, mixer_hidden = boundary(
         n, functools.partial(step_forward, 0.5), part, [start_rows], [vectors[2], vectors[3], vectors[4]], 1, 0, 2
     )
+    mixer_hidden, w_mixer = lax.optimization_barrier((mixer_hidden, w_mixer))
+    w_project = w_mixer[:, :, : 3 * inner].reshape(D, 3 * inner)
+    w_output = jnp.transpose(w_mixer[:, :, 3 * inner :], (1, 0, 2)).reshape(inner, D)
     packed = blocks((flat_dot(flat(mixer_hidden), w_project) + attention_shift).astype(jnp.bfloat16))
     blended = attend(packed, segment_rows, segment_columns, table)
     part = blocks(flat_dot(flat(blended), w_output).astype(jnp.bfloat16))
     second_rows, filter_hidden = boundary(
         n, functools.partial(step_forward, 1.0), part, [first_rows], [vectors[7], vectors[8], vectors[9]], 1, 0, 3
     )
+    filter_hidden, w_filter = lax.optimization_barrier((filter_hidden, w_filter))
+    w_filter_up = w_filter[:, :, : 2 * inner].reshape(D, 2 * inner)
+    w_filter_down = jnp.transpose(w_filter[:, :, 2 * inner :], (1, 0, 2)).reshape(inner, D)
     opened = blocks(flat_dot(flat(filter_hidden), w_filter_up) + filter_lifts)
     gated, filtered = convolve(opened, behind, ahead, taps, own_vectors[10:11])
     filtered = flat(filtered)
@@ -1452,6 +1567,7 @@
     third_rows, late_hidden = boundary(
         n, functools.partial(step_forward, 1.0), part, [second_rows], [vectors[13], vectors[14], vectors[15]], 1, 0, 5
     )
+    late_hidden, w_late_up, w_late_down = lax.optimization_barrier((late_hidden, w_late_up, w_late_down))
     late_wide, late_active, part = feed(late_hidden, w_late_up, late_lifts, w_late_down)
     layer_out, grad, low, turn_sums = boundary(
         n, step_turn, part, [third_rows, final_upstream], [vectors[16], vectors[17], vectors[18]], 2, 3, 6
@@ -1460,11 +1576,13 @@
     part, late_down_slope, late_up_slope, late_lift_slope = feed_back(
         low, late_hidden, late_wide, late_active, w_late_up, w_late_down
     )
+    late_down_slope = scatter_rows(late_down_slope)
+    late_up_slope = scatter_split(late_up_slope, n)
     grad, low, late_sums = boundary(
         n, functools.partial(step_backward, 1.0), part, [grad, third_rows], [vectors[14]], 1, 3, 7
     )
     low = flat(low)
-    filter_down_slope = scatter_rows(lead_dot(swished, low))
+    filter_down_slope = lead_dot(swished, low).astype(jnp.bfloat16)
     middle_grad = swish_back(back_dot(low, w_filter_down), middle)
     middle_gain_slope = jnp.sum(middle_grad * middle_unit, axis=0)
     middle_shift_slope = jnp.sum(middle_grad, axis=0)
@@ -1487,24 +1605,37 @@
         opened, gated, blocks(filtered_grad), behind, ahead, taps
     )
     opened_low = flat(opened_low)
-    filter_up_slope = scatter_split(lead_dot(flat(filter_hidden), opened_low), n)
+    filter_up_slope = lead_dot(flat(filter_hidden), opened_low).astype(jnp.bfloat16)
     part = blocks(back_dot(opened_low, w_filter_up).astype(jnp.bfloat16))
+    part, filter_slope = lax.optimization_barrier((part, pair_slopes(filter_up_slope, filter_down_slope, n)))
+    filter_slope = lax.psum_scatter(filter_slope, "fsdp", scatter_dimension=1, tiled=True)
     grad, low, filter_sums = boundary(
         n, functools.partial(step_backward, 1.0), part, [grad, second_rows], [vectors[8]], 1, 3, 9
     )
     low = flat(low)
-    output_slope = scatter_rows(lead_dot(flat(blended), low))
+    output_slope = lead_dot(flat(blended), low).astype(jnp.bfloat16)
     blend_grad = blocks(back_dot(low, w_output).astype(jnp.bfloat16))
     packed_low, shift_sums, table_slope = unattend(packed, blend_grad, segment_rows, segment_columns, table)
     packed_low = flat(packed_low)
-    project_slope = scatter_split(lead_dot(flat(mixer_hidden), packed_low), n)
+    project_slope = lead_dot(flat(mixer_hidden), packed_low).astype(jnp.bfloat16)
     part = blocks(back_dot(packed_low, w_project).astype(jnp.bfloat16))
+    part, mixer_slope, late_down_slope, late_up_slope = lax.optimization_barrier(
+        (part, pair_slopes(project_slope, output_slope, n), late_down_slope, late_up_slope)
+    )
+    mixer_slope = lax.psum_scatter(mixer_slope, "fsdp", scatter_dimension=1, tiled=True)
     grad, low, mixer_sums = boundary(
         n, functools.partial(step_backward, 0.5), part, [grad, first_rows], [vectors[3]], 1, 3, 10
     )
     part, early_down_slope, early_up_slope, early_lift_slope = feed_back(
         low, early_hidden, early_wide, early_active, w_early_up, w_early_down
     )
+    early_down_slope = jnp.transpose(early_down_slope.reshape(m, spans, rows, D), (1, 0, 2, 3))
+    early_slope = jnp.concatenate(
+        [early_up_slope.reshape(n, D // n, hidden), early_down_slope.reshape(spans, m * rows, D)]
+    )
+    part, early_slope, filter_slope = lax.optimization_barrier((part, early_slope, filter_slope))
+    early_slope = lax.psum_scatter(early_slope, "fsdp", scatter_dimension=1, tiled=True)
+    early_up_slope, early_down_slope = early_slope[:n], early_slope[n:].reshape(spans * rows, D)
     slope_frames, early_sums = boundary(
         n, step_last, part, [grad, start_rows], [vectors[0]], 1, 2, 11, gathered=False
     )
@@ -1539,6 +1670,7 @@
     group_used = group.shape[1]
     group = jnp.pad(group, ((0, 0), (0, -group_used % LANES))).reshape(m, -1, LANES)
     wide_all, group_all = collect(n, m, wide, group, 12)
+    wide_all, mixer_slope = lax.optimization_barrier((wide_all, mixer_slope))
     tables = wide_all.reshape(n, m, -1)[:, :, wide_count * rows : table_used]
     wide = jnp.sum(wide_all, axis=0).reshape(-1)
     lift_total = wide[table_used:wide_used]
@@ -1546,9 +1678,12 @@
     tables = jnp.transpose(jnp.sum(tables, axis=1).reshape(HEADS, table_rows))
     group = jnp.sum(group_all, axis=0).reshape(-1)[:group_used].reshape(group_count, rows)
     late_up_wide, project_wide, filter_up_wide = giveback(
-        n, [late_up_slope, project_slope, filter_up_slope], sizes[1:], 13
-    )
-    (early_up_wide,) = giveback(n, [early_up_slope], sizes[:1], 14)
+        n, [late_up_slope, mixer_slope, filter_slope], [(1, hidden), (3, inner), (2, inner)], 13
+    )
+    (early_up_wide,) = giveback(n, [early_up_slope], [(1, hidden)], 14)
+
+    def rejoin(value, low):
+        return final(jnp.transpose(value[:, :, low:], (1, 0, 2)).reshape(rows, D))
 
     def final(value):
         return value.astype(jnp.float32)
@@ -1568,7 +1703,7 @@
         final(project_wide),
         group[0],
         group[1],
-        final(output_slope),
+        rejoin(mixer_slope, 3 * inner),
         wide[8],
         tables,
         wide[6],
@@ -1579,7 +1714,7 @@
         group[4 + KW],
         group[2],
         group[3],
-        final(filter_down_slope),
+        rejoin(filter_slope, 2 * inner),
         wide[5],
         wide[3],
         wide[4],

time: 627 us -> 482 us (0.77)
  waiting for transfers between devices: 127 us -> 12.5 us
  blocking collectives: 33 us -> 0 us
  Pallas kernels: 296 us -> 328 us
  matrix products: 77.8 us -> 58.9 us
  local copies, waits for them, and re-layouts: 42.5 us -> 35 us
    reduce_scatter x4 -> x1, waiting for transfers between devices: 65.2 us -> 0.01 us  [scatter_split(): return lax.psum_scatter(value, 'fsdp', scatter_dimension=1, tiled=True)]
    reduce_scatter x4 -> x1, waiting for transfers between devices: 58.4 us -> 0.01 us  [scatter_rows(): lax.psum_scatter(value.astype(jnp.bfloat16), 'fsdp', scatter_dimension=0,...]
    pallas_call x1, Pallas kernels: 22.3 us -> 58.8 us  [exchange(): pl.pallas_call(functools.partial(exchange_kernel, n, m, width, inner), ou...]
    all_gather x2 -> x0, blocking collectives: 33 us -> none  [gather_rows(): return lax.all_gather(value, 'fsdp', axis=0, tiled=True)]
    another operation x23 -> x1, local copies, waits for them, and re-layouts: 15.5 us -> 0.08 us  [split_body(): filter_lifts = small_all[:, lines + 2, :2 * D // (n * m)].reshape(2, D)]
    dot_general x8, matrix products: 25.6 us -> 11.8 us  [lead_dot(): lax.dot_general(left_rows, right_rows, (((0,), (0,)), ((), ())), preferre...]
    reduce_scatter x0 -> x3, waiting for transfers between devices: none -> 9.23 us  [the longest x1 9.21 us: split_body(): lax.psum_scatter(early_slope, 'fsdp', scatter_dimension=1, tiled=True)]
    pallas_call x9 -> x8, Pallas kernels: 202 us -> 193 us  [boundary(): pl.pallas_call(functools.partial(boundary_kernel, n, step, shape), out_sh...]
  transfers between devices with their start and end apart: 14 -> 10, of which waited for: 4 -> 1; matrix products, arithmetic and copies ran while one was open for 17% -> 19% of each run, Pallas kernels for 35% -> 62%
where the time goes in v2:
time: 482 us; the launch traced here: 477 us
  Pallas kernels  328 us (68%)
  matrix products  58.9 us (12%)
  local copies, waits for them, and re-layouts  35 us (7%)
  other arithmetic  27.3 us (6%)
  between operations  15.3 us (3%)
  waiting for transfers between devices  12.5 us (3%)
    pallas_call x8, Pallas kernels, boundary(): pl.pallas_call(functools.partial(boundary_kernel, n, step, shape), out_sh...  193 us
    pallas_call x1, Pallas kernels, exchange(): pl.pallas_call(functools.partial(exchange_kernel, n, m, width, inner), ou...  58.8 us
    dot_general x8, matrix products, back_dot(): lax.dot_general(left_rows, right_rows, (((1,), (1,)), ((), ())), preferre...  24.1 us
    dot_general x8, matrix products, flat_dot(): return jnp.dot(left_rows, right_rows, preferred_element_type=jnp.float32)  23.1 us
    pallas_call x2, Pallas kernels, giveback(): pl.pallas_call(functools.partial(giveback_kernel, n, sizes), out_shape=ou...  17.3 us
    pallas_call x1, Pallas kernels, collect(): pl.pallas_call(functools.partial(collect_kernel, n, m), out_shape=[jax.Sh...  12.5 us
    pallas_call x1, Pallas kernels, unattend(): pl.pallas_call(functools.partial(unattend_kernel, heads), grid=(blocks,),...  12 us
    pallas_call x2, Pallas kernels, share(): pl.pallas_call(functools.partial(share_kernel, n), out_shape=jax.ShapeDty...  11.8 us
  transfers between devices with their start and end apart: 10, of which 1 were waited for; matrix products, arithmetic and copies ran while one was open for 19% of the time, Pallas kernels for 62%

profile of v2, /device:TPU:0, one launch (start us, length us, event | category | flops | bytes accessed | tf_op | source)
XLA Modules:
  0.0 477.0 jit_solution(1320890665283300304)
XLA Ops:
  8.0 58.8 %exchange.1 = (bf16[32,32,1024]{2,1,0:T(8,128)(2,1)}, bf16[4,32,1024]{2,1,0:T(8,128)(2,1)}, bf16[4,32,1024]{2,1,0:T(8,128)(2,1)}, bf16[4,32,768]{2,1,0:T(8,128)(...) custom-call(bf16[32,4096]{1,0:T(8,128)(2,1)} %refs_0_.1, ...), custom_call_target="tpu_custom_call" | custom-call | tf_op jit(solution)/shard_map/exchange/pallas_call | solution.py:833
  73.5 4.3 fusion.16
  84.5 4.6 convolution_convert_fusion.10
  89.0 29.0 %boundary.8 = (f32[128,1024]{1,0:T(8,128)}, bf16[4,128,1024]{2,1,0:T(8,128)(2,1)}) custom-call(bf16[4,128,1024]{2,1,0:T(8,128)(2,1)} %bitcast.217, f32[128,1024]{1,0:T(8,128)} %convert_element_type.135.refs_1_.refs_2_, f32[3,1024]{1,0:T(4,128)} %get-tuple-element.289.refs_2_), custom_call_target="tpu_custom_call" | custom-call | tf_op jit(solution)/shard_map/boundary/pallas_call | solution.py:1149
  121.3 3.1 add_convert_fusion
  124.4 8.1 %attend.1 = bf16[4,128,256]{2,1,0:T(8,128)(2,1)} custom-call(bf16[4,128,768]{2,1,0:T(8,128)(2,1)} %bitcast.194, s32[4,1,128]{2,1,0:T(1,128)} %get-tuple-element.107.segment_rows, s32[4,128,1]{2,1,0:T(8,128)} %copy.121.segment_columns, f32[4,256]{1,0:T(4,128)} %rev.4.table), custom_call_target="tpu_custom_call" | custom-call | tf_op jit(solution)/shard_map/attend/pallas_call | solution.py:1196
  132.5 2.4 convolution_convert_fusion.9
  134.9 28.4 %boundary.9 = (f32[128,1024]{1,0:T(8,128)}, bf16[4,128,1024]{2,1,0:T(8,128)(2,1)}) custom-call(bf16[4,128,1024]{2,1,0:T(8,128)(2,1)} %bitcast.190, f32[128,1024]{1,0:T(8,128)} %get-tuple-element.108.refs_1_.refs_2_, f32[3,1024]{1,0:T(4,128)} %get-tuple-element.288.refs_2_), custom_call_target="tpu_custom_call" | custom-call | tf_op jit(solution)/shard_map/boundary/pallas_call | solution.py:1149
  167.5 5.0 %convolve.1 = (f32[4,128,256]{2,1,0:T(8,128)}, f32[4,128,256]{2,1,0:T(8,128)}) custom-call(f32[4,128,512]{2,1,0:T(8,128)} %bitcast.192, s32[4,128,1]{2,1,0:T(8,128)} %get-tuple-element.324.behind, s32[4,128,1]{2,1,0:T(8,128)} %get-tuple-element.323.ahead, f32[31,256]{1,0:T(8,128)} %bitcast.229, f32[1,256]{1,0:T(1,128)} %get-tuple-element.291.bias), custom_call_target="tpu_custom_call" | custom-call | tf_op jit(solution)/shard_map/convolve/pallas_call | solution.py:1324
  175.6 5.9 %share.2 = f32[4,8,128]{2,1,0:T(8,128)} custom-call(f32[8,128]{1,0:T(8,128)} %pad_maximum_fusion.4.mine), custom_call_target="tpu_custom_call" | custom-call | tf_op jit(solution)/shard_map/share/pallas_call | solution.py:917
  184.6 26.8 %boundary.10 = (f32[128,1024]{1,0:T(8,128)}, bf16[4,128,1024]{2,1,0:T(8,128)(2,1)}) custom-call(bf16[4,128,1024]{2,1,0:T(8,128)(2,1)} %bitcast.191, f32[128,1024]{1,0:T(8,128)} %get-tuple-element.115.refs_1_.refs_2_, f32[3,1024]{1,0:T(4,128)} %get-tuple-element.287.refs_2_), custom_call_target="tpu_custom_call" | custom-call | tf_op jit(solution)/shard_map/boundary/pallas_call | solution.py:1149
  211.5 3.3 fusion.17
  214.8 2.3 convolution_convert_fusion.7
  217.1 26.0 %boundary.11 = (f32[128,1024]{1,0:T(8,128)}, f32[128,1024]{1,0:T(8,128)}, bf16[4,128,1024]{2,1,0:T(8,128)(2,1)}, f32[3,1024]{1,0:T(4,128)}) custom-call(bf16[4,128,1024]{2,1,0:T(8,128)(2,1)} %bitcast.224, f32[128,1024]{1,0:T(8,128)} %get-tuple-element.121.refs_1_.refs_2_, f32[128,1024]{1,0:T(8,128)} %convert_element_type.148.refs_2_, ...), custom_call_target="tpu_custom_call" | custom-call | tf_op jit(solution)/shard_map/boundary/pallas_call | solution.py:1149
  243.1 5.4 %fusion.15 = (f32[1024]{0:T(1024)S(1)}, bf16[512,1024]{1,0:T(8,128)(2,1)}) fusion(f32[512,1024]{1,0:T(8,128)} %copy-done.39, f32[1024]{0:T(1024)S(1)} %bitcast.257, bf16[512,1024]{1,0:T(8,128)(2,1)} %bitcast.277, bf16[1024,1024]{1,0:T(8,128)(2,1)} %all-gather.14.cloned.1.call-done), kind=kOutput, calls=%fused_computation.95 | convolution fusion | flops 1079507968 | bytes 6299648 | tf_op jit(solution)/shard_map/dot_general | solution.py:38
  248.6 2.7 convolution_convert_fusion.3
  251.3 4.3 convolution_convert_fusion.6
  255.7 2.7 convolution_convert_fusion.2
  259.8 24.7 %boundary.12 = (f32[128,1024]{1,0:T(8,128)}, bf16[4,128,1024]{2,1,0:T(8,128)(2,1)}, f32[3,1024]{1,0:T(4,128)}) custom-call(bf16[4,128,1024]{2,1,0:T(8,128)(2,1)} %bitcast.221, f32[128,1024]{1,0:T(8,128)} %get-tuple-element.126.refs_1_, f32[128,1024]{1,0:T(8,128)} %get-tuple-element.121.refs_1_.refs_2_, f32[1,1024]{1,0:T(1,128)} %get-tuple-element.285.refs_3_), custom_call_target="tpu_custom_call" | custom-call | tf_op jit(solution)/shard_map/boundary/pallas_call | solution.py:1149
  287.3 5.9 %share.3 = f32[4,8,128]{2,1,0:T(8,128)} custom-call(f32[8,128]{1,0:T(8,128)} %pad_maximum_fusion.5.mine), custom_call_target="tpu_custom_call" | custom-call | tf_op jit(solution)/shard_map/share/pallas_call | solution.py:917
  296.0 8.9 %unconvolve.1 = (bf16[4,128,512]{2,1,0:T(8,128)(2,1)}, f32[1,512]{1,0:T(1,128)}, f32[32,256]{1,0:T(8,128)}) custom-call(f32[4,128,512]{2,1,0:T(8,128)} %bitcast.193, f32[4,128,256]{2,1,0:T(8,128)} %get-tuple-element.123.gated, f32[4,128,256]{2,1,0:T(8,128)} %bitcast.208, s32[4,128,1]{2,1,0:T(8,128)} %get-tuple-element.324.behind, ...), custom_call_target="tpu_custom_call" | custom-call | tf_op jit(solution)/shard_map/unconvolve/pallas_call | solution.py:1386
  310.5 23.0 %boundary.13 = (f32[128,1024]{1,0:T(8,128)}, bf16[4,128,1024]{2,1,0:T(8,128)(2,1)}, f32[3,1024]{1,0:T(4,128)}) custom-call(bf16[4,128,1024]{2,1,0:T(8,128)(2,1)} %bitcast.223, f32[128,1024]{1,0:T(8,128)} %get-tuple-element.130.refs_1_, f32[128,1024]{1,0:T(8,128)} %get-tuple-element.115.refs_1_.refs_2_, f32[1,1024]{1,0:T(1,128)} %get-tuple-element.284.refs_3_), custom_call_target="tpu_custom_call" | custom-call | tf_op jit(solution)/shard_map/boundary/pallas_call | solution.py:1149
  333.5 2.5 convolution_convert_fusion.12
  335.9 12.0 %unattend.1 = (bf16[4,128,768]{2,1,0:T(8,128)(2,1)}, f32[2,256]{1,0:T(2,128)}, f32[4,256]{1,0:T(4,128)}) custom-call(bf16[4,128,768]{2,1,0:T(8,128)(2,1)} %bitcast.195, bf16[4,128,256]{2,1,0:T(8,128)(2,1)} %bitcast.231, s32[4,1,128]{2,1,0:T(1,128)} %get-tuple-element.107.segment_rows, s32[4,128,1]{2,1,0:T(8,128)} %copy.121.segment_columns, f32[4,256]{1,0:T(4,128)} %rev.4.table), custom_call_target="tpu_custom_call" | custom-call | tf_op jit(solution)/shard_map/unattend/pallas_call | solution.py:1264
  355.1 22.3 %boundary.14 = (f32[128,1024]{1,0:T(8,128)}, bf16[4,128,1024]{2,1,0:T(8,128)(2,1)}, f32[3,1024]{1,0:T(4,128)}) custom-call(bf16[4,128,1024]{2,1,0:T(8,128)(2,1)} %bitcast.222, f32[128,1024]{1,0:T(8,128)} %get-tuple-element.136.refs_1_, f32[128,1024]{1,0:T(8,128)} %get-tuple-element.108.refs_1_.refs_2_, f32[1,1024]{1,0:T(1,128)} %get-tuple-element.283.refs_3_), custom_call_target="tpu_custom_call" | custom-call | tf_op jit(solution)/shard_map/boundary/pallas_call | solution.py:1149
  377.4 3.7 fusion.14
  386.6 2.3 pad_maximum_fusion
  391.8 13.1 %boundary.15 = (f32[128,1024]{1,0:T(8,128)}, f32[2,1024]{1,0:T(2,128)}) custom-call(bf16[4,128,1024]{2,1,0:T(8,128)(2,1)} %bitcast.220, f32[128,1024]{1,0:T(8,128)} %get-tuple-element.143.refs_1_, f32[128,1024]{1,0:T(8,128)} %convert_element_type.135.refs_1_.refs_2_, f32[1,1024]{1,0:T(1,128)} %get-tuple-element.282.refs_3_), custom_call_target="tpu_custom_call" | custom-call | tf_op jit(solution)/shard_map/boundary/pallas_call | solution.py:1149
  408.2 12.5 %collect.1 = (f32[32,5,128]{2,1,0:T(8,128)}, f32[8,11,128]{2,1,0:T(8,128)}) custom-call(f32[32,5,128]{2,1,0:T(8,128)} %reshape.491.wide, f32[8,11,128]{2,1,0:T(8,128)} %reshape.494.group), custom_call_target="tpu_custom_call" | custom-call | tf_op jit(solution)/shard_map/collect/pallas_call | solution.py:977
  428.7 11.0 %giveback.3 = (bf16[32,4096]{1,0:T(8,128)(2,1)}, bf16[32,3072]{1,0:T(8,128)(2,1)}, bf16[32,2048]{1,0:T(8,128)(2,1)}) custom-call(bf16[4,32,1024]{2,1,0:T(8,128)(2,1)} %reduce-scatter.8.cloned.1.call-done.refs_0_, bf16[4,32,1024]{2,1,0:T(8,128)(2,1)} %reduce-scatter.12.cloned.1.call-done.refs_1_, bf16[4,32,768]{2,1,0:T(8,128)(2,1)} %reduce-scatter.10.cloned.1.call-done.refs_2_), custom_call_target="tpu_custom_call" | custom-call | tf_op jit(solution)/shard_map/giveback/pallas_call | solution.py:887
  448.5 9.2 %reduce-scatter.14.cloned.1.call-done = bf16[8,32,1024]{2,1,0:T(8,128)(2,1)} async-done(((bf16[8,256,1024]{2,1,0:T(8,128)(2,1)}), bf16[8,32,1024]{2,1,0:T(8,128)(2,1)}) %reduce-scatter.14.cloned.1.call-update) | async-done | bytes 524304 | tf_op jit(solution)/shard_map/reduce_scatter | solution.py:1637
  459.5 6.2 %giveback.2 = bf16[32,4096]{1,0:T(8,128)(2,1)} custom-call(bf16[4,32,1024]{2,1,0:T(8,128)(2,1)} %get-tuple-element.279.refs_0_), custom_call_target="tpu_custom_call" | custom-call | tf_op jit(solution)/shard_map/giveback/pallas_call | solution.py:887
  (246 shorter events, 81.3 us)
Async XLA Ops:
  7.2 77.3 %all-gather.6.cloned.1.call-start = ((), (), s32[]{:S(2)}) async-start(), calls=%async_computation.5 | async-start | bytes 2359296 | tf_op jit(solution)/shard_map/all_gather | solution.py:1406
  8.0 110.1 %all-gather.8.cloned.1.call-start = ((), (), s32[]{:S(2)}) async-start(), calls=%async_computation.6 | async-start | bytes 2359296 | tf_op jit(solution)/shard_map/all_gather | solution.py:1493
  66.8 5.9 %copy-start.15 = (s32[4,1,128]{2,1,0:T(1,128)S(1)}, s32[4,1,128]{2,1,0:T(1,128)}, u32[]{:S(2)}) copy-start(s32[4,1,128]{2,1,0:T(1,128)} %get-tuple-element.107.segment_rows) | copy-start | bytes 6148
  66.8 6.6 %copy-start.14 = (bf16[8,32,31]{2,1,0:T(8,128)(2,1)S(1)}, bf16[8,32,31]{2,1,0:T(8,128)(2,1)}, u32[]{:S(2)}) copy-start(bf16[8,32,31]{2,1,0:T(8,128)(2,1)} %get-tuple-element.113) | copy-start | bytes 47620
  66.8 6.6 %copy-start.27 = (bf16[4,128,1024]{2,1,0:T(8,128)(2,1)S(1)}, bf16[4,128,1024]{2,1,0:T(8,128)(2,1)}, u32[]{:S(2)}) copy-start(bf16[4,128,1024]{2,1,0:T(8,128)(2,1)} %get-tuple-element.100) | copy-start | bytes 3145732
  66.9 96.5 %all-gather.10.cloned.1.call-start = ((), (), s32[]{:S(2)}) async-start(), calls=%async_computation.7 | async-start | bytes 1769472 | tf_op jit(solution)/shard_map/all_gather | solution.py:1494
  67.6 143.8 %all-gather.12.cloned.1.call-start = ((), (), s32[]{:S(2)}) async-start(), calls=%async_computation.8 | async-start | bytes 2359296 | tf_op jit(solution)/shard_map/all_gather | solution.py:1410
  68.2 143.3 %all-gather.14.cloned.1.call-start = ((), (), s32[]{:S(2)}) async-start(), calls=%async_computation.9 | async-start | bytes 2359296 | tf_op jit(solution)/shard_map/all_gather | solution.py:1406
  68.8 286.3 %reduce-scatter.6.cloned.1.call-start = ((), (), s32[]{:S(2)}) async-start(), calls=%async_computation.10 | async-start | bytes 2359296 | tf_op jit(solution)/shard_map/reduce_scatter | solution.py:1415
  73.4 6.8 %copy-start.8 = (bf16[128,1024]{1,0:T(8,128)(2,1)S(1)}, bf16[128,1024]{1,0:T(8,128)(2,1)}, u32[]{:S(2)}) copy-start(bf16[128,1024]{1,0:T(8,128)(2,1)} %refs_8_.1) | copy-start | bytes 786436
  77.7 5.9 %copy-start.11 = (bf16[128,1024]{1,0:T(8,128)(2,1)S(1)}, bf16[128,1024]{1,0:T(8,128)(2,1)}, u32[]{:S(2)}) copy-start(bf16[128,1024]{1,0:T(8,128)(2,1)} %param.37) | copy-start | bytes 786436
  119.6 4.8 %copy-start.2 = (bf16[4,256,768]{2,1,0:T(8,128)(2,1)}, bf16[4,256,768]{2,1,0:T(8,128)(2,1)S(1)}, u32[]{:S(2)}) copy-start(bf16[4,256,768]{2,1,0:T(8,128)(2,1)S(1)} %slice.227) | copy-start | bytes 4718596
  172.4 10.4 %copy-start = (f32[4,128,256]{2,1,0:T(8,128)S(1)}, f32[4,128,256]{2,1,0:T(8,128)}, u32[]{:S(2)}) copy-start(f32[4,128,256]{2,1,0:T(8,128)} %get-tuple-element.114) | copy-start | bytes 1572868
  243.1 5.5 %copy-start.34 = (bf16[4,128,1024]{2,1,0:T(8,128)(2,1)S(1)}, bf16[4,128,1024]{2,1,0:T(8,128)(2,1)}, u32[]{:S(2)}) copy-start(bf16[4,128,1024]{2,1,0:T(8,128)(2,1)} %get-tuple-element.124) | copy-start | bytes 3145732
  243.1 5.5 %copy-start.40 = (f32[512,1024]{1,0:T(8,128)S(1)}, f32[512,1024]{1,0:T(8,128)}, u32[]{:S(2)}) copy-start(f32[512,1024]{1,0:T(8,128)} %copy-done.39) | copy-start | bytes 6291460
  251.3 4.3 copy-start.41
  258.4 96.7 %reduce-scatter.8.cloned.1.call-start = ((), (), s32[]{:S(2)}) async-start(), calls=%async_computation.11 | async-start | bytes 2359296 | tf_op jit(solution)/shard_map/reduce_scatter | solution.py:1420
  259.1 129.9 %reduce-scatter.10.cloned.1.call-start = ((), (), s32[]{:S(2)}) async-start(), calls=%async_computation.12 | async-start | bytes 1769472 | tf_op jit(solution)/shard_map/reduce_scatter | solution.py:1611
  284.7 9.3 %copy-start.4 = (bf16[4,128,1024]{2,1,0:T(8,128)(2,1)S(1)}, bf16[4,128,1024]{2,1,0:T(8,128)(2,1)}, u32[]{:S(2)}) copy-start(bf16[4,128,1024]{2,1,0:T(8,128)(2,1)} %get-tuple-element.127) | copy-start | bytes 3145732
  294.9 10.1 %copy-start.31 = (bf16[4,128,1024]{2,1,0:T(8,128)(2,1)S(1)}, bf16[4,128,1024]{2,1,0:T(8,128)(2,1)}, u32[]{:S(2)}) copy-start(bf16[4,128,1024]{2,1,0:T(8,128)(2,1)} %get-tuple-element.111) | copy-start | bytes 3145732
  310.4 116.4 %reduce-scatter.12.cloned.1.call-start = ((), (), s32[]{:S(2)}) async-start(), calls=%async_computation.13 | async-start | bytes 2359296 | tf_op jit(solution)/shard_map/reduce_scatter | solution.py:1625
  333.5 14.5 %copy-start.1 = (bf16[4,128,256]{2,1,0:T(8,128)(2,1)S(1)}, bf16[4,128,256]{2,1,0:T(8,128)(2,1)}, u32[]{:S(2)}) copy-start(bf16[4,128,256]{2,1,0:T(8,128)(2,1)} %attend.1) | copy-start | bytes 786436
  333.5 14.5 %copy-start.5 = (bf16[4,128,1024]{2,1,0:T(8,128)(2,1)S(1)}, bf16[4,128,1024]{2,1,0:T(8,128)(2,1)}, u32[]{:S(2)}) copy-start(bf16[4,128,1024]{2,1,0:T(8,128)(2,1)} %get-tuple-element.131) | copy-start | bytes 3145732
  355.0 22.4 %copy-start.24 = (bf16[1024,1024]{1,0:T(8,128)(2,1)S(1)}, bf16[1024,1024]{1,0:T(8,128)(2,1)}, u32[]{:S(2)}) copy-start(bf16[1024,1024]{1,0:T(8,128)(2,1)} %all-gather.6.cloned.1.call-done) | copy-start | bytes 6291460
  355.1 102.6 %reduce-scatter.14.cloned.1.call-start = ((), (), s32[]{:S(2)}) async-start(), calls=%async_computation.14 | async-start | bytes 4718592 | tf_op jit(solution)/shard_map/reduce_scatter | solution.py:1637
  389.0 16.0 %copy-start.17 = (f32[3,1024]{1,0:T(4,128)S(1)}, f32[3,1024]{1,0:T(4,128)}, u32[]{:S(2)}) copy-start(f32[3,1024]{1,0:T(4,128)} %get-tuple-element.145) | copy-start | bytes 36868
  389.0 16.0 %copy-start.18 = (f32[3,1024]{1,0:T(4,128)S(1)}, f32[3,1024]{1,0:T(4,128)}, u32[]{:S(2)}) copy-start(f32[3,1024]{1,0:T(4,128)} %get-tuple-element.146) | copy-start | bytes 36868
  389.0 16.0 %copy-start.19 = (f32[3,1024]{1,0:T(4,128)S(1)}, f32[3,1024]{1,0:T(4,128)}, u32[]{:S(2)}) copy-start(f32[3,1024]{1,0:T(4,128)} %get-tuple-element.147) | copy-start | bytes 36868
  389.0 16.0 %copy-start.20 = (f32[3,1024]{1,0:T(4,128)S(1)}, f32[3,1024]{1,0:T(4,128)}, u32[]{:S(2)}) copy-start(f32[3,1024]{1,0:T(4,128)} %get-tuple-element.148) | copy-start | bytes 36868
  404.9 20.5 %copy-start.12 = (bf16[128,1024]{1,0:T(8,128)(2,1)S(1)}, bf16[128,1024]{1,0:T(8,128)(2,1)}, u32[]{:S(2)}) copy-start(bf16[128,1024]{1,0:T(8,128)(2,1)} %reduce-scatter.6.cloned.1.call-done) | copy-start | bytes 786436
  443.8 24.6 %copy-start.9 = (f32[128,1024]{1,0:T(8,128)S(1)}, f32[128,1024]{1,0:T(8,128)}, u32[]{:S(2)}) copy-start(f32[128,1024]{1,0:T(8,128)} %get-tuple-element.363) | copy-start | bytes 1572868
  448.5 20.7 %copy-start.10 = (f32[128,1024]{1,0:T(8,128)S(1)}, f32[128,1024]{1,0:T(8,128)}, u32[]{:S(2)}) copy-start(f32[128,1024]{1,0:T(8,128)} %get-tuple-element.364) | copy-start | bytes 1572868
  (20 other events, 41.7 us)
Sparse Core Ops, SparseCore 0:
  9.6 51.2 all-gather.5
  67.0 30.3 all-gather.7
  99.0 24.7 all-gather.9
  125.3 28.4 all-gather.11
  155.2 28.5 all-gather.13
  258.5 37.2 reduce-scatter.5
  298.1 34.5 reduce-scatter.7
  335.0 32.9 reduce-scatter.9
  370.3 34.3 reduce-scatter.11
  406.8 50.8 reduce-scatter.13

commit v3 on v2

--- a/solution.py
+++ b/solution.py
@@ -18,7 +18,8 @@
 MASKED = -1e30
 UTTERANCE_LIMIT = 4
 MESH = pl.DeviceIdType.MESH
-PIECES = 4
+PIECES = 2
+LAG = 2
 BLOCK = 16
 MARGIN = 16
 LANES = 128
@@ -652,9 +653,9 @@
     return pieces
 
 
-def row_of(shards, first):
+def row_of(shards, line, first):
     rows = shards.shape[0]
-    lines = shards[:, 0, :]
+    lines = shards[:, line, :]
     lanes = lax.broadcasted_iota(jnp.int32, lines.shape, 1) // 32
     places = lax.broadcasted_iota(jnp.int32, lines.shape, 0) % 4
     merged = jnp.zeros_like(lines)
@@ -682,10 +683,10 @@
 def exchange_kernel(n, m, width, inner, *refs):
     early_up, late_up, project, filter_up, output, filter_down, depth, segs, frames = refs[:9]
     singles, lifts, table = refs[9:28], refs[28:31], refs[31]
-    early_full, late_split, mixer_split, filter_split, small_all, depth_all, segs_all, spread = refs[32:40]
-    scratch = refs[40:]
-    small, gains, held, local, send, recv, small_send, small_recv = scratch[:8]
-    up_send, up_recv, pass_send, pass_recv, out_send, out_recv, depth_send, depth_recv = scratch[8:]
+    early_full, late_split, mixer_split, filter_split, small_all, gains, depth_all, segs_all, spread = refs[32:41]
+    scratch = refs[41:]
+    small, held, local, send, recv, small_send, small_recv = scratch[:7]
+    up_send, up_recv, pass_send, pass_recv, out_send, out_recv, depth_send, depth_recv = scratch[7:]
     pack_small(small, singles, lifts, table)
     me, lane = lax.axis_index("dp"), lax.axis_index("fsdp")
     here = me * m + lane
@@ -783,9 +784,9 @@
     to_partner(0).start()
     own_small.wait()
     lax.fori_loop(1, n * m, wait_small, 0)
-    for index in range(2):
-        for tile, line in enumerate(row_of(small_all, index)):
-            gains[pl.ds(index, 1), pl.ds(tile * LANES, LANES)] = line
+    for index in range(len(singles)):
+        for tile, line in enumerate(row_of(small_all, index // 4, index % 4)):
+            gains[index : index + 1, tile * LANES : (tile + 1) * LANES] = line
     gain, shift = gains[0:1, :], gains[1:2, :]
 
     def work(block, carry):
@@ -823,6 +824,7 @@
         jax.ShapeDtypeStruct((n, rows, 4 * inner), low),
         jax.ShapeDtypeStruct((n, rows, 3 * inner), low),
         jax.ShapeDtypeStruct((n * m,) + packed, jnp.float32),
+        jax.ShapeDtypeStruct((len(singles), deep), jnp.float32),
         jax.ShapeDtypeStruct((m,) + depth.shape, low),
         jax.ShapeDtypeStruct((n,) + segs.shape, segs.dtype),
         jax.ShapeDtypeStruct((n, frame_count, deep), low),
@@ -834,10 +836,9 @@
         functools.partial(exchange_kernel, n, m, width, inner),
         out_shape=outs,
         in_specs=[anywhere] * 8 + [inside] * (2 + len(singles) + len(lifts)),
-        out_specs=[anywhere] * 4 + [inside] + [anywhere] * 3,
+        out_specs=[anywhere] * 4 + [inside] * 2 + [anywhere] * 3,
         scratch_shapes=[
             pltpu.VMEM(packed, jnp.float32),
-            pltpu.VMEM((2, deep), jnp.float32),
             pltpu.VMEM((frame_count, deep), low),
             dma((2 * n + 8 + 3,)),
             dma((n - 1, 7)),
@@ -1032,129 +1033,193 @@
     return [grad], None, [total * unit, total]
 
 
-def boundary_kernel(n, step, shape, *refs):
-    summed, gathered, state_count, out_count, sum_count, vector_count = shape
+def boundary_kernel(step, shape, *refs):
+    gathered, state_count, out_count, sum_count, picked = shape
     refs = list(refs)
     take = lambda count: [refs.pop(0) for unused in range(count)]
-    part = take(1)[0] if summed else None
+    part = take(1)[0]
     states = take(state_count)
     vectors = take(1)[0]
     outs = take(out_count)
     spread = take(1)[0] if gathered else None
     sums = take(1)[0] if sum_count else None
-    if summed:
-        arrived, own, own_sem, send, recv = take(5)
+    arrived, passing, mine, merged, own, local = take(6)
+    relay_send, relay_recv, direct_send, direct_recv, merge_send, merge_recv = take(6)
     if gathered:
-        held, held_sem, out_send, out_recv = take(4)
+        held, held_sem, out_send, out_recv, pass_send, pass_recv = take(6)
     partials = take(1)[0] if sum_count else None
     me = lax.axis_index("dp")
-    others = near(me, n)
-    rows = states[0].shape[0]
-    height = rows // PIECES
-    greet([target for target, unused in others])
-    incoming = {}
-    if summed:
-        own_copy = pltpu.make_async_copy(part.at[me], own, own_sem)
-        for piece in range(PIECES):
-            span = pl.ds(piece * height, height)
-            for peer, (target, unused) in enumerate(others):
-                copy = remote(
-                    part.at[target, span], arrived.at[peer, span], send.at[peer, piece], recv.at[peer, piece], {"dp": target}
-                )
-                copy.start()
-                incoming[peer, piece] = copy
-        own_copy.start()
-        own_copy.wait()
+    row, column = me // 2, me % 2
+    sides = [row * 2 + 1 - column, (1 - row) * 2 + column]
+    across = (1 - row) * 2 + 1 - column
+    half = own.shape[0] // 2
+    height = half // PIECES
+    both, places = range(2), range(PIECES)
+
+    def span(axis, piece):
+        return pl.ds(axis * half + piece * height, height)
+
+    def inner(piece):
+        return pl.ds(piece * height, height)
+
+    def relay(axis, piece):
+        return remote(
+            part.at[across, span(axis, piece)],
+            passing.at[axis, inner(piece)],
+            relay_send.at[axis, piece],
+            relay_recv.at[axis, piece],
+            {"dp": sides[axis]},
+        )
+
+    def direct(axis, piece):
+        return remote(
+            part.at[sides[axis], span(axis, piece)],
+            arrived.at[axis, span(axis, piece)],
+            direct_send.at[axis, piece],
+            direct_recv.at[axis, piece],
+            {"dp": sides[axis]},
+        )
+
+    def merge(axis, piece):
+        return remote(
+            merged.at[axis, inner(piece)],
+            arrived.at[1 - axis, span(axis, piece)],
+            merge_send.at[axis, piece],
+            merge_recv.at[axis, piece],
+            {"dp": sides[1 - axis]},
+        )
+
+    def hand(target, axis, piece):
+        return remote(
+            held.at[span(axis, piece)],
+            spread.at[me, span(axis, piece)],
+            out_send.at[target, axis, piece],
+            out_recv.at[target, axis, piece],
+            {"dp": sides[target]},
+        )
+
+    def onward(axis, piece):
+        block = spread.at[sides[axis], span(axis, piece)]
+        return remote(
+            block, block, pass_send.at[axis, piece], pass_recv.at[axis, piece], {"dp": sides[1 - axis]}
+        )
+
+    def forward(axis, piece):
+        hand(axis, axis, piece).wait_recv()
+        onward(axis, piece).start()
+
+    greet(sides)
+    for piece in places:
+        for axis in both:
+            relay(axis, piece).start()
+    locals_ = [
+        pltpu.make_async_copy(part.at[sides[1 - axis], pl.ds(axis * half, half)], mine.at[axis], local.at[axis])
+        for axis in both
+    ]
+    locals_.append(pltpu.make_async_copy(part.at[me], own, local.at[2]))
+    for copy in locals_:
+        copy.start()
+    for piece in places:
+        for axis in both:
+            direct(axis, piece).start()
     if sum_count:
         partials[...] = jnp.zeros_like(partials)
-    outgoing = []
-    rows_of = [vectors[pl.ds(index, 1), :] for index in range(vector_count)]
-    for piece in range(PIECES):
-        if summed:
-            for peer in range(n - 1):
-                incoming[peer, piece].wait_recv()
+    for copy in locals_:
+        copy.wait()
+    for piece in places:
+        for axis in both:
+            relay(axis, piece).wait_recv()
+
+            def join(block, carry):
+                rows = pl.ds(pl.multiple_of(piece * height + block * BLOCK, BLOCK), BLOCK)
+                total = passing[axis, rows, :].astype(jnp.float32) + mine[axis, rows, :].astype(jnp.float32)
+                merged[axis, rows, :] = total.astype(jnp.bfloat16)
+                return carry
+
+            lax.fori_loop(0, height // BLOCK, join, 0)
+            merge(axis, piece).start()
+    rows_of = [vectors[pl.ds(index, 1), :] for index in picked]
+    order = [(axis, piece) for piece in places for axis in both]
+    for at, (axis, piece) in enumerate(order):
+        direct(axis, piece).wait_recv()
+        merge(axis, piece).wait_recv()
 
         def work(block, carry):
-            span = pl.ds(pl.multiple_of(piece * height + block * BLOCK, BLOCK), BLOCK)
-            total = None
-            if summed:
-                total = own[span, :].astype(jnp.float32)
-                for peer in range(n - 1):
-                    total = total + arrived[peer, span, :].astype(jnp.float32)
-            made, sent, terms = step(total, [state[span, :] for state in states], rows_of)
+            rows = pl.ds(pl.multiple_of(axis * half + piece * height + block * BLOCK, BLOCK), BLOCK)
+            total = own[rows, :].astype(jnp.float32)
+            for side in both:
+                total = total + arrived[side, rows, :].astype(jnp.float32)
+            made, sent, terms = step(total, [state[rows, :].astype(jnp.float32) for state in states], rows_of)
             for out, value in zip(outs, made):
-                out[span, :] = value
+                out[rows, :] = value
             if gathered:
-                held[span, :] = sent.astype(jnp.bfloat16)
+                held[rows, :] = sent.astype(jnp.bfloat16)
             for index, term in enumerate(terms):
                 partials[index] += sum(term[8 * low : 8 * low + 8] for low in range(BLOCK // 8))
             return carry
 
         lax.fori_loop(0, height // BLOCK, work, 0)
         if gathered:
-            span = pl.ds(piece * height, height)
-            for peer, (target, unused) in enumerate(others):
-                copy = remote(
-                    held.at[span], spread.at[me, span], out_send.at[peer, piece], out_recv.at[peer, piece], {"dp": target}
-                )
-                copy.start()
-                outgoing.append(copy)
+            for target in both:
+                hand(target, axis, piece).start()
+            if at >= LAG:
+                forward(*order[at - LAG])
     if gathered:
         keep = pltpu.make_async_copy(held, spread.at[me], held_sem)
         keep.start()
+        for axis, piece in order[len(order) - LAG :]:
+            forward(axis, piece)
     for index in range(sum_count):
         sums[pl.ds(index, 1), :] = jnp.sum(partials[index], axis=0, keepdims=True)
-    for copy in incoming.values():
-        copy.wait_send()
-    for copy in outgoing:
-        copy.wait()
+    for axis, piece in order:
+        relay(axis, piece).wait_send()
+        direct(axis, piece).wait_send()
+        merge(axis, piece).wait_send()
     if gathered:
+        for axis, piece in order:
+            hand(axis, axis, piece).wait_send()
+            hand(1 - axis, axis, piece).wait()
+        for axis, piece in order:
+            onward(axis, piece).wait()
         keep.wait()
 
 
-def boundary(n, step, part, states, vectors, out_count, sum_count, number, gathered=True):
-    rows, width = states[0].shape
-    summed = part is not None
+def boundary(step, part, states, vectors, picked, out_count, sum_count, number, gathered=True):
+    n, rows, width = part.shape
     inside = pl.BlockSpec(memory_space=pltpu.VMEM)
     anywhere = pl.BlockSpec(memory_space=pl.ANY)
-    shape = (summed, gathered, len(states), out_count, sum_count, len(vectors))
-    operands, in_specs, outs, out_specs, scratch = [], [], [], [], []
-    if summed:
-        operands.append(part)
-        in_specs.append(anywhere)
-        scratch += [
-            pltpu.VMEM((n - 1, rows, width), jnp.bfloat16),
-            pltpu.VMEM((rows, width), jnp.bfloat16),
-            pltpu.SemaphoreType.DMA,
-            pltpu.SemaphoreType.DMA((n - 1, PIECES)),
-            pltpu.SemaphoreType.DMA((n - 1, PIECES)),
-        ]
-    operands += list(states) + [jnp.stack(vectors)]
-    in_specs += [inside] * (len(states) + 1)
-    outs += [jax.ShapeDtypeStruct((rows, width), jnp.float32)] * out_count
-    out_specs += [inside] * out_count
+    dma = pltpu.SemaphoreType.DMA
+    shape = (gathered, len(states), out_count, sum_count, picked)
+    low = jnp.bfloat16
+    scratch = [
+        pltpu.VMEM((2, rows, width), low),
+        pltpu.VMEM((2, rows // 2, width), low),
+        pltpu.VMEM((2, rows // 2, width), low),
+        pltpu.VMEM((2, rows // 2, width), low),
+        pltpu.VMEM((rows, width), low),
+        dma((3,)),
+    ]
+    scratch += [dma((2, PIECES))] * 6
+    outs = [jax.ShapeDtypeStruct((rows, width), jnp.float32)] * out_count
+    out_specs = [inside] * out_count
     if gathered:
-        outs.append(jax.ShapeDtypeStruct((n, rows, width), jnp.bfloat16))
+        outs.append(jax.ShapeDtypeStruct((n, rows, width), low))
         out_specs.append(anywhere)
-        scratch += [
-            pltpu.VMEM((rows, width), jnp.bfloat16),
-            pltpu.SemaphoreType.DMA,
-            pltpu.SemaphoreType.DMA((n - 1, PIECES)),
-            pltpu.SemaphoreType.DMA((n - 1, PIECES)),
-        ]
+        scratch += [pltpu.VMEM((rows, width), low), dma]
+        scratch += [dma((2, 2, PIECES))] * 2 + [dma((2, PIECES))] * 2
     if sum_count:
         outs.append(jax.ShapeDtypeStruct((sum_count, width), jnp.float32))
         out_specs.append(inside)
         scratch.append(pltpu.VMEM((sum_count, 8, width), jnp.float32))
     return pl.pallas_call(
-        functools.partial(boundary_kernel, n, step, shape),
+        functools.partial(boundary_kernel, step, shape),
         out_shape=outs,
-        in_specs=in_specs,
+        in_specs=[anywhere] + [inside] * (len(states) + 1),
         out_specs=out_specs,
         scratch_shapes=scratch,
         compiler_params=pltpu.CompilerParams(collective_id=number, has_side_effects=True),
         name="boundary",
-    )(*operands)
+    )(part, *states, vectors)
 
 
 def toeplitz(line, frame_count):
@@ -1476,8 +1541,6 @@
     hidden = early_up.shape[1] // n
     inner = D // n
     heads = HEADS // n
-    start_rows = frames.astype(jnp.float32)
-    final_upstream = cotangent.astype(jnp.float32)
     singles = [
         early_gain, early_shift, early_drop, mixer_gain, mixer_shift, query_bias, value_bias, mixer_drop,
         filter_gain, filter_shift, depth_bias, middle_gain, middle_shift, filter_drop, late_gain, late_shift,
@@ -1485,7 +1548,9 @@
     ]
     spans = hidden * n // D
     w_early_down = gather_rows(early_down)
-    w_early_up, late_up_split, mixer_split, filter_split, small_all, depth_all, segments_all, early_hidden = exchange(
+    (
+        w_early_up, late_up_split, mixer_split, filter_split, small_all, vectors, depth_all, segments_all, early_hidden
+    ) = exchange(
         n, m, early_up, late_up, mixer_project, filter_up, mixer_output, filter_down, depth_weight,
         segments.reshape(1, frame_count), frames, singles, [early_lift, late_lift, filter_lift], distance_table,
     )
@@ -1496,7 +1561,6 @@
     w_late_down = gather_rows(late_down)
 
     lines = -(-len(singles) * rows // LANES)
-    vectors = jnp.transpose(small_all[:, :lines].reshape(n * m, lines, LANES // rows, rows), (1, 2, 0, 3)).reshape(-1, D)
     own_vectors = lax.dynamic_slice(vectors, (0, me * inner), (vectors.shape[0], inner))
     own_lifts = lax.dynamic_slice(small_all, (me * m, lines, 0), (m, 2, LANES))
     early_lifts, late_lifts = own_lifts[:, 0].reshape(-1), own_lifts[:, 1].reshape(-1)
@@ -1529,12 +1593,14 @@
         widened_low = widened_grad.astype(jnp.bfloat16)
         up_slope = lead_dot(flat(hidden_rows), widened_low).astype(jnp.bfloat16)
         part = blocks(back_dot(widened_low, w_up).astype(jnp.bfloat16))
-        part, down_slope, up_slope = lax.optimization_barrier((part, down_slope, up_slope))
-        return part, down_slope, up_slope, jnp.sum(widened_grad, axis=0)
+        down_slope = jnp.transpose(down_slope.reshape(m, spans, rows, D), (1, 0, 2, 3)).reshape(spans, m * rows, D)
+        slope = jnp.concatenate([up_slope.reshape(n, D // n, hidden), down_slope])
+        part, slope = lax.optimization_barrier((part, slope))
+        return part, slope, jnp.sum(widened_grad, axis=0)
 
     early_wide, early_active, part = feed(early_hidden, w_early_up, early_lifts, w_early_down)
     first_rows, mixer_hidden = boundary(
-        n, functools.partial(step_forward, 0.5), part, [start_rows], [vectors[2], vectors[3], vectors[4]], 1, 0, 2
+        functools.partial(step_forward, 0.5), part, [frames], vectors, (2, 3, 4), 1, 0, 2
     )
     mixer_hidden, w_mixer = lax.optimization_barrier((mixer_hidden, w_mixer))
     w_project = w_mixer[:, :, : 3 * inner].reshape(D, 3 * inner)
@@ -1543,7 +1609,7 @@
     blended = attend(packed, segment_rows, segment_columns, table)
     part = blocks(flat_dot(flat(blended), w_output).astype(jnp.bfloat16))
     second_rows, filter_hidden = boundary(
-        n, functools.partial(step_forward, 1.0), part, [first_rows], [vectors[7], vectors[8], vectors[9]], 1, 0, 3
+        functools.partial(step_forward, 1.0), part, [first_rows], vectors, (7, 8, 9), 1, 0, 3
     )
     filter_hidden, w_filter = lax.optimization_barrier((filter_hidden, w_filter))
     w_filter_up = w_filter[:, :, : 2 * inner].reshape(D, 2 * inner)
@@ -1565,21 +1631,20 @@
     swished = (middle * jax.nn.sigmoid(middle)).astype(jnp.bfloat16)
     part = blocks(flat_dot(swished, w_filter_down).astype(jnp.bfloat16))
     third_rows, late_hidden = boundary(
-        n, functools.partial(step_forward, 1.0), part, [second_rows], [vectors[13], vectors[14], vectors[15]], 1, 0, 5
+        functools.partial(step_forward, 1.0), part, [second_rows], vectors, (13, 14, 15), 1, 0, 5
     )
     late_hidden, w_late_up, w_late_down = lax.optimization_barrier((late_hidden, w_late_up, w_late_down))
     late_wide, late_active, part = feed(late_hidden, w_late_up, late_lifts, w_late_down)
     layer_out, grad, low, turn_sums = boundary(
-        n, step_turn, part, [third_rows, final_upstream], [vectors[16], vectors[17], vectors[18]], 2, 3, 6
-    )
-
-    part, late_down_slope, late_up_slope, late_lift_slope = feed_back(
+        step_turn, part, [third_rows, cotangent], vectors, (16, 17, 18), 2, 3, 6
+    )
+
+    part, late_slope, late_lift_slope = feed_back(
         low, late_hidden, late_wide, late_active, w_late_up, w_late_down
     )
-    late_down_slope = scatter_rows(late_down_slope)
-    late_up_slope = scatter_split(late_up_slope, n)
+    late_slope = lax.psum_scatter(late_slope, "fsdp", scatter_dimension=1, tiled=True)
     grad, low, late_sums = boundary(
-        n, functools.partial(step_backward, 1.0), part, [grad, third_rows], [vectors[14]], 1, 3, 7
+        functools.partial(step_backward, 1.0), part, [grad, third_rows], vectors, (14,), 1, 3, 7
     )
     low = flat(low)
     filter_down_slope = lead_dot(swished, low).astype(jnp.bfloat16)
@@ -1610,7 +1675,7 @@
     part, filter_slope = lax.optimization_barrier((part, pair_slopes(filter_up_slope, filter_down_slope, n)))
     filter_slope = lax.psum_scatter(filter_slope, "fsdp", scatter_dimension=1, tiled=True)
     grad, low, filter_sums = boundary(
-        n, functools.partial(step_backward, 1.0), part, [grad, second_rows], [vectors[8]], 1, 3, 9
+        functools.partial(step_backward, 1.0), part, [grad, second_rows], vectors, (8,), 1, 3, 9
     )
     low = flat(low)
     output_slope = lead_dot(flat(blended), low).astype(jnp.bfloat16)
@@ -1619,25 +1684,20 @@
     packed_low = flat(packed_low)
     project_slope = lead_dot(flat(mixer_hidden), packed_low).astype(jnp.bfloat16)
     part = blocks(back_dot(packed_low, w_project).astype(jnp.bfloat16))
-    part, mixer_slope, late_down_slope, late_up_slope = lax.optimization_barrier(
-        (part, pair_slopes(project_slope, output_slope, n), late_down_slope, late_up_slope)
+    part, mixer_slope, late_slope = lax.optimization_barrier(
+        (part, pair_slopes(project_slope, output_slope, n), late_slope)
     )
     mixer_slope = lax.psum_scatter(mixer_slope, "fsdp", scatter_dimension=1, tiled=True)
     grad, low, mixer_sums = boundary(
-        n, functools.partial(step_backward, 0.5), part, [grad, first_rows], [vectors[3]], 1, 3, 10
-    )
-    part, early_down_slope, early_up_slope, early_lift_slope = feed_back(
+        functools.partial(step_backward, 0.5), part, [grad, first_rows], vectors, (3,), 1, 3, 10
+    )
+    part, early_slope, early_lift_slope = feed_back(
         low, early_hidden, early_wide, early_active, w_early_up, w_early_down
-    )
-    early_down_slope = jnp.transpose(early_down_slope.reshape(m, spans, rows, D), (1, 0, 2, 3))
-    early_slope = jnp.concatenate(
-        [early_up_slope.reshape(n, D // n, hidden), early_down_slope.reshape(spans, m * rows, D)]
     )
     part, early_slope, filter_slope = lax.optimization_barrier((part, early_slope, filter_slope))
     early_slope = lax.psum_scatter(early_slope, "fsdp", scatter_dimension=1, tiled=True)
-    early_up_slope, early_down_slope = early_slope[:n], early_slope[n:].reshape(spans * rows, D)
     slope_frames, early_sums = boundary(
-        n, step_last, part, [grad, start_rows], [vectors[0]], 1, 2, 11, gathered=False
+        step_last, part, [grad, frames], vectors, (0,), 1, 2, 11, gathered=False
     )
 
     table_slope = jnp.roll(table_slope[:, ::-1], 1 - NREL // 2, axis=1)
@@ -1678,9 +1738,9 @@
     tables = jnp.transpose(jnp.sum(tables, axis=1).reshape(HEADS, table_rows))
     group = jnp.sum(group_all, axis=0).reshape(-1)[:group_used].reshape(group_count, rows)
     late_up_wide, project_wide, filter_up_wide = giveback(
-        n, [late_up_slope, mixer_slope, filter_slope], [(1, hidden), (3, inner), (2, inner)], 13
-    )
-    (early_up_wide,) = giveback(n, [early_up_slope], [(1, hidden)], 14)
+        n, [late_slope, mixer_slope, filter_slope], [(1, hidden), (3, inner), (2, inner)], 13
+    )
+    (early_up_wide,) = giveback(n, [early_slope], [(1, hidden)], 14)
 
     def rejoin(value, low):
         return final(jnp.transpose(value[:, :, low:], (1, 0, 2)).reshape(rows, D))
@@ -1696,7 +1756,7 @@
         wide[13],
         final(early_up_wide),
         jnp.transpose(group[lift_slopes : lift_slopes + spans]).reshape(-1),
-        final(early_down_slope),
+        final(early_slope[n:]).reshape(spans * rows, D),
         wide[11],
         wide[9],
         wide[10],
@@ -1720,7 +1780,7 @@
         wide[4],
         final(late_up_wide),
         jnp.transpose(group[lift_slopes + spans : lift_slopes + 2 * spans]).reshape(-1),
-        final(late_down_slope),
+        final(late_slope[n:]).reshape(spans * rows, D),
         wide[2],
         wide[0],
         wide[1],

time: 482 us -> 449 us (0.932)
  Pallas kernels: 328 us -> 312 us
  waiting for transfers between devices: 12.5 us -> 2.63 us
  matrix products: 58.9 us -> 53.4 us
    pallas_call x8, Pallas kernels: 193 us -> 176 us  [boundary(): pl.pallas_call(functools.partial(boundary_kernel, step, shape), out_shape...]
    reduce_scatter x1, waiting for transfers between devices: 9.21 us -> 0.02 us  [split_body(): lax.psum_scatter(early_slope, 'fsdp', scatter_dimension=1, tiled=True)]
  transfers between devices with their start and end apart: 10 -> 9, of which waited for: 1 -> 0; matrix products, arithmetic and copies ran while one was open for 19% -> 20% of each run, Pallas kernels for 62% -> 64%
where the time goes in v3:
time: 449 us; the launch traced here: 444 us
  Pallas kernels  312 us (69%)
  matrix products  53.4 us (12%)
  local copies, waits for them, and re-layouts  32.3 us (7%)
  other arithmetic  28.6 us (6%)
  between operations  15 us (3%)
    pallas_call x8, Pallas kernels, boundary(): pl.pallas_call(functools.partial(boundary_kernel, step, shape), out_shape...  176 us
    pallas_call x1, Pallas kernels, exchange(): pl.pallas_call(functools.partial(exchange_kernel, n, m, width, inner), ou...  58.8 us
    dot_general x8, matrix products, flat_dot(): return jnp.dot(left_rows, right_rows, preferred_element_type=jnp.float32)  22.7 us
    dot_general x8, matrix products, back_dot(): lax.dot_general(left_rows, right_rows, (((1,), (1,)), ((), ())), preferre...  20.4 us
    pallas_call x2, Pallas kernels, giveback(): pl.pallas_call(functools.partial(giveback_kernel, n, sizes), out_shape=ou...  17.4 us
    pallas_call x1, Pallas kernels, collect(): pl.pallas_call(functools.partial(collect_kernel, n, m), out_shape=[jax.Sh...  13.3 us
    pallas_call x2, Pallas kernels, share(): pl.pallas_call(functools.partial(share_kernel, n), out_shape=jax.ShapeDty...  12.4 us
    pallas_call x1, Pallas kernels, unattend(): pl.pallas_call(functools.partial(unattend_kernel, heads), grid=(blocks,),...  12 us
  transfers between devices with their start and end apart: 9, of which 0 were waited for; matrix products, arithmetic and copies ran while one was open for 20% of the time, Pallas kernels for 64%

profile of v3, /device:TPU:0, one launch (start us, length us, event | category | flops | bytes accessed | tf_op | source)
XLA Modules:
  0.0 444.2 jit_solution(10739626965928201541)
XLA Ops:
  8.0 58.8 %exchange.1 = (bf16[32,32,1024]{2,1,0:T(8,128)(2,1)}, bf16[4,32,1024]{2,1,0:T(8,128)(2,1)}, bf16[4,32,1024]{2,1,0:T(8,128)(2,1)}, bf16[4,32,768]{2,1,0:T(8,128)(...) custom-call(bf16[32,4096]{1,0:T(8,128)(2,1)} %refs_0_.1, ...), custom_call_target="tpu_custom_call" | custom-call | tf_op jit(solution)/shard_map/exchange/pallas_call | solution.py:835
  73.1 3.9 fusion.13
  82.8 4.6 %convolution_convert_fusion.10 = bf16[512,1024]{1,0:T(8,128)(2,1)} fusion(bf16[1024,1024]{1,0:T(8,128)(2,1)} %all-gather.6.cloned.1.call-done, f32[512,1024]{1,0:T(8,128)} %fusion.13, f32[1024]{0:T(1024)S(1)} %bitcast.256), kind=kOutput, calls=%fused_computation.23 | convolution fusion | flops 1077411840 | bytes 5246976 | tf_op jit(solution)/shard_map/dot_general | solution.py:29
  87.4 26.2 %boundary.8 = (f32[128,1024]{1,0:T(8,128)}, bf16[4,128,1024]{2,1,0:T(8,128)(2,1)}) custom-call(bf16[4,128,1024]{2,1,0:T(8,128)(2,1)} %bitcast.225, bf16[128,1024]{1,0:T(8,128)(2,1)} %refs_2_.5, f32[19,1024]{1,0:T(8,128)} %get-tuple-element.101.refs_2_.refs_3_), custom_call_target="tpu_custom_call" | custom-call | tf_op jit(solution)/shard_map/boundary/pallas_call | solution.py:1214
  116.9 3.1 add_convert_fusion
  120.0 8.1 %attend.1 = bf16[4,128,256]{2,1,0:T(8,128)(2,1)} custom-call(bf16[4,128,768]{2,1,0:T(8,128)(2,1)} %bitcast.197, s32[4,1,128]{2,1,0:T(1,128)} %get-tuple-element.106.segment_rows, s32[4,128,1]{2,1,0:T(8,128)} %copy.118.segment_columns, f32[4,256]{1,0:T(4,128)} %rev.4.table), custom_call_target="tpu_custom_call" | custom-call | tf_op jit(solution)/shard_map/attend/pallas_call | solution.py:1261
  128.1 2.4 convolution_convert_fusion.9
  130.5 23.3 %boundary.9 = (f32[128,1024]{1,0:T(8,128)}, bf16[4,128,1024]{2,1,0:T(8,128)(2,1)}) custom-call(bf16[4,128,1024]{2,1,0:T(8,128)(2,1)} %bitcast.193, f32[128,1024]{1,0:T(8,128)} %get-tuple-element.107.refs_1_.refs_2_, f32[19,1024]{1,0:T(8,128)} %get-tuple-element.101.refs_2_.refs_3_), custom_call_target="tpu_custom_call" | custom-call | tf_op jit(solution)/shard_map/boundary/pallas_call | solution.py:1214
  157.9 5.0 %convolve.1 = (f32[4,128,256]{2,1,0:T(8,128)}, f32[4,128,256]{2,1,0:T(8,128)}) custom-call(f32[4,128,512]{2,1,0:T(8,128)} %bitcast.195, s32[4,128,1]{2,1,0:T(8,128)} %get-tuple-element.310.behind, s32[4,128,1]{2,1,0:T(8,128)} %get-tuple-element.309.ahead, f32[31,256]{1,0:T(8,128)} %bitcast.232, f32[1,256]{1,0:T(1,128)} %get-tuple-element.277.bias), custom_call_target="tpu_custom_call" | custom-call | tf_op jit(solution)/shard_map/convolve/pallas_call | solution.py:1389
  166.0 6.5 %share.2 = f32[4,8,128]{2,1,0:T(8,128)} custom-call(f32[8,128]{1,0:T(8,128)} %pad_maximum_fusion.5.mine), custom_call_target="tpu_custom_call" | custom-call | tf_op jit(solution)/shard_map/share/pallas_call | solution.py:918
  175.6 24.2 %boundary.10 = (f32[128,1024]{1,0:T(8,128)}, bf16[4,128,1024]{2,1,0:T(8,128)(2,1)}) custom-call(bf16[4,128,1024]{2,1,0:T(8,128)(2,1)} %bitcast.194, f32[128,1024]{1,0:T(8,128)} %get-tuple-element.114.refs_1_.refs_2_, f32[19,1024]{1,0:T(8,128)} %get-tuple-element.101.refs_2_.refs_3_), custom_call_target="tpu_custom_call" | custom-call | tf_op jit(solution)/shard_map/boundary/pallas_call | solution.py:1214
  199.9 3.3 fusion.14
  203.2 2.3 convolution_convert_fusion.7
  205.5 22.6 %boundary.11 = (f32[128,1024]{1,0:T(8,128)}, f32[128,1024]{1,0:T(8,128)}, bf16[4,128,1024]{2,1,0:T(8,128)(2,1)}, f32[3,1024]{1,0:T(4,128)}) custom-call(bf16[4,128,1024]{2,1,0:T(8,128)(2,1)} %bitcast.228, f32[128,1024]{1,0:T(8,128)} %get-tuple-element.120.refs_1_.refs_2_, bf16[128,1024]{1,0:T(8,128)(2,1)} %refs_2_.4, ...), custom_call_target="tpu_custom_call" | custom-call | tf_op jit(solution)/shard_map/boundary/pallas_call | solution.py:1214
  228.1 4.4 fusion.12
  234.2 2.3 convolution_convert_fusion.6
  237.9 2.3 pad_maximum_fusion
  240.3 22.0 %boundary.12 = (f32[128,1024]{1,0:T(8,128)}, bf16[4,128,1024]{2,1,0:T(8,128)(2,1)}, f32[3,1024]{1,0:T(4,128)}) custom-call(bf16[4,128,1024]{2,1,0:T(8,128)(2,1)} %bitcast.222, f32[128,1024]{1,0:T(8,128)} %get-tuple-element.125.refs_1_, f32[128,1024]{1,0:T(8,128)} %get-tuple-element.120.refs_1_.refs_2_, f32[19,1024]{1,0:T(8,128)} %get-tuple-element.101.refs_2_.refs_3_), custom_call_target="tpu_custom_call" | custom-call | tf_op jit(solution)/shard_map/boundary/pallas_call | solution.py:1214
  265.2 5.9 %share.3 = f32[4,8,128]{2,1,0:T(8,128)} custom-call(f32[8,128]{1,0:T(8,128)} %pad_maximum_fusion.6.mine), custom_call_target="tpu_custom_call" | custom-call | tf_op jit(solution)/shard_map/share/pallas_call | solution.py:918
  273.9 8.9 %unconvolve.1 = (bf16[4,128,512]{2,1,0:T(8,128)(2,1)}, f32[1,512]{1,0:T(1,128)}, f32[32,256]{1,0:T(8,128)}) custom-call(f32[4,128,512]{2,1,0:T(8,128)} %bitcast.196, f32[4,128,256]{2,1,0:T(8,128)} %get-tuple-element.122.gated, f32[4,128,256]{2,1,0:T(8,128)} %bitcast.212, s32[4,128,1]{2,1,0:T(8,128)} %get-tuple-element.310.behind, ...), custom_call_target="tpu_custom_call" | custom-call | tf_op jit(solution)/shard_map/unconvolve/pallas_call | solution.py:1451
  288.5 22.1 %boundary.13 = (f32[128,1024]{1,0:T(8,128)}, bf16[4,128,1024]{2,1,0:T(8,128)(2,1)}, f32[3,1024]{1,0:T(4,128)}) custom-call(bf16[4,128,1024]{2,1,0:T(8,128)(2,1)} %bitcast.224, f32[128,1024]{1,0:T(8,128)} %get-tuple-element.129.refs_1_, f32[128,1024]{1,0:T(8,128)} %get-tuple-element.114.refs_1_.refs_2_, f32[19,1024]{1,0:T(8,128)} %get-tuple-element.101.refs_2_.refs_3_), custom_call_target="tpu_custom_call" | custom-call | tf_op jit(solution)/shard_map/boundary/pallas_call | solution.py:1214
  310.6 2.5 convolution_convert_fusion.12
  313.1 12.0 %unattend.1 = (bf16[4,128,768]{2,1,0:T(8,128)(2,1)}, f32[2,256]{1,0:T(2,128)}, f32[4,256]{1,0:T(4,128)}) custom-call(bf16[4,128,768]{2,1,0:T(8,128)(2,1)} %bitcast.198, bf16[4,128,256]{2,1,0:T(8,128)(2,1)} %bitcast.234, s32[4,1,128]{2,1,0:T(1,128)} %get-tuple-element.106.segment_rows, s32[4,128,1]{2,1,0:T(8,128)} %copy.118.segment_columns, f32[4,256]{1,0:T(4,128)} %rev.4.table), custom_call_target="tpu_custom_call" | custom-call | tf_op jit(solution)/shard_map/unattend/pallas_call | solution.py:1329
  330.2 2.1 convolution_convert_fusion.4
  332.3 23.3 %boundary.14 = (f32[128,1024]{1,0:T(8,128)}, bf16[4,128,1024]{2,1,0:T(8,128)(2,1)}, f32[3,1024]{1,0:T(4,128)}) custom-call(bf16[4,128,1024]{2,1,0:T(8,128)(2,1)} %bitcast.223, f32[128,1024]{1,0:T(8,128)} %get-tuple-element.134.refs_1_, f32[128,1024]{1,0:T(8,128)} %get-tuple-element.107.refs_1_.refs_2_, f32[19,1024]{1,0:T(8,128)} %get-tuple-element.101.refs_2_.refs_3_), custom_call_target="tpu_custom_call" | custom-call | tf_op jit(solution)/shard_map/boundary/pallas_call | solution.py:1214
  355.6 2.7 convolution_convert_fusion
  363.3 2.3 pad_maximum_fusion.1
  365.6 3.6 convolution_convert_fusion.5
  372.1 12.1 %boundary.15 = (f32[128,1024]{1,0:T(8,128)}, f32[2,1024]{1,0:T(2,128)}) custom-call(bf16[4,128,1024]{2,1,0:T(8,128)(2,1)} %bitcast.227, f32[128,1024]{1,0:T(8,128)} %get-tuple-element.140.refs_1_, bf16[128,1024]{1,0:T(8,128)(2,1)} %refs_2_.5, f32[19,1024]{1,0:T(8,128)} %get-tuple-element.101.refs_2_.refs_3_), custom_call_target="tpu_custom_call" | custom-call | tf_op jit(solution)/shard_map/boundary/pallas_call | solution.py:1214
  387.4 13.3 %collect.1 = (f32[32,5,128]{2,1,0:T(8,128)}, f32[8,11,128]{2,1,0:T(8,128)}) custom-call(f32[32,5,128]{2,1,0:T(8,128)} %reshape.500.wide, f32[8,11,128]{2,1,0:T(8,128)} %reshape.503.group), custom_call_target="tpu_custom_call" | custom-call | tf_op jit(solution)/shard_map/collect/pallas_call | solution.py:978
  407.1 11.1 %giveback.3 = (bf16[32,4096]{1,0:T(8,128)(2,1)}, bf16[32,3072]{1,0:T(8,128)(2,1)}, bf16[32,2048]{1,0:T(8,128)(2,1)}) custom-call(bf16[8,32,1024]{2,1,0:T(8,128)(2,1)} %reduce-scatter.5.cloned.1.call-done.refs_0_, bf16[4,32,1024]{2,1,0:T(8,128)(2,1)} %reduce-scatter.9.cloned.1.call-done.refs_1_, bf16[4,32,768]{2,1,0:T(8,128)(2,1)} %reduce-scatter.7.cloned.1.call-done.refs_2_), custom_call_target="tpu_custom_call" | custom-call | tf_op jit(solution)/shard_map/giveback/pallas_call | solution.py:888
  426.8 6.4 %giveback.2 = bf16[32,4096]{1,0:T(8,128)(2,1)} custom-call(bf16[8,32,1024]{2,1,0:T(8,128)(2,1)} %reduce-scatter.11.cloned.1.call-done.refs_0_), custom_call_target="tpu_custom_call" | custom-call | tf_op jit(solution)/shard_map/giveback/pallas_call | solution.py:888
  (237 shorter events, 75.8 us)
Async XLA Ops:
  7.2 75.6 %all-gather.6.cloned.1.call-start = ((), (), s32[]{:S(2)}) async-start(), calls=%async_computation.4 | async-start | bytes 2359296 | tf_op jit(solution)/shard_map/all_gather | solution.py:1471
  8.0 105.7 %all-gather.8.cloned.1.call-start = ((), (), s32[]{:S(2)}) async-start(), calls=%async_computation.5 | async-start | bytes 2359296 | tf_op jit(solution)/shard_map/all_gather | solution.py:1558
  66.8 6.2 %copy-start.22 = (bf16[32,32,1024]{2,1,0:T(8,128)(2,1)S(1)}, bf16[32,32,1024]{2,1,0:T(8,128)(2,1)}, u32[]{:S(2)}) copy-start(bf16[32,32,1024]{2,1,0:T(8,128)(2,1)} %get-tuple-element.99) | copy-start | bytes 6291460
  66.9 87.0 %all-gather.10.cloned.1.call-start = ((), (), s32[]{:S(2)}) async-start(), calls=%async_computation.6 | async-start | bytes 1769472 | tf_op jit(solution)/shard_map/all_gather | solution.py:1559
  67.6 132.2 %all-gather.12.cloned.1.call-start = ((), (), s32[]{:S(2)}) async-start(), calls=%async_computation.7 | async-start | bytes 2359296 | tf_op jit(solution)/shard_map/all_gather | solution.py:1475
  68.2 131.7 %all-gather.14.cloned.1.call-start = ((), (), s32[]{:S(2)}) async-start(), calls=%async_computation.8 | async-start | bytes 2359296 | tf_op jit(solution)/shard_map/all_gather | solution.py:1471
  68.8 263.4 %reduce-scatter.5.cloned.1.call-start = ((), (), s32[]{:S(2)}) async-start(), calls=%async_computation.9 | async-start | bytes 4718592 | tf_op jit(solution)/shard_map/reduce_scatter | solution.py:1645
  73.1 7.2 %copy-start.12 = (s32[4,1,128]{2,1,0:T(1,128)S(1)}, s32[4,1,128]{2,1,0:T(1,128)}, u32[]{:S(2)}) copy-start(s32[4,1,128]{2,1,0:T(1,128)} %get-tuple-element.106.segment_rows) | copy-start | bytes 6148
  115.2 4.8 %copy-start.2 = (bf16[4,256,768]{2,1,0:T(8,128)(2,1)}, bf16[4,256,768]{2,1,0:T(8,128)(2,1)S(1)}, u32[]{:S(2)}) copy-start(bf16[4,256,768]{2,1,0:T(8,128)(2,1)S(1)} %slice.186) | copy-start | bytes 4718596
  162.9 11.0 %copy-start = (f32[4,128,256]{2,1,0:T(8,128)S(1)}, f32[4,128,256]{2,1,0:T(8,128)}, u32[]{:S(2)}) copy-start(f32[4,128,256]{2,1,0:T(8,128)} %get-tuple-element.113) | copy-start | bytes 1572868
  199.9 3.3 copy-start.25
  228.1 4.4 %copy-start.32 = (bf16[4,128,1024]{2,1,0:T(8,128)(2,1)S(1)}, bf16[4,128,1024]{2,1,0:T(8,128)(2,1)}, u32[]{:S(2)}) copy-start(bf16[4,128,1024]{2,1,0:T(8,128)(2,1)} %get-tuple-element.123) | copy-start | bytes 3145732
  228.1 4.4 %copy-start.39 = (f32[512,1024]{1,0:T(8,128)S(1)}, f32[512,1024]{1,0:T(8,128)}, u32[]{:S(2)}) copy-start(f32[512,1024]{1,0:T(8,128)} %copy-done.38) | copy-start | bytes 6291460
  240.3 129.0 %reduce-scatter.7.cloned.1.call-start = ((), (), s32[]{:S(2)}) async-start(), calls=%async_computation.10 | async-start | bytes 1769472 | tf_op jit(solution)/shard_map/reduce_scatter | solution.py:1676
  262.5 9.3 %copy-start.4 = (bf16[4,128,1024]{2,1,0:T(8,128)(2,1)S(1)}, bf16[4,128,1024]{2,1,0:T(8,128)(2,1)}, u32[]{:S(2)}) copy-start(bf16[4,128,1024]{2,1,0:T(8,128)(2,1)} %get-tuple-element.126) | copy-start | bytes 3145732
  272.7 10.1 %copy-start.29 = (bf16[4,128,1024]{2,1,0:T(8,128)(2,1)S(1)}, bf16[4,128,1024]{2,1,0:T(8,128)(2,1)}, u32[]{:S(2)}) copy-start(bf16[4,128,1024]{2,1,0:T(8,128)(2,1)} %get-tuple-element.110) | copy-start | bytes 3145732
  288.3 118.7 %reduce-scatter.9.cloned.1.call-start = ((), (), s32[]{:S(2)}) async-start(), calls=%async_computation.11 | async-start | bytes 2359296 | tf_op jit(solution)/shard_map/reduce_scatter | solution.py:1690
  310.6 14.5 %copy-start.1 = (bf16[4,128,256]{2,1,0:T(8,128)(2,1)S(1)}, bf16[4,128,256]{2,1,0:T(8,128)(2,1)}, u32[]{:S(2)}) copy-start(bf16[4,128,256]{2,1,0:T(8,128)(2,1)} %attend.1) | copy-start | bytes 786436
  310.6 14.5 %copy-start.5 = (bf16[4,128,1024]{2,1,0:T(8,128)(2,1)S(1)}, bf16[4,128,1024]{2,1,0:T(8,128)(2,1)}, u32[]{:S(2)}) copy-start(bf16[4,128,1024]{2,1,0:T(8,128)(2,1)} %get-tuple-element.130) | copy-start | bytes 3145732
  332.2 23.3 %copy-start.36 = (f32[512,1024]{1,0:T(8,128)S(1)}, f32[512,1024]{1,0:T(8,128)}, u32[]{:S(2)}) copy-start(f32[512,1024]{1,0:T(8,128)} %fusion.13) | copy-start | bytes 6291460
  332.2 94.6 %reduce-scatter.11.cloned.1.call-start = ((), (), s32[]{:S(2)}) async-start(), calls=%async_computation.12 | async-start | bytes 4718592 | tf_op jit(solution)/shard_map/reduce_scatter | solution.py:1698
  355.6 2.9 copy-start.37
  369.2 2.5 copy-start.13
  369.3 14.9 %copy-start.14 = (f32[3,1024]{1,0:T(4,128)S(1)}, f32[3,1024]{1,0:T(4,128)}, u32[]{:S(2)}) copy-start(f32[3,1024]{1,0:T(4,128)} %get-tuple-element.142) | copy-start | bytes 36868
  369.3 14.9 %copy-start.15 = (f32[3,1024]{1,0:T(4,128)S(1)}, f32[3,1024]{1,0:T(4,128)}, u32[]{:S(2)}) copy-start(f32[3,1024]{1,0:T(4,128)} %get-tuple-element.143) | copy-start | bytes 36868
  369.3 14.9 %copy-start.16 = (f32[3,1024]{1,0:T(4,128)S(1)}, f32[3,1024]{1,0:T(4,128)}, u32[]{:S(2)}) copy-start(f32[3,1024]{1,0:T(4,128)} %get-tuple-element.144) | copy-start | bytes 36868
  369.3 14.9 %copy-start.17 = (f32[3,1024]{1,0:T(4,128)S(1)}, f32[3,1024]{1,0:T(4,128)}, u32[]{:S(2)}) copy-start(f32[3,1024]{1,0:T(4,128)} %get-tuple-element.145) | copy-start | bytes 36868
  384.2 22.0 %slice-start.1 = ((bf16[8,32,1024]{2,1,0:T(8,128)(2,1)}), bf16[4,32,1024]{2,1,0:T(8,128)(2,1)S(1)}, s32[]{:S(2)}) async-start(bf16[8,32,1024]{2,1,0:T(8,128)(2,1)} %reduce-scatter.5.cloned.1.call-done.refs_0_), calls=%async_computation.14 | async-start | bytes 524288 | tf_op jit(solution)/shard_map/slice | solution.py:1783
  400.8 6.2 %copy-start.10 = (f32[32,5,128]{2,1,0:T(8,128)S(1)}, f32[32,5,128]{2,1,0:T(8,128)}, u32[]{:S(2)}) copy-start(f32[32,5,128]{2,1,0:T(8,128)} %get-tuple-element.153) | copy-start | bytes 245764
  421.3 14.5 %copy-start.8 = (f32[128,1024]{1,0:T(8,128)S(1)}, f32[128,1024]{1,0:T(8,128)}, u32[]{:S(2)}) copy-start(f32[128,1024]{1,0:T(8,128)} %get-tuple-element.349) | copy-start | bytes 1572868
  426.2 10.5 %copy-start.9 = (f32[128,1024]{1,0:T(8,128)S(1)}, f32[128,1024]{1,0:T(8,128)}, u32[]{:S(2)}) copy-start(f32[128,1024]{1,0:T(8,128)} %get-tuple-element.350) | copy-start | bytes 1572868
  426.8 8.2 %slice-start = ((bf16[8,32,1024]{2,1,0:T(8,128)(2,1)}), bf16[4,32,1024]{2,1,0:T(8,128)(2,1)S(1)}, s32[]{:S(2)}) async-start(bf16[8,32,1024]{2,1,0:T(8,128)(2,1)} %reduce-scatter.11.cloned.1.call-done.refs_0_), calls=%async_computation.13 | async-start | bytes 524288 | tf_op jit(solution)/shard_map/slice | solution.py:1759
  (20 other events, 34.3 us)
Sparse Core Ops, SparseCore 0:
  9.6 51.2 all-gather.5
  67.0 30.3 all-gather.7
  99.1 24.6 all-gather.9
  125.2 28.3 all-gather.11
  155.1 28.5 all-gather.13
  240.4 50.2 reduce-scatter.4
  292.9 32.9 reduce-scatter.6
  332.4 36.5 reduce-scatter.8
  371.3 50.5 reduce-scatter.10

commit v4 on v3

--- a/solution.py
+++ b/solution.py
@@ -680,20 +680,84 @@
     small[8 : 8 + table.shape[0], 0 : table.shape[1]] = table[...].astype(jnp.float32)
 
 
+def spread_vectors(n, m, inner, me, single_count, small_all, gains, own, lifts, wide_lifts):
+    for index in range(single_count):
+        for tile, line in enumerate(row_of(small_all, index // 4, index % 4)):
+            gains[index : index + 1, tile * LANES : (tile + 1) * LANES] = line
+    own[...] = gains[:, columns(me, inner)]
+    for index in range(2):
+        lines = small_all[pl.ds(me * m, m), 5 + index, :]
+        for tile in range(m):
+            lifts[index : index + 1, tile * LANES : (tile + 1) * LANES] = lines[tile : tile + 1, :]
+    lanes = lax.broadcasted_iota(jnp.int32, (1, LANES), 1)
+    for group in range(2):
+        for tile in range(inner // LANES):
+            first = group * n * m // 2 + me * n + 2 * tile
+            left, right = small_all[pl.ds(first, 1), 7, :], small_all[pl.ds(first + 1, 1), 7, :]
+            low = group * inner + tile * LANES
+            wide_lifts[0:1, low : low + LANES] = jnp.where(
+                lanes < LANES // 2, left, pltpu.roll(right, LANES // 2, 1)
+            )
+
+
 def exchange_kernel(n, m, width, inner, *refs):
-    early_up, late_up, project, filter_up, output, filter_down, depth, segs, frames = refs[:9]
-    singles, lifts, table = refs[9:28], refs[28:31], refs[31]
-    early_full, late_split, mixer_split, filter_split, small_all, gains, depth_all, segs_all, spread = refs[32:41]
-    scratch = refs[41:]
-    small, held, local, send, recv, small_send, small_recv = scratch[:7]
-    up_send, up_recv, pass_send, pass_recv, out_send, out_recv, depth_send, depth_recv = scratch[7:]
-    pack_small(small, singles, lifts, table)
+    early_up, early_down, late_up, project, filter_up, output, filter_down, depth, segs, frames = refs[:10]
+    singles, lift_shards, table = refs[10:29], refs[29:32], refs[32]
+    up_full, down_full, late_split, mixer_split, filter_split, small_all = refs[33:39]
+    gains, own, lifts, wide_lifts, depth_all, segs_all, spread = refs[39:46]
+    gathered, small, held, local, send, recv, small_send, small_recv, up_send, up_recv = refs[46:56]
+    climb_send, climb_recv, pass_send, pass_recv, out_send, out_recv, depth_send, depth_recv = refs[56:]
+    pack_small(gathered.at[0], singles, lift_shards, table)
+    small[...] = gathered[0].astype(jnp.bfloat16)
     me, lane = lax.axis_index("dp"), lax.axis_index("fsdp")
     here = me * m + lane
-    half = m // 2
+    levels = m // 2
+    level = lane // 2
+    units = early_down.shape[0]
     beside = lane + 1 - 2 * (lane % 2)
     others = near(me, n)
+    ways = (1, -1)
     greet_all(n, m)
+
+    def place(kind, unit, source):
+        if kind:
+            return up_full.at[((me + n - unit) % n) * m + source]
+        return down_full.at[source, unit]
+
+    def climb(kind, way, distance, unit, src=None):
+        block = place(kind, unit, (lane + m - 2 * ways[way] * (distance - 1)) % m)
+        return remote(
+            block if src is None else src,
+            block,
+            climb_send.at[kind, way, distance - 1, unit],
+            climb_recv.at[kind, way, distance - 1, unit],
+            {"fsdp": (lane + m + 2 * ways[way]) % m},
+        )
+
+    def across(kind, offset, unit, src=None):
+        block = place(kind, unit, (lane + 2 * offset) % m)
+        return remote(
+            block if src is None else src,
+            block,
+            pass_send.at[kind, offset, unit],
+            pass_recv.at[kind, offset, unit],
+            {"fsdp": beside},
+        )
+
+    def open_way(way):
+        return level < levels - 1 if ways[way] > 0 else level > 0
+
+    def reached(way, distance):
+        return level >= distance if ways[way] > 0 else level + distance < levels
+
+    def launch(kind, unit, src=None):
+        for way in range(2):
+
+            @pl.when(open_way(way))
+            def _():
+                climb(kind, way, 1, unit, src).start()
+
+        across(kind, 0, unit, src).start()
 
     def to_device(step):
         target = {"dp": (me + step // m) % n, "fsdp": (lane + step % m) % m}
@@ -704,48 +768,18 @@
             depth, depth_all.at[lane], depth_send.at[step], depth_recv.at[step], {"fsdp": (lane + step) % m}
         )
 
-    def start_depth(step, carry):
-        to_lane(step).start()
-        return carry
-
-    def wait_depth(step, carry):
-        to_lane(step).wait()
-        return carry
-
     def to_column(step):
-        other, above = (me + step // half) % n, (lane + 2 * (step % half)) % m
-        target = {"dp": other, "fsdp": above}
+        other = (me + step) % n
         return remote(
-            early_up.at[:, columns(other, width)], early_full.at[here], up_send.at[step], up_recv.at[step], target
+            early_up.at[:, columns(other, width)], up_full.at[here], up_send.at[step], up_recv.at[step], {"dp": other}
         )
 
-    def to_partner(step):
-        source = ((me + n - step // half) % n) * m + (lane + m - 2 * (step % half)) % m
-        return remote(
-            early_full.at[source], early_full.at[source], pass_send.at[step], pass_recv.at[step], {"fsdp": beside}
-        )
-
-    def start_small(step, carry):
-        to_device(step).start()
-        return carry
-
-    def wait_small(step, carry):
-        to_device(step).wait()
-        return carry
-
-    def start_column(step, carry):
-        to_column(step).start()
-        return carry
-
-    def relay_column(step, carry):
-        to_column(step).wait_recv()
-        to_partner(step).start()
-        return carry
-
-    def wait_column(step, carry):
-        to_column(step).wait_send()
-        to_partner(step).wait()
-        return carry
+    def each(call):
+        def turn(step, carry):
+            call(step)
+            return carry
+
+        return turn
 
     def pieces(index):
         found = [(late_up.at[:, columns(index, width)], late_split.at[me])]
@@ -758,35 +792,64 @@
         found.append((segs, segs_all.at[me]))
         return found
 
-    lax.fori_loop(1, n * m, start_small, 0)
-    own_small = pltpu.make_async_copy(small, small_all.at[here], local.at[0])
-    own_small.start()
-    own_up = pltpu.make_async_copy(early_up.at[:, columns(me, width)], early_full.at[here], local.at[1])
-    own_up.start()
-    lax.fori_loop(1, n * half, start_column, 0)
+    lax.fori_loop(1, n * m, each(lambda step: to_device(step).start()), 0)
+    lax.fori_loop(1, n, each(lambda step: to_column(step).start()), 0)
+    lax.fori_loop(0, units, each(lambda unit: launch(0, unit, early_down.at[unit])), 0)
+    mine = early_up.at[:, columns(me, width)]
+    launch(1, 0, mine)
     copies = []
     for peer, (target, unused) in enumerate(others):
         for at, (src, dst) in enumerate(pieces(target)):
             copies.append(remote(src, dst, send.at[peer, at], recv.at[peer, at], {"dp": target}))
-    owns = []
-    for src, dst in pieces(me):
-        owns.append((src, dst))
+    owns = [(small, small_all.at[here]), (mine, up_full.at[here]), (early_down, down_full.at[lane])]
+    owns += pieces(me)
     for group in range(n):
         wide = pl.ds(group * inner, inner)
         owns.append((output.at[:, wide], mixer_split.at[group, :, pl.ds(3 * inner, inner)]))
         owns.append((filter_down.at[:, wide], filter_split.at[group, :, pl.ds(2 * inner, inner)]))
-    owns = [pltpu.make_async_copy(src, dst, local.at[2 + at]) for at, (src, dst) in enumerate(owns)]
-    owns.append(pltpu.make_async_copy(depth, depth_all.at[lane], local.at[2 + len(owns)]))
-    for copy in copies + owns:
+    owns.append((depth, depth_all.at[lane]))
+    owns = [pltpu.make_async_copy(src, dst, local.at[at]) for at, (src, dst) in enumerate(owns)]
+    for copy in owns:
         copy.start()
-    lax.fori_loop(1, m, start_depth, 0)
-    own_up.wait()
-    to_partner(0).start()
-    own_small.wait()
-    lax.fori_loop(1, n * m, wait_small, 0)
-    for index in range(len(singles)):
-        for tile, line in enumerate(row_of(small_all, index // 4, index % 4)):
-            gains[index : index + 1, tile * LANES : (tile + 1) * LANES] = line
+    for step in range(1, n):
+        to_column(step).wait_recv()
+        launch(1, step)
+    for copy in copies:
+        copy.start()
+    lax.fori_loop(1, m, each(lambda step: to_lane(step).start()), 0)
+    def carry_on(kind, distance, unit):
+        for way in range(2):
+
+            @pl.when(reached(way, distance))
+            def _():
+                climb(kind, way, distance, unit).wait_recv()
+                offset = levels - distance if ways[way] > 0 else distance
+                across(kind, offset, unit).start()
+                if distance < levels - 1:
+
+                    @pl.when(open_way(way))
+                    def _():
+                        climb(kind, way, distance + 1, unit).start()
+
+    def finish(kind, unit):
+        for offset in range(levels):
+            across(kind, offset, unit).wait()
+        for way in range(2):
+            for distance in range(1, levels):
+                begun = open_way(way)
+                if distance > 1:
+                    begun = begun & reached(way, distance - 1)
+
+                @pl.when(begun)
+                def _():
+                    climb(kind, way, distance, unit).wait_send()
+
+    for kind in range(2):
+        lax.fori_loop(0, units, each(functools.partial(carry_on, kind, 1)), 0)
+    owns[0].wait()
+    lax.fori_loop(1, n * m, each(lambda step: to_device(step).wait()), 0)
+    gathered[...] = small_all[...].astype(jnp.float32)
+    spread_vectors(n, m, inner, me, len(singles), gathered, gains, own, lifts, wide_lifts)
     gain, shift = gains[0:1, :], gains[1:2, :]
 
     def work(block, carry):
@@ -796,38 +859,48 @@
         return carry
 
     lax.fori_loop(0, frames.shape[0] // BLOCK, work, 0)
-    keep = pltpu.make_async_copy(held, spread.at[me], local.at[len(owns) + 2])
+    keep = pltpu.make_async_copy(held, spread.at[me], local.at[len(owns)])
     keep.start()
     outgoing = []
     for peer, (target, unused) in enumerate(others):
         outgoing.append(remote(held, spread.at[me], out_send.at[peer], out_recv.at[peer], {"dp": target}))
     for copy in outgoing:
         copy.start()
-    lax.fori_loop(1, n * half, relay_column, 0)
-    for copy in owns + copies + outgoing:
+
+    for distance in range(2, levels):
+        for kind in range(2):
+            lax.fori_loop(0, units, each(functools.partial(carry_on, kind, distance)), 0)
+    for copy in owns[1:] + copies + outgoing:
         copy.wait()
     keep.wait()
-    to_partner(0).wait()
-    lax.fori_loop(1, n * half, wait_column, 0)
-    lax.fori_loop(1, m, wait_depth, 0)
-
-
-def exchange(n, m, early_up, late_up, project, filter_up, output, filter_down, depth, segs, frames, singles, lifts, table):
+    for kind in range(2):
+        lax.fori_loop(0, units, each(functools.partial(finish, kind)), 0)
+    lax.fori_loop(1, n, each(lambda step: to_column(step).wait_send()), 0)
+    lax.fori_loop(1, m, each(lambda step: to_lane(step).wait()), 0)
+
+
+def exchange(n, m, early_up, early_down, late_up, project, filter_up, output, filter_down, depth, segs, frames, singles, lifts, table):
     rows, width = early_up.shape[0], early_up.shape[1] // n
     inner = output.shape[1] // n
     frame_count, deep = frames.shape
-    low = jnp.bfloat16
+    units, levels = early_down.shape[0], m // 2
+    low, full = jnp.bfloat16, jnp.float32
     packed = (16, LANES)
+    struct = jax.ShapeDtypeStruct
     outs = [
-        jax.ShapeDtypeStruct((n * m, rows, width), low),
-        jax.ShapeDtypeStruct((n, rows, width), low),
-        jax.ShapeDtypeStruct((n, rows, 4 * inner), low),
-        jax.ShapeDtypeStruct((n, rows, 3 * inner), low),
-        jax.ShapeDtypeStruct((n * m,) + packed, jnp.float32),
-        jax.ShapeDtypeStruct((len(singles), deep), jnp.float32),
-        jax.ShapeDtypeStruct((m,) + depth.shape, low),
-        jax.ShapeDtypeStruct((n,) + segs.shape, segs.dtype),
-        jax.ShapeDtypeStruct((n, frame_count, deep), low),
+        struct((n * m, rows, width), low),
+        struct((m,) + early_down.shape, low),
+        struct((n, rows, width), low),
+        struct((n, rows, 4 * inner), low),
+        struct((n, rows, 3 * inner), low),
+        struct((n * m,) + packed, low),
+        struct((len(singles), deep), full),
+        struct((len(singles), inner), full),
+        struct((2, width), full),
+        struct((1, 2 * inner), full),
+        struct((m,) + depth.shape, low),
+        struct((n,) + segs.shape, segs.dtype),
+        struct((n, frame_count, deep), low),
     ]
     anywhere = pl.BlockSpec(memory_space=pl.ANY)
     inside = pl.BlockSpec(memory_space=pltpu.VMEM)
@@ -835,20 +908,23 @@
     return pl.pallas_call(
         functools.partial(exchange_kernel, n, m, width, inner),
         out_shape=outs,
-        in_specs=[anywhere] * 8 + [inside] * (2 + len(singles) + len(lifts)),
-        out_specs=[anywhere] * 4 + [inside] * 2 + [anywhere] * 3,
+        in_specs=[anywhere] * 9 + [inside] * (2 + len(singles) + len(lifts)),
+        out_specs=[anywhere] * 5 + [inside] * 5 + [anywhere] * 3,
         scratch_shapes=[
-            pltpu.VMEM(packed, jnp.float32),
+            pltpu.VMEM((n * m,) + packed, full),
+            pltpu.VMEM(packed, low),
             pltpu.VMEM((frame_count, deep), low),
-            dma((2 * n + 8 + 3,)),
+            dma((2 * n + 12,)),
             dma((n - 1, 7)),
             dma((n - 1, 7)),
             dma((n * m,)),
             dma((n * m,)),
-            dma((n * m // 2,)),
-            dma((n * m // 2,)),
-            dma((n * m // 2,)),
-            dma((n * m // 2,)),
+            dma((n,)),
+            dma((n,)),
+            dma((2, 2, levels - 1, units)),
+            dma((2, 2, levels - 1, units)),
+            dma((2, levels, units)),
+            dma((2, levels, units)),
             dma((n - 1,)),
             dma((n - 1,)),
             dma((m,)),
@@ -856,24 +932,31 @@
         ],
         compiler_params=pltpu.CompilerParams(collective_id=0, has_side_effects=True),
         name="exchange",
-    )(early_up, late_up, project, filter_up, output, filter_down, depth, segs, frames, *singles, *lifts, table)
-
-
-def giveback_kernel(n, sizes, *refs):
-    count = len(sizes)
-    narrows, wides = refs[:count], refs[count : 2 * count]
-    local, send, recv = refs[2 * count :]
+    )(
+        early_up, early_down, late_up, project, filter_up, output, filter_down, depth, segs, frames,
+        *singles, *lifts, table,
+    )
+
+
+def return_copies(n, sizes, narrows, wides, local, send, recv):
     me = lax.axis_index("dp")
-    others = near(me, n)
-    greet([target for target, unused in others])
     copies = []
-    for peer, (target, unused) in enumerate(others):
+    for peer, (target, unused) in enumerate(near(me, n)):
         for at, (place, wide, narrow) in enumerate(column_pieces(me, n, sizes)):
             copies.append(
                 remote(narrows[place].at[target, :, narrow], wides[place].at[:, wide], send.at[peer, at], recv.at[peer, at], {"dp": target})
             )
     for at, (place, wide, narrow) in enumerate(column_pieces(me, n, sizes)):
         copies.append(pltpu.make_async_copy(narrows[place].at[me, :, narrow], wides[place].at[:, wide], local.at[at]))
+    return copies
+
+
+def giveback_kernel(n, sizes, *refs):
+    count = len(sizes)
+    narrows, wides = refs[:count], refs[count : 2 * count]
+    local, send, recv = refs[2 * count :]
+    greet([target for target, unused in near(lax.axis_index("dp"), n)])
+    copies = return_copies(n, sizes, narrows, wides, local, send, recv)
     for copy in copies:
         copy.start()
     for copy in copies:
@@ -930,7 +1013,12 @@
     )(mine)
 
 
-def collect_kernel(n, m, wide, group, wide_all, group_all, local, send, recv, group_send, group_recv):
+def collect_kernel(n, m, sizes, *refs):
+    count = len(sizes)
+    wide, group = refs[:2]
+    narrows, wides = refs[2 : 2 + count], refs[4 + count : 4 + 2 * count]
+    wide_all, group_all = refs[2 + count : 4 + count]
+    local, send, recv, group_send, group_recv, back_local, back_send, back_recv = refs[4 + 2 * count :]
     me, lane = lax.axis_index("dp"), lax.axis_index("fsdp")
     here = me * m + lane
     greet_all(n, m)
@@ -967,29 +1055,58 @@
     own_group.start()
     lax.fori_loop(1, n * m, start_wide, 0)
     lax.fori_loop(1, m, start_group, 0)
+    copies = return_copies(n, sizes, narrows, wides, back_local, back_send, back_recv)
+    for copy in copies:
+        copy.start()
     own.wait()
     own_group.wait()
     lax.fori_loop(1, n * m, wait_wide, 0)
     lax.fori_loop(1, m, wait_group, 0)
-
-
-def collect(n, m, wide, group, number):
+    for copy in copies:
+        copy.wait()
+
+
+def collect(n, m, wide, group, narrows, sizes, number):
     inside = pl.BlockSpec(memory_space=pltpu.VMEM)
+    anywhere = pl.BlockSpec(memory_space=pl.ANY)
+    rows = narrows[0].shape[1]
+    total = sum(groups for groups, width in sizes)
+    outs = [jax.ShapeDtypeStruct(wide.shape, wide.dtype), jax.ShapeDtypeStruct(group.shape, group.dtype)]
+    outs += [jax.ShapeDtypeStruct((rows, groups * width * n), jnp.bfloat16) for groups, width in sizes]
     return pl.pallas_call(
-        functools.partial(collect_kernel, n, m),
-        out_shape=[jax.ShapeDtypeStruct(wide.shape, wide.dtype), jax.ShapeDtypeStruct(group.shape, group.dtype)],
-        in_specs=[inside] * 2,
-        out_specs=[inside] * 2,
+        functools.partial(collect_kernel, n, m, sizes),
+        out_shape=outs,
+        in_specs=[inside] * 2 + [anywhere] * len(sizes),
+        out_specs=[inside] * 2 + [anywhere] * len(sizes),
         scratch_shapes=[
             pltpu.SemaphoreType.DMA((2,)),
             pltpu.SemaphoreType.DMA((n * m,)),
             pltpu.SemaphoreType.DMA((n * m,)),
             pltpu.SemaphoreType.DMA((m,)),
             pltpu.SemaphoreType.DMA((m,)),
+            pltpu.SemaphoreType.DMA((total,)),
+            pltpu.SemaphoreType.DMA((n - 1, total)),
+            pltpu.SemaphoreType.DMA((n - 1, total)),
         ],
         compiler_params=pltpu.CompilerParams(collective_id=number, has_side_effects=True),
         name="collect",
-    )(wide, group)
+    )(wide, group, *narrows)
+
+
+def keep_kernel(first, second, first_out, second_out):
+    first_out[...] = first[...]
+    second_out[...] = second[...]
+
+
+def keep(first, second):
+    inside = pl.BlockSpec(memory_space=pltpu.VMEM)
+    return pl.pallas_call(
+        keep_kernel,
+        out_shape=[jax.ShapeDtypeStruct(value.shape, value.dtype) for value in (first, second)],
+        in_specs=[inside] * 2,
+        out_specs=[inside] * 2,
+        name="keep",
+    )(first, second)
 
 
 def unit_of(values):
@@ -1547,26 +1664,23 @@
         late_drop, final_gain, final_shift,
     ]
     spans = hidden * n // D
-    w_early_down = gather_rows(early_down)
     (
-        w_early_up, late_up_split, mixer_split, filter_split, small_all, vectors, depth_all, segments_all, early_hidden
+        w_early_up, w_early_down, late_up_split, mixer_split, filter_split, small_all, vectors, own_vectors, lifts,
+        filter_lifts, depth_all, segments_all, early_hidden,
     ) = exchange(
-        n, m, early_up, late_up, mixer_project, filter_up, mixer_output, filter_down, depth_weight,
-        segments.reshape(1, frame_count), frames, singles, [early_lift, late_lift, filter_lift], distance_table,
+        n, m, early_up, early_down.reshape(spans, rows, D), late_up, mixer_project, filter_up, mixer_output,
+        filter_down, depth_weight, segments.reshape(1, frame_count), frames, singles,
+        [early_lift, late_lift, filter_lift], distance_table,
     )
     w_early_up = w_early_up.reshape(D, hidden)
+    w_early_down = w_early_down.reshape(hidden, D)
     w_mixer = lax.all_gather(mixer_split, "fsdp", axis=1, tiled=True)
     w_filter = lax.all_gather(filter_split, "fsdp", axis=1, tiled=True)
     w_late_up = gather_split(late_up_split)
     w_late_down = gather_rows(late_down)
 
-    lines = -(-len(singles) * rows // LANES)
-    own_vectors = lax.dynamic_slice(vectors, (0, me * inner), (vectors.shape[0], inner))
-    own_lifts = lax.dynamic_slice(small_all, (me * m, lines, 0), (m, 2, LANES))
-    early_lifts, late_lifts = own_lifts[:, 0].reshape(-1), own_lifts[:, 1].reshape(-1)
-    filter_lifts = small_all[:, lines + 2, : 2 * D // (n * m)].reshape(2, D)
-    filter_lifts = lax.dynamic_slice(filter_lifts, (0, me * inner), (2, inner)).reshape(2 * inner)
-    table = small_all[:, 8 : 8 + distance_table.shape[0], :HEADS].reshape(NREL, HEADS)
+    early_lifts, late_lifts = lifts[0], lifts[1]
+    table = small_all[:, 8 : 8 + distance_table.shape[0], :HEADS].astype(jnp.float32).reshape(NREL, HEADS)
     table = jnp.transpose(lax.dynamic_slice(table, (0, me * heads), (NREL, heads)))[:, ::-1]
     taps = jnp.transpose(depth_all.reshape(inner, KW)).astype(jnp.float32)
     attention_shift = jnp.concatenate([own_vectors[5], jnp.zeros((inner,), jnp.float32), own_vectors[6]])
@@ -1729,19 +1843,15 @@
     group = jnp.transpose(group.reshape(group_count, m, rows), (1, 0, 2)).reshape(m, group_count * rows)
     group_used = group.shape[1]
     group = jnp.pad(group, ((0, 0), (0, -group_used % LANES))).reshape(m, -1, LANES)
-    wide_all, group_all = collect(n, m, wide, group, 12)
-    wide_all, mixer_slope = lax.optimization_barrier((wide_all, mixer_slope))
+    wide_all, group_all, late_up_wide, project_wide, filter_up_wide = collect(
+        n, m, wide, group, [late_slope, mixer_slope, filter_slope], [(1, hidden), (3, inner), (2, inner)], 12
+    )
     tables = wide_all.reshape(n, m, -1)[:, :, wide_count * rows : table_used]
     wide = jnp.sum(wide_all, axis=0).reshape(-1)
     lift_total = wide[table_used:wide_used]
     wide = wide[: wide_count * rows].reshape(wide_count, rows)
     tables = jnp.transpose(jnp.sum(tables, axis=1).reshape(HEADS, table_rows))
     group = jnp.sum(group_all, axis=0).reshape(-1)[:group_used].reshape(group_count, rows)
-    late_up_wide, project_wide, filter_up_wide = giveback(
-        n, [late_slope, mixer_slope, filter_slope], [(1, hidden), (3, inner), (2, inner)], 13
-    )
-    (early_up_wide,) = giveback(n, [early_slope], [(1, hidden)], 14)
-
     def rejoin(value, low):
         return final(jnp.transpose(value[:, :, low:], (1, 0, 2)).reshape(rows, D))
 
@@ -1749,14 +1859,12 @@
         return value.astype(jnp.float32)
 
     lift_slopes = KW + 5
-    return (
+    results = [
         layer_out,
         slope_frames,
         wide[12],
         wide[13],
-        final(early_up_wide),
         jnp.transpose(group[lift_slopes : lift_slopes + spans]).reshape(-1),
-        final(early_slope[n:]).reshape(spans * rows, D),
         wide[11],
         wide[9],
         wide[10],
@@ -1784,7 +1892,13 @@
         wide[2],
         wide[0],
         wide[1],
-    )
+    ]
+    results[:2] = keep(layer_out, slope_frames)
+    *results, early_slope = lax.optimization_barrier((*results, early_slope))
+    (early_up_wide,) = giveback(n, [early_slope], [(1, hidden)], 14)
+    results.insert(4, final(early_up_wide))
+    results.insert(6, final(early_slope[n:]).reshape(spans * rows, D))
+    return tuple(results)
 
 
 def solution(mesh):

time: 449 us -> 434 us (0.967)
  Pallas kernels: 312 us -> 298 us
    pallas_call x2 -> x1, Pallas kernels: 17.4 us -> 6.48 us  [giveback(): pl.pallas_call(functools.partial(giveback_kernel, n, sizes), out_shape=ou...]
    pallas_call x1, Pallas kernels: 58.8 us -> 51.8 us  [exchange(): pl.pallas_call(functools.partial(exchange_kernel, n, m, width, inner), ou...]
    pallas_call x1 -> x2, Pallas kernels: 13.3 us -> 19.2 us  [the longest x1 17 us: collect(): pl.pallas_call(functools.partial(collect_kernel, n, m, sizes), out_shape=...]
  transfers between devices with their start and end apart: 9 -> 8, of which waited for: 0 -> 0; matrix products, arithmetic and copies ran while one was open for 20% -> 20% of each run, Pallas kernels for 64% -> 51%
where the time goes in v4:
time: 434 us; the launch traced here: 429 us
  Pallas kernels  298 us (69%)
  matrix products  54.2 us (12%)
  local copies, waits for them, and re-layouts  30.2 us (7%)
  other arithmetic  28.5 us (7%)
  between operations  15.2 us (4%)
    pallas_call x8, Pallas kernels, boundary(): pl.pallas_call(functools.partial(boundary_kernel, step, shape), out_shape...  175 us
    pallas_call x1, Pallas kernels, exchange(): pl.pallas_call(functools.partial(exchange_kernel, n, m, width, inner), ou...  51.8 us
    dot_general x8, matrix products, flat_dot(): return jnp.dot(left_rows, right_rows, preferred_element_type=jnp.float32)  23.4 us
    dot_general x8, matrix products, back_dot(): lax.dot_general(left_rows, right_rows, (((1,), (1,)), ((), ())), preferre...  20.4 us
    pallas_call x1, Pallas kernels, collect(): pl.pallas_call(functools.partial(collect_kernel, n, m, sizes), out_shape=...  17 us
    pallas_call x1, Pallas kernels, unattend(): pl.pallas_call(functools.partial(unattend_kernel, heads), grid=(blocks,),...  12 us
    pallas_call x2, Pallas kernels, share(): pl.pallas_call(functools.partial(share_kernel, n), out_shape=jax.ShapeDty...  11.8 us
    dot_general x8, matrix products, lead_dot(): lax.dot_general(left_rows, right_rows, (((0,), (0,)), ((), ())), preferre...  10.3 us
  transfers between devices with their start and end apart: 8, of which 0 were waited for; matrix products, arithmetic and copies ran while one was open for 20% of the time, Pallas kernels for 51%

profile of v4, /device:TPU:0, one launch (start us, length us, event | category | flops | bytes accessed | tf_op | source)
XLA Modules:
  0.0 429.1 jit_solution(10485287609436257580)
XLA Ops:
  7.3 51.8 %exchange.1 = (bf16[32,32,1024]{2,1,0:T(8,128)(2,1)}, bf16[8,4,32,1024]{3,2,1,0:T(8,128)(2,1)}, bf16[4,32,1024]{2,1,0:T(8,128)(2,1)}, bf16[4,32,1024]{2,1,0:T(8,...) custom-call(bf16[32,4096]{1,0:T(8,128)(2,1)} %refs_0_.1, ...), custom_call_target="tpu_custom_call" | custom-call | tf_op jit(solution)/shard_map/exchange/pallas_call | solution.py:908
  65.0 4.6 %fusion.14 = f32[512,1024]{1,0:T(8,128)} fusion(bf16[512,1024]{1,0:T(8,128)(2,1)} %bitcast.275, bf16[1024,1024]{1,0:T(8,128)(2,1)} %bitcast.269), kind=kOutput, calls=%fused_computation.92 | convolution fusion | flops 1073741824 | bytes 5242880 | tf_op jit(solution)/shard_map/dot_general | solution.py:29
  69.6 4.6 %convolution_convert_fusion.10 = bf16[512,1024]{1,0:T(8,128)(2,1)} fusion(bf16[1024,1024]{1,0:T(8,128)(2,1)} %bitcast.271, f32[512,1024]{1,0:T(8,128)} %fusion.14, f32[1024]{0:T(1024)S(1)} %bitcast.260), kind=kOutput, calls=%fused_computation.23 | convolution fusion | flops 1077411840 | bytes 5246976 | tf_op jit(solution)/shard_map/dot_general | solution.py:29
  76.9 25.6 %boundary.8 = (f32[128,1024]{1,0:T(8,128)}, bf16[4,128,1024]{2,1,0:T(8,128)(2,1)}) custom-call(bf16[4,128,1024]{2,1,0:T(8,128)(2,1)} %bitcast.225, bf16[128,1024]{1,0:T(8,128)(2,1)} %refs_2_.5, f32[19,1024]{1,0:T(8,128)} %get-tuple-element.139.refs_2_.refs_3_), custom_call_target="tpu_custom_call" | custom-call | tf_op jit(solution)/shard_map/boundary/pallas_call | solution.py:1331
  108.0 3.1 add_convert_fusion
  111.1 8.1 %attend.1 = bf16[4,128,256]{2,1,0:T(8,128)(2,1)} custom-call(bf16[4,128,768]{2,1,0:T(8,128)(2,1)} %bitcast.198, s32[4,1,128]{2,1,0:T(1,128)} %get-tuple-element.145.segment_rows, s32[4,128,1]{2,1,0:T(8,128)} %copy.118.segment_columns, f32[4,256]{1,0:T(4,128)} %rev.4.table), custom_call_target="tpu_custom_call" | custom-call | tf_op jit(solution)/shard_map/attend/pallas_call | solution.py:1378
  119.2 2.4 convolution_convert_fusion.9
  121.6 24.0 %boundary.9 = (f32[128,1024]{1,0:T(8,128)}, bf16[4,128,1024]{2,1,0:T(8,128)(2,1)}) custom-call(bf16[4,128,1024]{2,1,0:T(8,128)(2,1)} %bitcast.194, f32[128,1024]{1,0:T(8,128)} %get-tuple-element.147.refs_1_.refs_2_, f32[19,1024]{1,0:T(8,128)} %get-tuple-element.139.refs_2_.refs_3_), custom_call_target="tpu_custom_call" | custom-call | tf_op jit(solution)/shard_map/boundary/pallas_call | solution.py:1331
  149.7 5.0 %convolve.1 = (f32[4,128,256]{2,1,0:T(8,128)}, f32[4,128,256]{2,1,0:T(8,128)}) custom-call(f32[4,128,512]{2,1,0:T(8,128)} %bitcast.196, s32[4,128,1]{2,1,0:T(8,128)} %get-tuple-element.384.behind, s32[4,128,1]{2,1,0:T(8,128)} %get-tuple-element.383.ahead, f32[31,256]{1,0:T(8,128)} %bitcast.233, f32[1,256]{1,0:T(1,128)} %get-tuple-element.355.bias), custom_call_target="tpu_custom_call" | custom-call | tf_op jit(solution)/shard_map/convolve/pallas_call | solution.py:1506
  157.9 5.9 %share.2 = f32[4,8,128]{2,1,0:T(8,128)} custom-call(f32[8,128]{1,0:T(8,128)} %pad_maximum_fusion.5.mine), custom_call_target="tpu_custom_call" | custom-call | tf_op jit(solution)/shard_map/share/pallas_call | solution.py:1001
  166.9 24.1 %boundary.10 = (f32[128,1024]{1,0:T(8,128)}, bf16[4,128,1024]{2,1,0:T(8,128)(2,1)}) custom-call(bf16[4,128,1024]{2,1,0:T(8,128)(2,1)} %bitcast.195, f32[128,1024]{1,0:T(8,128)} %get-tuple-element.155.refs_1_.refs_2_, f32[19,1024]{1,0:T(8,128)} %get-tuple-element.139.refs_2_.refs_3_), custom_call_target="tpu_custom_call" | custom-call | tf_op jit(solution)/shard_map/boundary/pallas_call | solution.py:1331
  191.0 3.3 fusion.15
  194.4 2.3 convolution_convert_fusion.7
  196.7 22.7 %boundary.11 = (f32[128,1024]{1,0:T(8,128)}, f32[128,1024]{1,0:T(8,128)}, bf16[4,128,1024]{2,1,0:T(8,128)(2,1)}, f32[3,1024]{1,0:T(4,128)}) custom-call(bf16[4,128,1024]{2,1,0:T(8,128)(2,1)} %bitcast.229, f32[128,1024]{1,0:T(8,128)} %get-tuple-element.161.refs_1_.refs_2_, bf16[128,1024]{1,0:T(8,128)(2,1)} %refs_2_.4, ...), custom_call_target="tpu_custom_call" | custom-call | tf_op jit(solution)/shard_map/boundary/pallas_call | solution.py:1331
  219.3 4.4 %fusion.13 = (f32[1024]{0:T(1024)S(1)}, bf16[512,1024]{1,0:T(8,128)(2,1)S(1)}) fusion(f32[512,1024]{1,0:T(8,128)} %copy-done.36, f32[1024]{0:T(1024)S(1)} %bitcast.264, bf16[512,1024]{1,0:T(8,128)(2,1)} %bitcast.283, bf16[1024,1024]{1,0:T(8,128)(2,1)} %all-gather.11.cloned.1.call-done), kind=kOutput, calls=%fused_computation.91 | convolution fusion | flops 1079507968 | bytes 6299648 | tf_op jit(solution)/shard_map/dot_general | solution.py:39
  225.4 2.3 convolution_convert_fusion.6
  229.1 2.3 pad_maximum_fusion
  231.5 22.0 %boundary.12 = (f32[128,1024]{1,0:T(8,128)}, bf16[4,128,1024]{2,1,0:T(8,128)(2,1)}, f32[3,1024]{1,0:T(4,128)}) custom-call(bf16[4,128,1024]{2,1,0:T(8,128)(2,1)} %bitcast.223, f32[128,1024]{1,0:T(8,128)} %get-tuple-element.166.refs_1_, f32[128,1024]{1,0:T(8,128)} %get-tuple-element.161.refs_1_.refs_2_, f32[19,1024]{1,0:T(8,128)} %get-tuple-element.139.refs_2_.refs_3_), custom_call_target="tpu_custom_call" | custom-call | tf_op jit(solution)/shard_map/boundary/pallas_call | solution.py:1331
  253.7 2.1 multiply_reduce_fusion
  256.4 5.9 %share.3 = f32[4,8,128]{2,1,0:T(8,128)} custom-call(f32[8,128]{1,0:T(8,128)} %pad_maximum_fusion.6.mine), custom_call_target="tpu_custom_call" | custom-call | tf_op jit(solution)/shard_map/share/pallas_call | solution.py:1001
  265.1 8.9 %unconvolve.1 = (bf16[4,128,512]{2,1,0:T(8,128)(2,1)}, f32[1,512]{1,0:T(1,128)}, f32[32,256]{1,0:T(8,128)}) custom-call(f32[4,128,512]{2,1,0:T(8,128)} %bitcast.197, f32[4,128,256]{2,1,0:T(8,128)} %get-tuple-element.163.gated, f32[4,128,256]{2,1,0:T(8,128)} %bitcast.213, s32[4,128,1]{2,1,0:T(8,128)} %get-tuple-element.384.behind, ...), custom_call_target="tpu_custom_call" | custom-call | tf_op jit(solution)/shard_map/unconvolve/pallas_call | solution.py:1568
  279.7 22.0 %boundary.13 = (f32[128,1024]{1,0:T(8,128)}, bf16[4,128,1024]{2,1,0:T(8,128)(2,1)}, f32[3,1024]{1,0:T(4,128)}) custom-call(bf16[4,128,1024]{2,1,0:T(8,128)(2,1)} %bitcast.226, f32[128,1024]{1,0:T(8,128)} %get-tuple-element.170.refs_1_, f32[128,1024]{1,0:T(8,128)} %get-tuple-element.155.refs_1_.refs_2_, f32[19,1024]{1,0:T(8,128)} %get-tuple-element.139.refs_2_.refs_3_), custom_call_target="tpu_custom_call" | custom-call | tf_op jit(solution)/shard_map/boundary/pallas_call | solution.py:1331
  301.8 2.5 convolution_convert_fusion.12
  304.3 12.0 %unattend.1 = (bf16[4,128,768]{2,1,0:T(8,128)(2,1)}, f32[2,256]{1,0:T(2,128)}, f32[4,256]{1,0:T(4,128)}) custom-call(bf16[4,128,768]{2,1,0:T(8,128)(2,1)} %bitcast.199, bf16[4,128,256]{2,1,0:T(8,128)(2,1)} %bitcast.236, s32[4,1,128]{2,1,0:T(1,128)} %get-tuple-element.145.segment_rows, s32[4,128,1]{2,1,0:T(8,128)} %copy.118.segment_columns, f32[4,256]{1,0:T(4,128)} %rev.4.table), custom_call_target="tpu_custom_call" | custom-call | tf_op jit(solution)/shard_map/unattend/pallas_call | solution.py:1446
  323.4 22.3 %boundary.14 = (f32[128,1024]{1,0:T(8,128)}, bf16[4,128,1024]{2,1,0:T(8,128)(2,1)}, f32[3,1024]{1,0:T(4,128)}) custom-call(bf16[4,128,1024]{2,1,0:T(8,128)(2,1)} %bitcast.224, f32[128,1024]{1,0:T(8,128)} %get-tuple-element.175.refs_1_, f32[128,1024]{1,0:T(8,128)} %get-tuple-element.147.refs_1_.refs_2_, f32[19,1024]{1,0:T(8,128)} %get-tuple-element.139.refs_2_.refs_3_), custom_call_target="tpu_custom_call" | custom-call | tf_op jit(solution)/shard_map/boundary/pallas_call | solution.py:1331
  345.7 2.7 convolution_convert_fusion
  353.5 2.3 pad_maximum_fusion.1
  355.8 3.6 convolution_convert_fusion.5
  362.2 12.4 %boundary.15 = (f32[128,1024]{1,0:T(8,128)}, f32[2,1024]{1,0:T(2,128)}) custom-call(bf16[4,128,1024]{2,1,0:T(8,128)(2,1)} %bitcast.228, f32[128,1024]{1,0:T(8,128)} %get-tuple-element.181.refs_1_, bf16[128,1024]{1,0:T(8,128)(2,1)} %refs_2_.5, f32[19,1024]{1,0:T(8,128)} %get-tuple-element.139.refs_2_.refs_3_), custom_call_target="tpu_custom_call" | custom-call | tf_op jit(solution)/shard_map/boundary/pallas_call | solution.py:1331
  379.5 2.2 keep.1
  382.5 17.0 %collect.1 = (f32[32,5,128]{2,1,0:T(8,128)}, f32[8,11,128]{2,1,0:T(8,128)}, bf16[32,4096]{1,0:T(8,128)(2,1)}, bf16[32,3072]{1,0:T(8,128)(2,1)}, bf16[32,2048]{1,0:T(8,128)(2,1)}) custom-call(f32[32,5,128]{2,1,0:T(8,128)} %reshape.509.refs_0_, f32[8,11,128]{2,1,0:T(8,128)} %reshape.512.refs_1_, bf16[8,32,1024]{2,1,0:T(8,128)(2,1)} %reduce-scatter.5.cloned.1.call-done.refs_2_, ...), custom_call_target="tpu_custom_call" | custom-call | tf_op jit(solution)/shard_map/collect/pallas_call | solution.py:1076
  411.6 6.5 %giveback.1 = bf16[32,4096]{1,0:T(8,128)(2,1)} custom-call(bf16[8,32,1024]{2,1,0:T(8,128)(2,1)} %reduce-scatter.11.cloned.1.call-done.refs_0_), custom_call_target="tpu_custom_call" | custom-call | tf_op jit(solution)/shard_map/giveback/pallas_call | solution.py:971
  (224 shorter events, 73.2 us)
Async XLA Ops:
  7.2 97.5 %all-gather.5.cloned.1.call-start = ((), (), s32[]{:S(2)}) async-start(), calls=%async_computation.4 | async-start | bytes 2359296 | tf_op jit(solution)/shard_map/all_gather | solution.py:1677
  59.1 86.5 %all-gather.7.cloned.1.call-start = ((), (), s32[]{:S(2)}) async-start(), calls=%async_computation.5 | async-start | bytes 1769472 | tf_op jit(solution)/shard_map/all_gather | solution.py:1678
  59.9 131.1 %all-gather.9.cloned.1.call-start = ((), (), s32[]{:S(2)}) async-start(), calls=%async_computation.6 | async-start | bytes 2359296 | tf_op jit(solution)/shard_map/all_gather | solution.py:1592
  60.6 130.4 %all-gather.11.cloned.1.call-start = ((), (), s32[]{:S(2)}) async-start(), calls=%async_computation.7 | async-start | bytes 2359296 | tf_op jit(solution)/shard_map/all_gather | solution.py:1588
  61.2 262.2 %reduce-scatter.5.cloned.1.call-start = ((), (), s32[]{:S(2)}) async-start(), calls=%async_computation.8 | async-start | bytes 4718592 | tf_op jit(solution)/shard_map/reduce_scatter | solution.py:1759
  69.6 4.7 %copy-start.10 = (s32[4,1,128]{2,1,0:T(1,128)S(1)}, s32[4,1,128]{2,1,0:T(1,128)}, u32[]{:S(2)}) copy-start(s32[4,1,128]{2,1,0:T(1,128)} %get-tuple-element.145.segment_rows) | copy-start | bytes 6148
  106.3 4.8 %copy-start.2 = (bf16[4,256,768]{2,1,0:T(8,128)(2,1)}, bf16[4,256,768]{2,1,0:T(8,128)(2,1)S(1)}, u32[]{:S(2)}) copy-start(bf16[4,256,768]{2,1,0:T(8,128)(2,1)S(1)} %slice.183) | copy-start | bytes 4718596
  121.6 26.4 %copy-start.33 = (f32[1,512]{1,0:T(1,128)S(1)}, f32[1,512]{1,0:T(1,128)}, u32[]{:S(2)}) copy-start(f32[1,512]{1,0:T(1,128)} %get-tuple-element.152) | copy-start | bytes 6148
  145.6 2.4 copy-start.25
  154.7 10.5 %copy-start = (f32[4,128,256]{2,1,0:T(8,128)S(1)}, f32[4,128,256]{2,1,0:T(8,128)}, u32[]{:S(2)}) copy-start(f32[4,128,256]{2,1,0:T(8,128)} %get-tuple-element.154) | copy-start | bytes 1572868
  191.0 3.3 copy-start.22
  219.3 4.5 %copy-start.29 = (bf16[4,128,1024]{2,1,0:T(8,128)(2,1)S(1)}, bf16[4,128,1024]{2,1,0:T(8,128)(2,1)}, u32[]{:S(2)}) copy-start(bf16[4,128,1024]{2,1,0:T(8,128)(2,1)} %get-tuple-element.164) | copy-start | bytes 3145732
  219.3 4.5 %copy-start.37 = (f32[512,1024]{1,0:T(8,128)S(1)}, f32[512,1024]{1,0:T(8,128)}, u32[]{:S(2)}) copy-start(f32[512,1024]{1,0:T(8,128)} %copy-done.36) | copy-start | bytes 6291460
  231.5 127.9 %reduce-scatter.7.cloned.1.call-start = ((), (), s32[]{:S(2)}) async-start(), calls=%async_computation.9 | async-start | bytes 1769472 | tf_op jit(solution)/shard_map/reduce_scatter | solution.py:1790
  253.7 9.3 %copy-start.4 = (bf16[4,128,1024]{2,1,0:T(8,128)(2,1)S(1)}, bf16[4,128,1024]{2,1,0:T(8,128)(2,1)}, u32[]{:S(2)}) copy-start(bf16[4,128,1024]{2,1,0:T(8,128)(2,1)} %get-tuple-element.167) | copy-start | bytes 3145732
  264.0 10.1 %copy-start.26 = (bf16[4,128,1024]{2,1,0:T(8,128)(2,1)S(1)}, bf16[4,128,1024]{2,1,0:T(8,128)(2,1)}, u32[]{:S(2)}) copy-start(bf16[4,128,1024]{2,1,0:T(8,128)(2,1)} %get-tuple-element.150) | copy-start | bytes 3145732
  279.5 103.0 %reduce-scatter.9.cloned.1.call-start = ((), (), s32[]{:S(2)}) async-start(), calls=%async_computation.10 | async-start | bytes 2359296 | tf_op jit(solution)/shard_map/reduce_scatter | solution.py:1804
  301.8 14.5 %copy-start.1 = (bf16[4,128,256]{2,1,0:T(8,128)(2,1)S(1)}, bf16[4,128,256]{2,1,0:T(8,128)(2,1)}, u32[]{:S(2)}) copy-start(bf16[4,128,256]{2,1,0:T(8,128)(2,1)} %attend.1) | copy-start | bytes 786436
  301.8 14.5 %copy-start.5 = (bf16[4,128,1024]{2,1,0:T(8,128)(2,1)S(1)}, bf16[4,128,1024]{2,1,0:T(8,128)(2,1)}, u32[]{:S(2)}) copy-start(bf16[4,128,1024]{2,1,0:T(8,128)(2,1)} %get-tuple-element.171) | copy-start | bytes 3145732
  318.9 2.4 copy-start.31
  323.4 22.4 %copy-start.34 = (f32[512,1024]{1,0:T(8,128)S(1)}, f32[512,1024]{1,0:T(8,128)}, u32[]{:S(2)}) copy-start(f32[512,1024]{1,0:T(8,128)} %fusion.14) | copy-start | bytes 6291460
  323.4 88.2 %reduce-scatter.11.cloned.1.call-start = ((), (), s32[]{:S(2)}) async-start(), calls=%async_computation.11 | async-start | bytes 4718592 | tf_op jit(solution)/shard_map/reduce_scatter | solution.py:1812
  345.7 2.9 copy-start.35
  353.5 2.3 copy-start.19
  359.3 2.5 copy-start.11
  359.4 15.3 %copy-start.12 = (f32[3,1024]{1,0:T(4,128)S(1)}, f32[3,1024]{1,0:T(4,128)}, u32[]{:S(2)}) copy-start(f32[3,1024]{1,0:T(4,128)} %get-tuple-element.185) | copy-start | bytes 36868
  359.4 15.3 %copy-start.13 = (f32[3,1024]{1,0:T(4,128)S(1)}, f32[3,1024]{1,0:T(4,128)}, u32[]{:S(2)}) copy-start(f32[3,1024]{1,0:T(4,128)} %get-tuple-element.186) | copy-start | bytes 36868
  359.4 15.3 %copy-start.14 = (f32[3,1024]{1,0:T(4,128)S(1)}, f32[3,1024]{1,0:T(4,128)}, u32[]{:S(2)}) copy-start(f32[3,1024]{1,0:T(4,128)} %get-tuple-element.187) | copy-start | bytes 36868
  359.4 15.3 %copy-start.15 = (f32[3,1024]{1,0:T(4,128)S(1)}, f32[3,1024]{1,0:T(4,128)}, u32[]{:S(2)}) copy-start(f32[3,1024]{1,0:T(4,128)} %get-tuple-element.188) | copy-start | bytes 36868
  375.7 6.0 %slice-start.1 = ((bf16[8,32,1024]{2,1,0:T(8,128)(2,1)}), bf16[4,32,1024]{2,1,0:T(8,128)(2,1)S(1)}, s32[]{:S(2)}) async-start(bf16[8,32,1024]{2,1,0:T(8,128)(2,1)} %reduce-scatter.5.cloned.1.call-done.refs_2_), calls=%async_computation.13 | async-start | bytes 524288 | tf_op jit(solution)/shard_map/slice | solution.py:1891
  399.5 9.3 %copy-start.8 = (bf16[32,4096]{1,0:T(8,128)(2,1)S(1)}, bf16[32,4096]{1,0:T(8,128)(2,1)}, u32[]{:S(2)}) copy-start(bf16[32,4096]{1,0:T(8,128)(2,1)} %get-tuple-element.201) | copy-start | bytes 786436
  411.6 8.3 %slice-start = ((bf16[8,32,1024]{2,1,0:T(8,128)(2,1)}), bf16[4,32,1024]{2,1,0:T(8,128)(2,1)S(1)}, s32[]{:S(2)}) async-start(bf16[8,32,1024]{2,1,0:T(8,128)(2,1)} %reduce-scatter.11.cloned.1.call-done.refs_0_), calls=%async_computation.12 | async-start | bytes 524288 | tf_op jit(solution)/shard_map/slice | solution.py:1900
  (17 other events, 27.3 us)
Sparse Core Ops, SparseCore 0:
  59.2 27.0 all-gather.4
  88.0 24.6 all-gather.6
  114.3 28.2 all-gather.8
  144.1 28.5 all-gather.10
  231.6 48.0 reduce-scatter.4
  281.8 32.7 reduce-scatter.6
  323.5 34.2 reduce-scatter.8
  360.1 50.7 reduce-scatter.10

commit v5 on v4

--- a/solution.py
+++ b/solution.py
@@ -983,36 +983,6 @@
     )(*narrows)
 
 
-def share_kernel(n, mine, shared, local, send, recv):
-    me = lax.axis_index("dp")
-    others = near(me, n)
-    greet([target for target, unused in others])
-    copies = [pltpu.make_async_copy(mine, shared.at[me], local)]
-    for peer, (target, unused) in enumerate(others):
-        copies.append(remote(mine, shared.at[me], send.at[peer], recv.at[peer], {"dp": target}))
-    for copy in copies:
-        copy.start()
-    for copy in copies:
-        copy.wait()
-
-
-def share(n, mine, number):
-    inside = pl.BlockSpec(memory_space=pltpu.VMEM)
-    return pl.pallas_call(
-        functools.partial(share_kernel, n),
-        out_shape=jax.ShapeDtypeStruct((n,) + mine.shape, mine.dtype),
-        in_specs=[inside],
-        out_specs=inside,
-        scratch_shapes=[
-            pltpu.SemaphoreType.DMA,
-            pltpu.SemaphoreType.DMA((n - 1,)),
-            pltpu.SemaphoreType.DMA((n - 1,)),
-        ],
-        compiler_params=pltpu.CompilerParams(collective_id=number, has_side_effects=True),
-        name="share",
-    )(mine)
-
-
 def collect_kernel(n, m, sizes, *refs):
     count = len(sizes)
     wide, group = refs[:2]
@@ -1477,111 +1447,186 @@
     return ahead >= offset
 
 
-def convolve_kernel(opened, behind, ahead, taps, bias, gated, filtered, padded):
+def to_rows(wide, count):
+    return jnp.transpose(wide)[:count]
+
+
+def to_columns(rows):
+    count, length = rows.shape
+    wide = jnp.transpose(jnp.concatenate([rows, jnp.zeros((LANES - count, length), rows.dtype)]))
+    return [wide[:, at : at + 1] for at in range(count)]
+
+
+def swap(n, mine, shared, send, recv):
+    me = lax.axis_index("dp")
+    shared[me] = mine[...]
+    copies = []
+    for peer, (target, unused) in enumerate(near(me, n)):
+        copies.append(remote(mine, shared.at[me], send.at[peer], recv.at[peer], {"dp": target}))
+    for copy in copies:
+        copy.start()
+    for copy in copies:
+        copy.wait()
+
+
+def fill(store, value):
+    frame_count, channels = value.shape
+    store[pl.ds(0, MARGIN), :] = jnp.zeros((MARGIN, channels), jnp.float32)
+    store[pl.ds(MARGIN + frame_count, MARGIN), :] = jnp.zeros((MARGIN, channels), jnp.float32)
+    store[pl.ds(MARGIN, frame_count), :] = value
+
+
+def convolve_kernel(
+    n, opened, behind, ahead, taps, vectors, gated, unit, inverse, swished, padded, mine, shared, send, recv
+):
     frame_count, channels = gated.shape[1:]
-    gates = opened[0, :, 0:channels] * jax.nn.sigmoid(opened[0, :, channels:])
-    gated[0] = gates
-    padded[pl.ds(0, MARGIN), :] = jnp.zeros((MARGIN, channels), jnp.float32)
-    padded[pl.ds(MARGIN + frame_count, MARGIN), :] = jnp.zeros((MARGIN, channels), jnp.float32)
-    padded[pl.ds(MARGIN, frame_count), :] = gates
-    back = jnp.broadcast_to(behind[0], (frame_count, LANES))
-    front = jnp.broadcast_to(ahead[0], (frame_count, LANES))
-    for low in range(0, channels, LANES):
-        lanes = slice(low, low + LANES)
-        running = jnp.broadcast_to(bias[:, lanes], (frame_count, LANES))
-        for tap in range(KW):
-            offset = tap - (KW - 1) // 2
-            moved = padded[pl.ds(MARGIN + offset, frame_count), lanes]
-            if offset:
-                moved = jnp.where(reach_mask(offset, back, front), moved, 0.0)
-            running = running + moved * taps[pl.ds(tap, 1), lanes]
-        filtered[0, :, lanes] = running
-
-
-def convolve(opened, behind, ahead, taps, bias):
+    greet([target for target, unused in near(lax.axis_index("dp"), n)])
+    places = lax.broadcasted_iota(jnp.int32, (frame_count, LANES), 1)
+
+    def filter_block(block, wide):
+        gates = opened[block, :, 0:channels] * jax.nn.sigmoid(opened[block, :, channels:])
+        gated[block] = gates
+        fill(padded, gates)
+        back = jnp.broadcast_to(behind[block], (frame_count, LANES))
+        front = jnp.broadcast_to(ahead[block], (frame_count, LANES))
+        for low in range(0, channels, LANES):
+            lanes = slice(low, low + LANES)
+            running = jnp.broadcast_to(vectors[10:11, lanes], (frame_count, LANES))
+            for tap in range(KW):
+                offset = tap - (KW - 1) // 2
+                moved = padded[pl.ds(MARGIN + offset, frame_count), lanes]
+                if offset:
+                    moved = jnp.where(reach_mask(offset, back, front), moved, 0.0)
+                running = running + moved * taps[pl.ds(tap, 1), lanes]
+            unit[block, :, lanes] = running
+        filtered = unit[block]
+        mean = jnp.mean(filtered, axis=-1, keepdims=True)
+        square = jnp.sum((filtered - mean) ** 2, axis=-1, keepdims=True)
+        return jnp.where(places == block, mean, jnp.where(places == n + block, square, wide))
+
+    wide = lax.fori_loop(0, n, filter_block, jnp.zeros((frame_count, LANES), jnp.float32))
+    mine[...] = to_rows(wide, 2 * n)
+    swap(n, mine, shared, send, recv)
+    everyone = [shared[at] for at in range(n)]
+    middle_mean = sum(rows[:n] for rows in everyone) / n
+    total = sum(rows[n:] + channels * (rows[:n] - middle_mean) ** 2 for rows in everyone)
+    scale = lax.rsqrt(total / (n * channels) + EPSILON)
+    found = to_columns(jnp.concatenate([middle_mean, scale]))
+    for block in range(n):
+        values = (unit[block] - found[block]) * found[n + block]
+        unit[block] = values
+        inverse[block] = found[n + block]
+        middle = values * vectors[11:12, :] + vectors[12:13, :]
+        swished[block] = (middle * jax.nn.sigmoid(middle)).astype(jnp.bfloat16)
+
+
+def swap_scratch(n, frame_count):
+    return [
+        pltpu.VMEM((2 * n, frame_count), jnp.float32),
+        pltpu.VMEM((n, 2 * n, frame_count), jnp.float32),
+        pltpu.SemaphoreType.DMA((n - 1,)),
+        pltpu.SemaphoreType.DMA((n - 1,)),
+    ]
+
+
+def convolve(opened, behind, ahead, taps, vectors, number):
     blocks, frame_count, width = opened.shape
     channels = width // 2
-    rows = pl.BlockSpec((1, frame_count, channels), lambda i: (i, 0, 0))
-    places = pl.BlockSpec((1, frame_count, 1), lambda i: (i, 0, 0))
+    inside = pl.BlockSpec(memory_space=pltpu.VMEM)
+    wide = (blocks, frame_count, channels)
     return pl.pallas_call(
-        convolve_kernel,
-        grid=(blocks,),
-        out_shape=[jax.ShapeDtypeStruct((blocks, frame_count, channels), jnp.float32)] * 2,
-        in_specs=[
-            pl.BlockSpec((1, frame_count, width), lambda i: (i, 0, 0)),
-            places,
-            places,
-            pl.BlockSpec((KW, channels), lambda i: (0, 0)),
-            pl.BlockSpec((1, channels), lambda i: (0, 0)),
+        functools.partial(convolve_kernel, blocks),
+        out_shape=[
+            jax.ShapeDtypeStruct(wide, jnp.float32),
+            jax.ShapeDtypeStruct(wide, jnp.float32),
+            jax.ShapeDtypeStruct((blocks, frame_count, 1), jnp.float32),
+            jax.ShapeDtypeStruct(wide, jnp.bfloat16),
         ],
-        out_specs=[rows, rows],
-        scratch_shapes=[pltpu.VMEM((frame_count + 2 * MARGIN, channels), jnp.float32)],
+        in_specs=[inside] * 5,
+        out_specs=[inside] * 4,
+        scratch_shapes=[pltpu.VMEM((frame_count + 2 * MARGIN, channels), jnp.float32)] + swap_scratch(blocks, frame_count),
+        compiler_params=pltpu.CompilerParams(collective_id=number, has_side_effects=True),
         name="convolve",
-    )(opened, behind, ahead, taps, bias)
-
-
-def unconvolve_kernel(opened, gated, upstream, behind, ahead, taps, grads, lifts, slopes, padded, padded_grad):
+    )(opened, behind, ahead, taps, vectors)
+
+
+def unconvolve_kernel(
+    n, opened, gated, upstream, unit, inverse, behind, ahead, taps, vectors, grads, lifts, slopes, *scratch
+):
+    padded, padded_grad, turned, mine, shared, send, recv = scratch
     frame_count, channels = gated.shape[1:]
-
-    @pl.when(pl.program_id(0) == 0)
-    def _():
-        lifts[...] = jnp.zeros_like(lifts)
-        slopes[...] = jnp.zeros_like(slopes)
-
-    for store, value in ((padded, gated[0]), (padded_grad, upstream[0])):
-        store[pl.ds(0, MARGIN), :] = jnp.zeros((MARGIN, channels), jnp.float32)
-        store[pl.ds(MARGIN + frame_count, MARGIN), :] = jnp.zeros((MARGIN, channels), jnp.float32)
-        store[pl.ds(MARGIN, frame_count), :] = value
-    back = jnp.broadcast_to(behind[0], (frame_count, LANES))
-    front = jnp.broadcast_to(ahead[0], (frame_count, LANES))
-    for low in range(0, channels, LANES):
-        lanes = slice(low, low + LANES)
-        above = upstream[0, :, lanes]
-        running = jnp.zeros((frame_count, LANES), jnp.float32)
-        for tap in range(KW):
-            offset = tap - (KW - 1) // 2
-            moved = padded[pl.ds(MARGIN + offset, frame_count), lanes]
-            moved_grad = padded_grad[pl.ds(MARGIN + offset, frame_count), lanes]
-            if offset:
-                mask = reach_mask(offset, back, front)
-                moved = jnp.where(mask, moved, 0.0)
-                moved_grad = jnp.where(mask, moved_grad, 0.0)
-            running = running + moved_grad * taps[pl.ds(KW - 1 - tap, 1), lanes]
-            slopes[pl.ds(tap, 1), lanes] += jnp.sum(moved * above, axis=0, keepdims=True)
-        slopes[pl.ds(KW, 1), lanes] += jnp.sum(above, axis=0, keepdims=True)
-        wide = slice(channels + low, channels + low + LANES)
-        left, gate = opened[0, :, lanes], jax.nn.sigmoid(opened[0, :, wide])
-        left_grad = running * gate
-        gate_grad = running * left * gate * (1.0 - gate)
-        grads[0, :, lanes] = left_grad.astype(jnp.bfloat16)
-        grads[0, :, wide] = gate_grad.astype(jnp.bfloat16)
-        lifts[:, lanes] += jnp.sum(left_grad, axis=0, keepdims=True)
-        lifts[:, wide] += jnp.sum(gate_grad, axis=0, keepdims=True)
-
-
-def unconvolve(opened, gated, upstream, behind, ahead, taps):
+    greet([target for target, unused in near(lax.axis_index("dp"), n)])
+    places = lax.broadcasted_iota(jnp.int32, (frame_count, LANES), 1)
+    lifts[...] = jnp.zeros_like(lifts)
+    slopes[...] = jnp.zeros_like(slopes)
+    wide = jnp.zeros((frame_count, LANES), jnp.float32)
+    for block in range(n):
+        scaled = upstream[block] * vectors[11:12, :]
+        plain = jnp.sum(scaled, axis=-1, keepdims=True)
+        along = jnp.sum(scaled * unit[block], axis=-1, keepdims=True)
+        wide = jnp.where(places == block, plain, jnp.where(places == n + block, along, wide))
+    mine[...] = to_rows(wide, 2 * n)
+    swap(n, mine, shared, send, recv)
+    found = to_columns(sum(shared[at] for at in range(n)) / (n * channels))
+    for block in range(n):
+        scaled = upstream[block] * vectors[11:12, :]
+        turned[block] = inverse[block] * (scaled - found[block] - unit[block] * found[n + block])
+
+    def block_back(block, carry):
+        fill(padded, gated[block])
+        fill(padded_grad, turned[block])
+        back = jnp.broadcast_to(behind[block], (frame_count, LANES))
+        front = jnp.broadcast_to(ahead[block], (frame_count, LANES))
+        for low in range(0, channels, LANES):
+            lanes = slice(low, low + LANES)
+            above = turned[block, :, lanes]
+            running = jnp.zeros((frame_count, LANES), jnp.float32)
+            for tap in range(KW):
+                offset = tap - (KW - 1) // 2
+                moved = padded[pl.ds(MARGIN + offset, frame_count), lanes]
+                moved_grad = padded_grad[pl.ds(MARGIN + offset, frame_count), lanes]
+                if offset:
+                    mask = reach_mask(offset, back, front)
+                    moved = jnp.where(mask, moved, 0.0)
+                    moved_grad = jnp.where(mask, moved_grad, 0.0)
+                running = running + moved_grad * taps[pl.ds(KW - 1 - tap, 1), lanes]
+                slopes[pl.ds(tap, 1), lanes] += jnp.sum(moved * above, axis=0, keepdims=True)
+            slopes[pl.ds(KW, 1), lanes] += jnp.sum(above, axis=0, keepdims=True)
+            far = slice(channels + low, channels + low + LANES)
+            left, gate = opened[block, :, lanes], jax.nn.sigmoid(opened[block, :, far])
+            left_grad = running * gate
+            gate_grad = running * left * gate * (1.0 - gate)
+            grads[block, :, lanes] = left_grad.astype(jnp.bfloat16)
+            grads[block, :, far] = gate_grad.astype(jnp.bfloat16)
+            lifts[:, lanes] += jnp.sum(left_grad, axis=0, keepdims=True)
+            lifts[:, far] += jnp.sum(gate_grad, axis=0, keepdims=True)
+        return carry
+
+    lax.fori_loop(0, n, block_back, 0)
+
+
+def unconvolve(opened, gated, upstream, unit, inverse, behind, ahead, taps, vectors, number):
     blocks, frame_count, width = opened.shape
     channels = width // 2
-    wide = pl.BlockSpec((1, frame_count, width), lambda i: (i, 0, 0))
-    rows = pl.BlockSpec((1, frame_count, channels), lambda i: (i, 0, 0))
-    places = pl.BlockSpec((1, frame_count, 1), lambda i: (i, 0, 0))
+    inside = pl.BlockSpec(memory_space=pltpu.VMEM)
     return pl.pallas_call(
-        unconvolve_kernel,
-        grid=(blocks,),
+        functools.partial(unconvolve_kernel, blocks),
         out_shape=[
             jax.ShapeDtypeStruct((blocks, frame_count, width), jnp.bfloat16),
             jax.ShapeDtypeStruct((1, width), jnp.float32),
             jax.ShapeDtypeStruct((KW + 1, channels), jnp.float32),
         ],
-        in_specs=[wide, rows, rows, places, places, pl.BlockSpec((KW, channels), lambda i: (0, 0))],
-        out_specs=[
-            wide,
-            pl.BlockSpec((1, width), lambda i: (0, 0)),
-            pl.BlockSpec((KW + 1, channels), lambda i: (0, 0)),
-        ],
-        scratch_shapes=[pltpu.VMEM((frame_count + 2 * MARGIN, channels), jnp.float32)] * 2,
+        in_specs=[inside] * 9,
+        out_specs=[inside] * 3,
+        scratch_shapes=[
+            pltpu.VMEM((frame_count + 2 * MARGIN, channels), jnp.float32),
+            pltpu.VMEM((frame_count + 2 * MARGIN, channels), jnp.float32),
+            pltpu.VMEM((blocks, frame_count, channels), jnp.float32),
+        ]
+        + swap_scratch(blocks, frame_count),
+        compiler_params=pltpu.CompilerParams(collective_id=number, has_side_effects=True),
         name="unconvolve",
-    )(opened, gated, upstream, behind, ahead, taps)
+    )(opened, gated, upstream, unit, inverse, behind, ahead, taps, vectors)
 
 
 def gather_rows(value):
@@ -1729,20 +1774,8 @@
     w_filter_up = w_filter[:, :, : 2 * inner].reshape(D, 2 * inner)
     w_filter_down = jnp.transpose(w_filter[:, :, 2 * inner :], (1, 0, 2)).reshape(inner, D)
     opened = blocks(flat_dot(flat(filter_hidden), w_filter_up) + filter_lifts)
-    gated, filtered = convolve(opened, behind, ahead, taps, own_vectors[10:11])
-    filtered = flat(filtered)
-    local_mean = jnp.mean(filtered, axis=-1)
-    local_square = jnp.sum((filtered - local_mean[:, None]) ** 2, axis=-1)
-    shared = share(
-        n, jnp.concatenate([local_mean.reshape(n, frame_count), local_square.reshape(n, frame_count)]), 4
-    )
-    means, squares = shared[:, :n], shared[:, n:]
-    middle_mean = jnp.mean(means, axis=0)
-    spread = jnp.sum(squares, axis=0) + inner * jnp.sum((means - middle_mean) ** 2, axis=0)
-    middle_inverse = lax.rsqrt(spread / D + EPSILON).reshape(-1, 1)
-    middle_unit = (filtered - middle_mean.reshape(-1, 1)) * middle_inverse
-    middle = middle_unit * own_vectors[11] + own_vectors[12]
-    swished = (middle * jax.nn.sigmoid(middle)).astype(jnp.bfloat16)
+    gated, middle_unit, middle_inverse, swished = convolve(opened, behind, ahead, taps, own_vectors, 4)
+    swished = flat(swished)
     part = blocks(flat_dot(swished, w_filter_down).astype(jnp.bfloat16))
     third_rows, late_hidden = boundary(
         functools.partial(step_forward, 1.0), part, [second_rows], vectors, (13, 14, 15), 1, 0, 5
@@ -1762,26 +1795,13 @@
     )
     low = flat(low)
     filter_down_slope = lead_dot(swished, low).astype(jnp.bfloat16)
+    flat_unit = flat(middle_unit)
+    middle = flat_unit * own_vectors[11] + own_vectors[12]
     middle_grad = swish_back(back_dot(low, w_filter_down), middle)
-    middle_gain_slope = jnp.sum(middle_grad * middle_unit, axis=0)
+    middle_gain_slope = jnp.sum(middle_grad * flat_unit, axis=0)
     middle_shift_slope = jnp.sum(middle_grad, axis=0)
-    scaled = middle_grad * own_vectors[11]
-    shared = share(
-        n,
-        jnp.concatenate(
-            [
-                jnp.sum(scaled, axis=-1).reshape(n, frame_count),
-                jnp.sum(scaled * middle_unit, axis=-1).reshape(n, frame_count),
-            ]
-        ),
-        8,
-    )
-    totals = jnp.sum(shared, axis=0) / D
-    filtered_grad = middle_inverse * (
-        scaled - totals[:n].reshape(-1, 1) - middle_unit * totals[n:].reshape(-1, 1)
-    )
     opened_low, filter_lift_slope, depth_slope = unconvolve(
-        opened, gated, blocks(filtered_grad), behind, ahead, taps
+        opened, gated, blocks(middle_grad), middle_unit, middle_inverse, behind, ahead, taps, own_vectors, 8
     )
     opened_low = flat(opened_low)
     filter_up_slope = lead_dot(flat(filter_hidden), opened_low).astype(jnp.bfloat16)

time: 434 us -> 425 us (0.979)
  other arithmetic: 28.5 us -> 21.7 us
    pallas_call x4 -> x2, Pallas kernels: 25.7 us -> 26.5 us  [the longest x1 15.1 us: unconvolve(): pl.pallas_call(functools.partial(unconvolve_kernel, blocks), out_shape=[j...]
  transfers between devices with their start and end apart: 8 -> 8, of which waited for: 0 -> 0; matrix products, arithmetic and copies ran while one was open for 20% -> 19% of each run, Pallas kernels for 51% -> 52%
where the time goes in v5:
time: 425 us; the launch traced here: 421 us
  Pallas kernels  298 us (70%)
  matrix products  55.3 us (13%)
  local copies, waits for them, and re-layouts  28.2 us (7%)
  other arithmetic  21.7 us (5%)
  between operations  15.2 us (4%)
    pallas_call x8, Pallas kernels, boundary(): pl.pallas_call(functools.partial(boundary_kernel, step, shape), out_shape...  175 us
    pallas_call x1, Pallas kernels, exchange(): pl.pallas_call(functools.partial(exchange_kernel, n, m, width, inner), ou...  51.8 us
    dot_general x8, matrix products, flat_dot(): return jnp.dot(left_rows, right_rows, preferred_element_type=jnp.float32)  21.3 us
    dot_general x8, matrix products, back_dot(): lax.dot_general(left_rows, right_rows, (((1,), (1,)), ((), ())), preferre...  21.2 us
    pallas_call x1, Pallas kernels, collect(): pl.pallas_call(functools.partial(collect_kernel, n, m, sizes), out_shape=...  15.8 us
    pallas_call x1, Pallas kernels, unconvolve(): pl.pallas_call(functools.partial(unconvolve_kernel, blocks), out_shape=[j...  15.1 us
    dot_general x8, matrix products, lead_dot(): lax.dot_general(left_rows, right_rows, (((0,), (0,)), ((), ())), preferre...  12.8 us
    pallas_call x1, Pallas kernels, unattend(): pl.pallas_call(functools.partial(unattend_kernel, heads), grid=(blocks,),...  12 us
  transfers between devices with their start and end apart: 8, of which 0 were waited for; matrix products, arithmetic and copies ran while one was open for 19% of the time, Pallas kernels for 52%

profile of v5, /device:TPU:0, one launch (start us, length us, event | category | flops | bytes accessed | tf_op | source)
XLA Modules:
  0.0 420.7 jit_solution(4478564766437606589)
XLA Ops:
  7.3 51.8 %exchange.1 = (bf16[32,32,1024]{2,1,0:T(8,128)(2,1)}, bf16[8,4,32,1024]{3,2,1,0:T(8,128)(2,1)}, bf16[4,32,1024]{2,1,0:T(8,128)(2,1)}, bf16[4,32,1024]{2,1,0:T(8,...) custom-call(bf16[32,4096]{1,0:T(8,128)(2,1)} %refs_0_.1, ...), custom_call_target="tpu_custom_call" | custom-call | tf_op jit(solution)/shard_map/exchange/pallas_call | solution.py:908
  66.8 2.6 fusion.15
  69.5 2.3 convolution_convert_fusion.10
  71.7 25.7 %boundary.8 = (f32[128,1024]{1,0:T(8,128)}, bf16[4,128,1024]{2,1,0:T(8,128)(2,1)}) custom-call(bf16[4,128,1024]{2,1,0:T(8,128)(2,1)} %bitcast.213, bf16[128,1024]{1,0:T(8,128)(2,1)} %refs_2_.5, f32[19,1024]{1,0:T(8,128)} %get-tuple-element.141.refs_2_.refs_3_), custom_call_target="tpu_custom_call" | custom-call | tf_op jit(solution)/shard_map/boundary/pallas_call | solution.py:1301
  102.3 3.1 add_convert_fusion
  105.4 8.1 %attend.1 = bf16[4,128,256]{2,1,0:T(8,128)(2,1)} custom-call(bf16[4,128,768]{2,1,0:T(8,128)(2,1)} %bitcast.186, s32[4,1,128]{2,1,0:T(1,128)} %get-tuple-element.147.segment_rows, s32[4,128,1]{2,1,0:T(8,128)} %copy.118.segment_columns, f32[4,256]{1,0:T(4,128)} %rev.4.table), custom_call_target="tpu_custom_call" | custom-call | tf_op jit(solution)/shard_map/attend/pallas_call | solution.py:1348
  113.5 2.4 convolution_convert_fusion.9
  115.9 23.3 %boundary.9 = (f32[128,1024]{1,0:T(8,128)}, bf16[4,128,1024]{2,1,0:T(8,128)(2,1)}) custom-call(bf16[4,128,1024]{2,1,0:T(8,128)(2,1)} %bitcast.182, f32[128,1024]{1,0:T(8,128)} %get-tuple-element.149.refs_1_.refs_2_, f32[19,1024]{1,0:T(8,128)} %get-tuple-element.141.refs_2_.refs_3_), custom_call_target="tpu_custom_call" | custom-call | tf_op jit(solution)/shard_map/boundary/pallas_call | solution.py:1301
  142.3 2.9 convolution_add_fusion
  145.3 11.4 %convolve.1 = (f32[4,128,256]{2,1,0:T(8,128)}, f32[4,128,256]{2,1,0:T(8,128)}, f32[4,128,1]{2,1,0:T(8,128)}, bf16[4,128,256]{2,1,0:T(8,128)(2,1)}) custom-call(f32[4,128,512]{2,1,0:T(8,128)} %bitcast.184, s32[4,128,1]{2,1,0:T(8,128)} %get-tuple-element.379.behind, s32[4,128,1]{2,1,0:T(8,128)} %get-tuple-element.378.ahead, f32[31,256]{1,0:T(8,128)} %bitcast.221, ...), custom_call_target="tpu_custom_call" | custom-call | tf_op jit(solution)/shard_map/convolve/pallas_call | solution.py:1537
  156.6 2.4 convolution_convert_fusion.8
  159.0 24.2 %boundary.10 = (f32[128,1024]{1,0:T(8,128)}, bf16[4,128,1024]{2,1,0:T(8,128)(2,1)}) custom-call(bf16[4,128,1024]{2,1,0:T(8,128)(2,1)} %bitcast.183, f32[128,1024]{1,0:T(8,128)} %get-tuple-element.157.refs_1_.refs_2_, f32[19,1024]{1,0:T(8,128)} %get-tuple-element.141.refs_2_.refs_3_), custom_call_target="tpu_custom_call" | custom-call | tf_op jit(solution)/shard_map/boundary/pallas_call | solution.py:1301
  183.3 3.3 fusion.16
  186.6 2.3 convolution_convert_fusion.7
  188.9 22.5 %boundary.11 = (f32[128,1024]{1,0:T(8,128)}, f32[128,1024]{1,0:T(8,128)}, bf16[4,128,1024]{2,1,0:T(8,128)(2,1)}, f32[3,1024]{1,0:T(4,128)}) custom-call(bf16[4,128,1024]{2,1,0:T(8,128)(2,1)} %bitcast.216, f32[128,1024]{1,0:T(8,128)} %get-tuple-element.163.refs_1_.refs_2_, bf16[128,1024]{1,0:T(8,128)(2,1)} %refs_2_.4, ...), custom_call_target="tpu_custom_call" | custom-call | tf_op jit(solution)/shard_map/boundary/pallas_call | solution.py:1301
  211.5 4.4 %fusion.14 = (f32[1024]{0:T(1024)S(1)}, bf16[512,1024]{1,0:T(8,128)(2,1)S(1)}) fusion(f32[512,1024]{1,0:T(8,128)} %copy-done.36, f32[1024]{0:T(1024)S(1)} %bitcast.242, bf16[512,1024]{1,0:T(8,128)(2,1)} %bitcast.263, bf16[1024,1024]{1,0:T(8,128)(2,1)} %all-gather.11.cloned.1.call-done), kind=kOutput, calls=%fused_computation.76 | convolution fusion | flops 1079507968 | bytes 6299648 | tf_op jit(solution)/shard_map/dot_general | solution.py:39
  217.5 2.3 convolution_convert_fusion.6
  221.3 2.3 pad_maximum_fusion
  223.7 22.0 %boundary.12 = (f32[128,1024]{1,0:T(8,128)}, bf16[4,128,1024]{2,1,0:T(8,128)(2,1)}, f32[3,1024]{1,0:T(4,128)}) custom-call(bf16[4,128,1024]{2,1,0:T(8,128)(2,1)} %bitcast.210, f32[128,1024]{1,0:T(8,128)} %get-tuple-element.168.refs_1_, f32[128,1024]{1,0:T(8,128)} %get-tuple-element.163.refs_1_.refs_2_, f32[19,1024]{1,0:T(8,128)} %get-tuple-element.141.refs_2_.refs_3_), custom_call_target="tpu_custom_call" | custom-call | tf_op jit(solution)/shard_map/boundary/pallas_call | solution.py:1301
  248.0 2.5 fusion.9
  250.5 15.1 %unconvolve.1 = (bf16[4,128,512]{2,1,0:T(8,128)(2,1)}, f32[1,512]{1,0:T(1,128)}, f32[32,256]{1,0:T(8,128)}) custom-call(f32[4,128,512]{2,1,0:T(8,128)} %bitcast.185, f32[4,128,256]{2,1,0:T(8,128)} %get-tuple-element.165.gated, f32[4,128,256]{2,1,0:T(8,128)} %bitcast.220, f32[4,128,256]{2,1,0:T(8,128)} %get-tuple-element.170.unit, ...), custom_call_target="tpu_custom_call" | custom-call | tf_op jit(solution)/shard_map/unconvolve/pallas_call | solution.py:1612
  271.2 22.2 %boundary.13 = (f32[128,1024]{1,0:T(8,128)}, bf16[4,128,1024]{2,1,0:T(8,128)(2,1)}, f32[3,1024]{1,0:T(4,128)}) custom-call(bf16[4,128,1024]{2,1,0:T(8,128)(2,1)} %bitcast.212, f32[128,1024]{1,0:T(8,128)} %get-tuple-element.174.refs_1_, f32[128,1024]{1,0:T(8,128)} %get-tuple-element.157.refs_1_.refs_2_, f32[19,1024]{1,0:T(8,128)} %get-tuple-element.141.refs_2_.refs_3_), custom_call_target="tpu_custom_call" | custom-call | tf_op jit(solution)/shard_map/boundary/pallas_call | solution.py:1301
  293.5 2.5 convolution_convert_fusion.12
  295.9 12.0 %unattend.1 = (bf16[4,128,768]{2,1,0:T(8,128)(2,1)}, f32[2,256]{1,0:T(2,128)}, f32[4,256]{1,0:T(4,128)}) custom-call(bf16[4,128,768]{2,1,0:T(8,128)(2,1)} %bitcast.187, bf16[4,128,256]{2,1,0:T(8,128)(2,1)} %bitcast.224, s32[4,1,128]{2,1,0:T(1,128)} %get-tuple-element.147.segment_rows, s32[4,128,1]{2,1,0:T(8,128)} %copy.118.segment_columns, f32[4,256]{1,0:T(4,128)} %rev.4.table), custom_call_target="tpu_custom_call" | custom-call | tf_op jit(solution)/shard_map/unattend/pallas_call | solution.py:1416
  315.7 22.8 %boundary.14 = (f32[128,1024]{1,0:T(8,128)}, bf16[4,128,1024]{2,1,0:T(8,128)(2,1)}, f32[3,1024]{1,0:T(4,128)}) custom-call(bf16[4,128,1024]{2,1,0:T(8,128)(2,1)} %bitcast.211, f32[128,1024]{1,0:T(8,128)} %get-tuple-element.179.refs_1_, f32[128,1024]{1,0:T(8,128)} %get-tuple-element.149.refs_1_.refs_2_, f32[19,1024]{1,0:T(8,128)} %get-tuple-element.141.refs_2_.refs_3_), custom_call_target="tpu_custom_call" | custom-call | tf_op jit(solution)/shard_map/boundary/pallas_call | solution.py:1301
  338.6 2.7 convolution_convert_fusion
  346.3 2.3 pad_maximum_fusion.1
  348.6 3.9 convolution_convert_fusion.5
  355.4 12.1 %boundary.15 = (f32[128,1024]{1,0:T(8,128)}, f32[2,1024]{1,0:T(2,128)}) custom-call(bf16[4,128,1024]{2,1,0:T(8,128)(2,1)} %bitcast.215, f32[128,1024]{1,0:T(8,128)} %get-tuple-element.185.refs_1_, bf16[128,1024]{1,0:T(8,128)(2,1)} %refs_2_.5, f32[19,1024]{1,0:T(8,128)} %get-tuple-element.141.refs_2_.refs_3_), custom_call_target="tpu_custom_call" | custom-call | tf_op jit(solution)/shard_map/boundary/pallas_call | solution.py:1301
  372.3 2.2 keep.1
  375.4 15.8 %collect.1 = (f32[32,5,128]{2,1,0:T(8,128)}, f32[8,11,128]{2,1,0:T(8,128)}, bf16[32,4096]{1,0:T(8,128)(2,1)}, bf16[32,3072]{1,0:T(8,128)(2,1)}, bf16[32,2048]{1,0:T(8,128)(2,1)}) custom-call(f32[32,5,128]{2,1,0:T(8,128)} %reshape.410.refs_0_, f32[8,11,128]{2,1,0:T(8,128)} %reshape.413.refs_1_, bf16[8,32,1024]{2,1,0:T(8,128)(2,1)} %reduce-scatter.5.cloned.1.call-done.refs_2_, ...), custom_call_target="tpu_custom_call" | custom-call | tf_op jit(solution)/shard_map/collect/pallas_call | solution.py:1046
  403.3 6.4 %giveback.1 = bf16[32,4096]{1,0:T(8,128)(2,1)} custom-call(bf16[8,32,1024]{2,1,0:T(8,128)(2,1)} %reduce-scatter.11.cloned.1.call-done.refs_0_), custom_call_target="tpu_custom_call" | custom-call | tf_op jit(solution)/shard_map/giveback/pallas_call | solution.py:971
  (210 shorter events, 63.5 us)
Async XLA Ops:
  7.2 91.9 %all-gather.5.cloned.1.call-start = ((), (), s32[]{:S(2)}) async-start(), calls=%async_computation.4 | async-start | bytes 2359296 | tf_op jit(solution)/shard_map/all_gather | solution.py:1722
  59.1 6.9 %copy-start.9 = (bf16[8,32,31]{2,1,0:T(8,128)(2,1)S(1)}, bf16[8,32,31]{2,1,0:T(8,128)(2,1)}, u32[]{:S(2)}) copy-start(bf16[8,32,31]{2,1,0:T(8,128)(2,1)} %get-tuple-element.155) | copy-start | bytes 47620
  59.1 7.7 %copy-start.16 = (f32[2,1024]{1,0:T(2,128)S(1)}, f32[2,1024]{1,0:T(2,128)}, u32[]{:S(2)}) copy-start(f32[2,1024]{1,0:T(2,128)} %get-tuple-element.139) | copy-start | bytes 24580
  59.1 7.7 %copy-start.19 = (bf16[32,32,1024]{2,1,0:T(8,128)(2,1)S(1)}, bf16[32,32,1024]{2,1,0:T(8,128)(2,1)}, u32[]{:S(2)}) copy-start(bf16[32,32,1024]{2,1,0:T(8,128)(2,1)} %get-tuple-element.138) | copy-start | bytes 6291460
  59.2 80.1 %all-gather.7.cloned.1.call-start = ((), (), s32[]{:S(2)}) async-start(), calls=%async_computation.5 | async-start | bytes 1769472 | tf_op jit(solution)/shard_map/all_gather | solution.py:1723
  59.9 123.3 %all-gather.9.cloned.1.call-start = ((), (), s32[]{:S(2)}) async-start(), calls=%async_computation.6 | async-start | bytes 2359296 | tf_op jit(solution)/shard_map/all_gather | solution.py:1637
  60.6 122.6 %all-gather.11.cloned.1.call-start = ((), (), s32[]{:S(2)}) async-start(), calls=%async_computation.7 | async-start | bytes 2359296 | tf_op jit(solution)/shard_map/all_gather | solution.py:1633
  61.2 254.4 %reduce-scatter.5.cloned.1.call-start = ((), (), s32[]{:S(2)}) async-start(), calls=%async_computation.8 | async-start | bytes 4718592 | tf_op jit(solution)/shard_map/reduce_scatter | solution.py:1792
  66.8 2.7 copy-start.20
  100.6 4.8 %copy-start.2 = (bf16[4,256,768]{2,1,0:T(8,128)(2,1)}, bf16[4,256,768]{2,1,0:T(8,128)(2,1)S(1)}, u32[]{:S(2)}) copy-start(bf16[4,256,768]{2,1,0:T(8,128)(2,1)S(1)} %slice.167) | copy-start | bytes 4718596
  139.3 3.0 copy-start.32
  140.6 4.6 %copy-start.6 = (bf16[4,256,512]{2,1,0:T(8,128)(2,1)}, bf16[4,256,512]{2,1,0:T(8,128)(2,1)S(1)}, u32[]{:S(2)}) copy-start(bf16[4,256,512]{2,1,0:T(8,128)(2,1)S(1)} %slice.172) | copy-start | bytes 3145732
  183.3 3.3 copy-start.23
  211.4 4.5 %copy-start.29 = (bf16[4,128,1024]{2,1,0:T(8,128)(2,1)S(1)}, bf16[4,128,1024]{2,1,0:T(8,128)(2,1)}, u32[]{:S(2)}) copy-start(bf16[4,128,1024]{2,1,0:T(8,128)(2,1)} %get-tuple-element.166) | copy-start | bytes 3145732
  211.5 4.5 %copy-start.37 = (f32[512,1024]{1,0:T(8,128)S(1)}, f32[512,1024]{1,0:T(8,128)}, u32[]{:S(2)}) copy-start(f32[512,1024]{1,0:T(8,128)} %copy-done.36) | copy-start | bytes 6291460
  223.6 22.1 %copy-start.4 = (bf16[4,128,256]{2,1,0:T(8,128)(2,1)S(1)}, bf16[4,128,256]{2,1,0:T(8,128)(2,1)}, u32[]{:S(2)}) copy-start(bf16[4,128,256]{2,1,0:T(8,128)(2,1)} %get-tuple-element.156) | copy-start | bytes 786436
  223.6 128.9 %reduce-scatter.7.cloned.1.call-start = ((), (), s32[]{:S(2)}) async-start(), calls=%async_computation.9 | async-start | bytes 1769472 | tf_op jit(solution)/shard_map/reduce_scatter | solution.py:1810
  250.5 15.1 %copy-start.26 = (bf16[4,128,1024]{2,1,0:T(8,128)(2,1)S(1)}, bf16[4,128,1024]{2,1,0:T(8,128)(2,1)}, u32[]{:S(2)}) copy-start(bf16[4,128,1024]{2,1,0:T(8,128)(2,1)} %get-tuple-element.152) | copy-start | bytes 3145732
  271.2 104.2 %reduce-scatter.9.cloned.1.call-start = ((), (), s32[]{:S(2)}) async-start(), calls=%async_computation.10 | async-start | bytes 2359296 | tf_op jit(solution)/shard_map/reduce_scatter | solution.py:1824
  293.4 14.5 %copy-start = (bf16[4,128,256]{2,1,0:T(8,128)(2,1)S(1)}, bf16[4,128,256]{2,1,0:T(8,128)(2,1)}, u32[]{:S(2)}) copy-start(bf16[4,128,256]{2,1,0:T(8,128)(2,1)} %attend.1) | copy-start | bytes 786436
  293.4 14.5 %copy-start.5 = (bf16[4,128,1024]{2,1,0:T(8,128)(2,1)S(1)}, bf16[4,128,1024]{2,1,0:T(8,128)(2,1)}, u32[]{:S(2)}) copy-start(bf16[4,128,1024]{2,1,0:T(8,128)(2,1)} %get-tuple-element.175) | copy-start | bytes 3145732
  315.6 22.9 %copy-start.34 = (f32[512,1024]{1,0:T(8,128)S(1)}, f32[512,1024]{1,0:T(8,128)}, u32[]{:S(2)}) copy-start(f32[512,1024]{1,0:T(8,128)} %copy-done.33) | copy-start | bytes 6291460
  315.7 87.6 %reduce-scatter.11.cloned.1.call-start = ((), (), s32[]{:S(2)}) async-start(), calls=%async_computation.11 | async-start | bytes 4718592 | tf_op jit(solution)/shard_map/reduce_scatter | solution.py:1832
  338.6 2.9 copy-start.35
  352.6 2.5 copy-start.10
  352.6 14.9 %copy-start.11 = (f32[3,1024]{1,0:T(4,128)S(1)}, f32[3,1024]{1,0:T(4,128)}, u32[]{:S(2)}) copy-start(f32[3,1024]{1,0:T(4,128)} %get-tuple-element.189) | copy-start | bytes 36868
  352.6 14.9 %copy-start.12 = (f32[3,1024]{1,0:T(4,128)S(1)}, f32[3,1024]{1,0:T(4,128)}, u32[]{:S(2)}) copy-start(f32[3,1024]{1,0:T(4,128)} %get-tuple-element.190) | copy-start | bytes 36868
  352.6 14.9 %copy-start.13 = (f32[3,1024]{1,0:T(4,128)S(1)}, f32[3,1024]{1,0:T(4,128)}, u32[]{:S(2)}) copy-start(f32[3,1024]{1,0:T(4,128)} %get-tuple-element.191) | copy-start | bytes 36868
  352.7 14.9 %copy-start.14 = (f32[3,1024]{1,0:T(4,128)S(1)}, f32[3,1024]{1,0:T(4,128)}, u32[]{:S(2)}) copy-start(f32[3,1024]{1,0:T(4,128)} %get-tuple-element.192) | copy-start | bytes 36868
  368.5 6.0 %slice-start.1 = ((bf16[8,32,1024]{2,1,0:T(8,128)(2,1)}), bf16[4,32,1024]{2,1,0:T(8,128)(2,1)S(1)}, s32[]{:S(2)}) async-start(bf16[8,32,1024]{2,1,0:T(8,128)(2,1)} %reduce-scatter.5.cloned.1.call-done.refs_2_), calls=%async_computation.13 | async-start | bytes 524288 | tf_op jit(solution)/shard_map/slice | solution.py:1911
  391.2 9.3 %copy-start.8 = (bf16[32,4096]{1,0:T(8,128)(2,1)S(1)}, bf16[32,4096]{1,0:T(8,128)(2,1)}, u32[]{:S(2)}) copy-start(bf16[32,4096]{1,0:T(8,128)(2,1)} %get-tuple-element.205) | copy-start | bytes 786436
  403.3 8.2 %slice-start = ((bf16[8,32,1024]{2,1,0:T(8,128)(2,1)}), bf16[4,32,1024]{2,1,0:T(8,128)(2,1)S(1)}, s32[]{:S(2)}) async-start(bf16[8,32,1024]{2,1,0:T(8,128)(2,1)} %reduce-scatter.11.cloned.1.call-done.refs_0_), calls=%async_computation.12 | async-start | bytes 524288 | tf_op jit(solution)/shard_map/slice | solution.py:1920
  (18 other events, 33.0 us)
Sparse Core Ops, SparseCore 0:
  59.3 27.0 all-gather.4
  88.0 24.6 all-gather.6
  114.4 28.1 all-gather.8
  144.0 28.6 all-gather.10
  223.8 48.3 reduce-scatter.4
  274.3 32.8 reduce-scatter.6
  315.8 34.6 reduce-scatter.8
  352.7 50.5 reduce-scatter.10

commit v6 on v5

--- a/solution.py
+++ b/solution.py
@@ -700,13 +700,43 @@
             )
 
 
+def pack_info(info, segs):
+    count = segs.shape[1]
+    row = segs[...].astype(jnp.float32)
+    wide = jnp.broadcast_to(row, (count, count))
+    tall = jnp.transpose(wide)
+    places = lax.broadcasted_iota(jnp.int32, (1, count), 1).astype(jnp.float32)
+    info[...] = jnp.zeros_like(info)
+    info[0:1, :] = row
+    info[1:2, :] = places - jnp.sum(jnp.where(tall < wide, 1.0, 0.0), axis=0, keepdims=True)
+    info[2:3, :] = jnp.sum(jnp.where(tall <= wide, 1.0, 0.0), axis=0, keepdims=True) - 1.0 - places
+
+
+def spread_info(infos, seg_rows, seg_columns, behind, ahead):
+    for block in range(infos.shape[0]):
+        found = to_columns(infos[block])
+        seg_rows[block] = infos[block, 0:1, :]
+        seg_columns[block], behind[block], ahead[block] = found[0], found[1], found[2]
+
+
+def spread_table(heads, me, gathered, table_all, own_table):
+    buckets = gathered[:, 8:16, :].reshape(NREL, LANES).astype(jnp.bfloat16)
+    sides = lax.broadcasted_iota(jnp.int32, (NREL, NREL), 0) + lax.broadcasted_iota(jnp.int32, (NREL, NREL), 1)
+    turned = jnp.where(sides == NREL - 1, 1.0, 0.0).astype(jnp.bfloat16)
+    table_all[...] = lead_dot(buckets, turned)
+    for head in range(heads):
+        own_table[head : head + 1, :] = table_all[pl.ds(me * heads + head, 1), :]
+
+
 def exchange_kernel(n, m, width, inner, *refs):
     early_up, early_down, late_up, project, filter_up, output, filter_down, depth, segs, frames = refs[:10]
     singles, lift_shards, table = refs[10:29], refs[29:32], refs[32]
     up_full, down_full, late_split, mixer_split, filter_split, small_all = refs[33:39]
-    gains, own, lifts, wide_lifts, depth_all, segs_all, spread = refs[39:46]
-    gathered, small, held, local, send, recv, small_send, small_recv, up_send, up_recv = refs[46:56]
-    climb_send, climb_recv, pass_send, pass_recv, out_send, out_recv, depth_send, depth_recv = refs[56:]
+    gains, own, lifts, wide_lifts, seg_rows, seg_columns, behind, ahead, own_table, depth_all, spread = refs[39:50]
+    info, infos, table_all = refs[50:53]
+    gathered, small, held, local, send, recv, small_send, small_recv, up_send, up_recv = refs[53:63]
+    climb_send, climb_recv, pass_send, pass_recv, out_send, out_recv, depth_send, depth_recv = refs[63:]
+    pack_info(info, segs)
     pack_small(gathered.at[0], singles, lift_shards, table)
     small[...] = gathered[0].astype(jnp.bfloat16)
     me, lane = lax.axis_index("dp"), lax.axis_index("fsdp")
@@ -789,10 +819,15 @@
         for group in range(2):
             wide = pl.ds(pl.multiple_of(group * inner * n + index * inner, inner), inner)
             found.append((filter_up.at[:, wide], filter_split.at[me, :, pl.ds(group * inner, inner)]))
-        found.append((segs, segs_all.at[me]))
         return found
 
     lax.fori_loop(1, n * m, each(lambda step: to_device(step).start()), 0)
+    infos[me] = info[...]
+    info_copies = []
+    for peer, (target, unused) in enumerate(others):
+        info_copies.append(remote(info, infos.at[me], send.at[peer, 6], recv.at[peer, 6], {"dp": target}))
+    for copy in info_copies:
+        copy.start()
     lax.fori_loop(1, n, each(lambda step: to_column(step).start()), 0)
     lax.fori_loop(0, units, each(lambda unit: launch(0, unit, early_down.at[unit])), 0)
     mine = early_up.at[:, columns(me, width)]
@@ -866,7 +901,10 @@
         outgoing.append(remote(held, spread.at[me], out_send.at[peer], out_recv.at[peer], {"dp": target}))
     for copy in outgoing:
         copy.start()
-
+    for copy in info_copies:
+        copy.wait()
+    spread_info(infos, seg_rows, seg_columns, behind, ahead)
+    spread_table(HEADS // n, me, gathered, table_all, own_table)
     for distance in range(2, levels):
         for kind in range(2):
             lax.fori_loop(0, units, each(functools.partial(carry_on, kind, distance)), 0)
@@ -898,8 +936,12 @@
         struct((len(singles), inner), full),
         struct((2, width), full),
         struct((1, 2 * inner), full),
+        struct((n, 1, frame_count), full),
+        struct((n, frame_count, 1), full),
+        struct((n, frame_count, 1), full),
+        struct((n, frame_count, 1), full),
+        struct((HEADS // n, NREL), full),
         struct((m,) + depth.shape, low),
-        struct((n,) + segs.shape, segs.dtype),
         struct((n, frame_count, deep), low),
     ]
     anywhere = pl.BlockSpec(memory_space=pl.ANY)
@@ -908,9 +950,12 @@
     return pl.pallas_call(
         functools.partial(exchange_kernel, n, m, width, inner),
         out_shape=outs,
-        in_specs=[anywhere] * 9 + [inside] * (2 + len(singles) + len(lifts)),
-        out_specs=[anywhere] * 5 + [inside] * 5 + [anywhere] * 3,
+        in_specs=[anywhere] * 8 + [inside] * (3 + len(singles) + len(lifts)),
+        out_specs=[anywhere] * 5 + [inside] * 10 + [anywhere] * 2,
         scratch_shapes=[
+            pltpu.VMEM((8, frame_count), full),
+            pltpu.VMEM((n, 8, frame_count), full),
+            pltpu.VMEM((LANES, NREL), full),
             pltpu.VMEM((n * m,) + packed, full),
             pltpu.VMEM(packed, low),
             pltpu.VMEM((frame_count, deep), low),
@@ -1711,7 +1756,7 @@
     spans = hidden * n // D
     (
         w_early_up, w_early_down, late_up_split, mixer_split, filter_split, small_all, vectors, own_vectors, lifts,
-        filter_lifts, depth_all, segments_all, early_hidden,
+        filter_lifts, segment_rows, segment_columns, behind, ahead, table, depth_all, early_hidden,
     ) = exchange(
         n, m, early_up, early_down.reshape(spans, rows, D), late_up, mixer_project, filter_up, mixer_output,
         filter_down, depth_weight, segments.reshape(1, frame_count), frames, singles,
@@ -1725,17 +1770,8 @@
     w_late_down = gather_rows(late_down)
 
     early_lifts, late_lifts = lifts[0], lifts[1]
-    table = small_all[:, 8 : 8 + distance_table.shape[0], :HEADS].astype(jnp.float32).reshape(NREL, HEADS)
-    table = jnp.transpose(lax.dynamic_slice(table, (0, me * heads), (NREL, heads)))[:, ::-1]
     taps = jnp.transpose(depth_all.reshape(inner, KW)).astype(jnp.float32)
     attention_shift = jnp.concatenate([own_vectors[5], jnp.zeros((inner,), jnp.float32), own_vectors[6]])
-    segment_rows = segments_all
-    segment_columns = segments_all.reshape(n, frame_count, 1)
-    places = jnp.arange(frame_count, dtype=jnp.int32)[None, :]
-    lower = (segment_rows < segment_columns).astype(jnp.int32)
-    upto = (segment_rows <= segment_columns).astype(jnp.int32)
-    behind = (places - jnp.sum(lower, axis=-1)).reshape(n, frame_count, 1)
-    ahead = (jnp.sum(upto, axis=-1) - 1 - places).reshape(n, frame_count, 1)
 
     def blocks(value):
         return value.reshape(n, frame_count, value.shape[-1])
@@ -1751,10 +1787,10 @@
         widened_grad = swish_back(back_dot(low, w_down), widened)
         widened_low = widened_grad.astype(jnp.bfloat16)
         up_slope = lead_dot(flat(hidden_rows), widened_low).astype(jnp.bfloat16)
-        part = blocks(back_dot(widened_low, w_up).astype(jnp.bfloat16))
         down_slope = jnp.transpose(down_slope.reshape(m, spans, rows, D), (1, 0, 2, 3)).reshape(spans, m * rows, D)
         slope = jnp.concatenate([up_slope.reshape(n, D // n, hidden), down_slope])
-        part, slope = lax.optimization_barrier((part, slope))
+        widened_low, slope = lax.optimization_barrier((widened_low, slope))
+        part = blocks(back_dot(widened_low, w_up).astype(jnp.bfloat16))
         return part, slope, jnp.sum(widened_grad, axis=0)
 
     early_wide, early_active, part = feed(early_hidden, w_early_up, early_lifts, w_early_down)
@@ -1828,7 +1864,7 @@
     part, early_slope, early_lift_slope = feed_back(
         low, early_hidden, early_wide, early_active, w_early_up, w_early_down
     )
-    part, early_slope, filter_slope = lax.optimization_barrier((part, early_slope, filter_slope))
+    early_slope, filter_slope = lax.optimization_barrier((early_slope, filter_slope))
     early_slope = lax.psum_scatter(early_slope, "fsdp", scatter_dimension=1, tiled=True)
     slope_frames, early_sums = boundary(
         step_last, part, [grad, frames], vectors, (0,), 1, 2, 11, gathered=False

time: 425 us -> 428 us (level)
  transfers between devices with their start and end apart: 8 -> 8, of which waited for: 0 -> 1; matrix products, arithmetic and copies ran while one was open for 19% -> 19% of each run, Pallas kernels for 52% -> 51%
where the time goes in v6:
time: 428 us; the launch traced here: 424 us
  Pallas kernels  300 us (70%)
  matrix products  57.4 us (13%)
  local copies, waits for them, and re-layouts  28.1 us (7%)
  other arithmetic  20.7 us (5%)
  between operations  15.2 us (4%)
    pallas_call x8, Pallas kernels, boundary(): pl.pallas_call(functools.partial(boundary_kernel, step, shape), out_shape...  176 us
    pallas_call x1, Pallas kernels, exchange(): pl.pallas_call(functools.partial(exchange_kernel, n, m, width, inner), ou...  52 us
    dot_general x8, matrix products, back_dot(): lax.dot_general(left_rows, right_rows, (((1,), (1,)), ((), ())), preferre...  22.4 us
    dot_general x8, matrix products, flat_dot(): return jnp.dot(left_rows, right_rows, preferred_element_type=jnp.float32)  22.2 us
    pallas_call x1, Pallas kernels, collect(): pl.pallas_call(functools.partial(collect_kernel, n, m, sizes), out_shape=...  16 us
    pallas_call x1, Pallas kernels, unconvolve(): pl.pallas_call(functools.partial(unconvolve_kernel, blocks), out_shape=[j...  15.1 us
    dot_general x8, matrix products, lead_dot(): lax.dot_general(left_rows, right_rows, (((0,), (0,)), ((), ())), preferre...  12.8 us
    pallas_call x1, Pallas kernels, unattend(): pl.pallas_call(functools.partial(unattend_kernel, heads), grid=(blocks,),...  12 us
  transfers between devices with their start and end apart: 8, of which 1 were waited for; matrix products, arithmetic and copies ran while one was open for 19% of the time, Pallas kernels for 51%

profile of v6, /device:TPU:0, one launch (start us, length us, event | category | flops | bytes accessed | tf_op | source)
XLA Modules:
  0.0 424.0 jit_solution(11219012050912644094)
XLA Ops:
  7.3 52.0 %exchange.1 = (bf16[32,32,1024]{2,1,0:T(8,128)(2,1)}, bf16[8,4,32,1024]{3,2,1,0:T(8,128)(2,1)}, bf16[4,32,1024]{2,1,0:T(8,128)(2,1)}, bf16[4,32,1024]{2,1,0:T(8,...) custom-call(bf16[32,4096]{1,0:T(8,128)(2,1)} %refs_0_.1, ...), custom_call_target="tpu_custom_call" | custom-call | tf_op jit(solution)/shard_map/exchange/pallas_call | solution.py:950
  64.0 3.5 fusion.11
  67.5 2.3 convolution_convert_fusion.10
  69.8 25.7 %boundary.8 = (f32[128,1024]{1,0:T(8,128)}, bf16[4,128,1024]{2,1,0:T(8,128)(2,1)}) custom-call(bf16[4,128,1024]{2,1,0:T(8,128)(2,1)} %bitcast.204, bf16[128,1024]{1,0:T(8,128)(2,1)} %refs_2_.5, f32[19,1024]{1,0:T(8,128)} %get-tuple-element.143.refs_2_.refs_3_), custom_call_target="tpu_custom_call" | custom-call | tf_op jit(solution)/shard_map/boundary/pallas_call | solution.py:1346
  99.5 3.1 add_convert_fusion
  102.6 8.1 %attend.1 = bf16[4,128,256]{2,1,0:T(8,128)(2,1)} custom-call(bf16[4,128,768]{2,1,0:T(8,128)(2,1)} %bitcast.177, f32[4,1,128]{2,1,0:T(1,128)} %get-tuple-element.149.segment_rows, f32[4,128,1]{2,1,0:T(8,128)} %get-tuple-element.150.segment_columns, f32[4,256]{1,0:T(4,128)} %get-tuple-element.151.table), custom_call_target="tpu_custom_call" | custom-call | tf_op jit(solution)/shard_map/attend/pallas_call | solution.py:1393
  110.7 2.4 convolution_convert_fusion.9
  113.1 23.3 %boundary.9 = (f32[128,1024]{1,0:T(8,128)}, bf16[4,128,1024]{2,1,0:T(8,128)(2,1)}) custom-call(bf16[4,128,1024]{2,1,0:T(8,128)(2,1)} %bitcast.173, f32[128,1024]{1,0:T(8,128)} %get-tuple-element.152.refs_1_.refs_2_, f32[19,1024]{1,0:T(8,128)} %get-tuple-element.143.refs_2_.refs_3_), custom_call_target="tpu_custom_call" | custom-call | tf_op jit(solution)/shard_map/boundary/pallas_call | solution.py:1346
  139.5 2.9 convolution_add_fusion
  142.4 11.6 %convolve.1 = (f32[4,128,256]{2,1,0:T(8,128)}, f32[4,128,256]{2,1,0:T(8,128)}, f32[4,128,1]{2,1,0:T(8,128)}, bf16[4,128,256]{2,1,0:T(8,128)(2,1)}) custom-call(f32[4,128,512]{2,1,0:T(8,128)} %bitcast.175, f32[4,128,1]{2,1,0:T(8,128)} %get-tuple-element.158.behind, f32[4,128,1]{2,1,0:T(8,128)} %get-tuple-element.159.ahead, f32[31,256]{1,0:T(8,128)} %bitcast.212, ...), custom_call_target="tpu_custom_call" | custom-call | tf_op jit(solution)/shard_map/convolve/pallas_call | solution.py:1582
  154.0 2.4 convolution_convert_fusion.8
  156.4 23.7 %boundary.10 = (f32[128,1024]{1,0:T(8,128)}, bf16[4,128,1024]{2,1,0:T(8,128)(2,1)}) custom-call(bf16[4,128,1024]{2,1,0:T(8,128)(2,1)} %bitcast.174, f32[128,1024]{1,0:T(8,128)} %get-tuple-element.162.refs_1_.refs_2_, f32[19,1024]{1,0:T(8,128)} %get-tuple-element.143.refs_2_.refs_3_), custom_call_target="tpu_custom_call" | custom-call | tf_op jit(solution)/shard_map/boundary/pallas_call | solution.py:1346
  180.2 3.3 fusion.12
  183.6 2.3 convolution_convert_fusion.7
  185.9 24.7 %boundary.11 = (f32[128,1024]{1,0:T(8,128)}, f32[128,1024]{1,0:T(8,128)}, bf16[4,128,1024]{2,1,0:T(8,128)(2,1)}, f32[3,1024]{1,0:T(4,128)}) custom-call(bf16[4,128,1024]{2,1,0:T(8,128)(2,1)} %bitcast.207, f32[128,1024]{1,0:T(8,128)} %get-tuple-element.168.refs_1_.refs_2_, bf16[128,1024]{1,0:T(8,128)(2,1)} %refs_2_.4, ...), custom_call_target="tpu_custom_call" | custom-call | tf_op jit(solution)/shard_map/boundary/pallas_call | solution.py:1346
  210.6 4.4 %fusion.6 = (f32[1024]{0:T(1024)S(1)}, bf16[512,1024]{1,0:T(8,128)(2,1)S(1)}) fusion(f32[512,1024]{1,0:T(8,128)} %copy-done.33, f32[1024]{0:T(1024)S(1)} %bitcast.229, bf16[512,1024]{1,0:T(8,128)(2,1)} %bitcast.250, bf16[1024,1024]{1,0:T(8,128)(2,1)} %all-gather.11.cloned.1.call-done), kind=kOutput, calls=%fused_computation.61 | convolution fusion | flops 1079507968 | bytes 6299648 | tf_op jit(solution)/shard_map/dot_general | solution.py:39
  218.1 2.3 pad_maximum_fusion
  221.7 3.9 convolution_convert_fusion.6
  225.6 22.6 %boundary.12 = (f32[128,1024]{1,0:T(8,128)}, bf16[4,128,1024]{2,1,0:T(8,128)(2,1)}, f32[3,1024]{1,0:T(4,128)}) custom-call(bf16[4,128,1024]{2,1,0:T(8,128)(2,1)} %bitcast.203, f32[128,1024]{1,0:T(8,128)} %get-tuple-element.173.refs_1_, f32[128,1024]{1,0:T(8,128)} %get-tuple-element.168.refs_1_.refs_2_, f32[19,1024]{1,0:T(8,128)} %get-tuple-element.143.refs_2_.refs_3_), custom_call_target="tpu_custom_call" | custom-call | tf_op jit(solution)/shard_map/boundary/pallas_call | solution.py:1346
  250.4 2.5 fusion.5
  253.0 15.1 %unconvolve.1 = (bf16[4,128,512]{2,1,0:T(8,128)(2,1)}, f32[1,512]{1,0:T(1,128)}, f32[32,256]{1,0:T(8,128)}) custom-call(f32[4,128,512]{2,1,0:T(8,128)} %bitcast.176, f32[4,128,256]{2,1,0:T(8,128)} %get-tuple-element.170.gated, f32[4,128,256]{2,1,0:T(8,128)} %bitcast.211, f32[4,128,256]{2,1,0:T(8,128)} %get-tuple-element.175.unit, ...), custom_call_target="tpu_custom_call" | custom-call | tf_op jit(solution)/shard_map/unconvolve/pallas_call | solution.py:1657
  273.7 22.2 %boundary.13 = (f32[128,1024]{1,0:T(8,128)}, bf16[4,128,1024]{2,1,0:T(8,128)(2,1)}, f32[3,1024]{1,0:T(4,128)}) custom-call(bf16[4,128,1024]{2,1,0:T(8,128)(2,1)} %bitcast.202, f32[128,1024]{1,0:T(8,128)} %get-tuple-element.179.refs_1_, f32[128,1024]{1,0:T(8,128)} %get-tuple-element.162.refs_1_.refs_2_, f32[19,1024]{1,0:T(8,128)} %get-tuple-element.143.refs_2_.refs_3_), custom_call_target="tpu_custom_call" | custom-call | tf_op jit(solution)/shard_map/boundary/pallas_call | solution.py:1346
  295.9 2.5 convolution_convert_fusion.12
  298.3 12.0 %unattend.1 = (bf16[4,128,768]{2,1,0:T(8,128)(2,1)}, f32[2,256]{1,0:T(2,128)}, f32[4,256]{1,0:T(4,128)}) custom-call(bf16[4,128,768]{2,1,0:T(8,128)(2,1)} %bitcast.178, bf16[4,128,256]{2,1,0:T(8,128)(2,1)} %bitcast.215, f32[4,1,128]{2,1,0:T(1,128)} %get-tuple-element.149.segment_rows, f32[4,128,1]{2,1,0:T(8,128)} %get-tuple-element.150.segment_columns, ...), custom_call_target="tpu_custom_call" | custom-call | tf_op jit(solution)/shard_map/unattend/pallas_call | solution.py:1461
  318.1 22.1 %boundary.14 = (f32[128,1024]{1,0:T(8,128)}, bf16[4,128,1024]{2,1,0:T(8,128)(2,1)}, f32[3,1024]{1,0:T(4,128)}) custom-call(bf16[4,128,1024]{2,1,0:T(8,128)(2,1)} %bitcast.201, f32[128,1024]{1,0:T(8,128)} %get-tuple-element.184.refs_1_, f32[128,1024]{1,0:T(8,128)} %get-tuple-element.152.refs_1_.refs_2_, f32[19,1024]{1,0:T(8,128)} %get-tuple-element.143.refs_2_.refs_3_), custom_call_target="tpu_custom_call" | custom-call | tf_op jit(solution)/shard_map/boundary/pallas_call | solution.py:1346
  340.3 2.7 convolution_convert_fusion
  348.0 2.3 pad_maximum_fusion.1
  354.9 3.6 convolution_convert_fusion.5
  358.5 12.1 %boundary.15 = (f32[128,1024]{1,0:T(8,128)}, f32[2,1024]{1,0:T(2,128)}) custom-call(bf16[4,128,1024]{2,1,0:T(8,128)(2,1)} %bitcast.206, f32[128,1024]{1,0:T(8,128)} %get-tuple-element.187.refs_1_, bf16[128,1024]{1,0:T(8,128)(2,1)} %refs_2_.5, f32[19,1024]{1,0:T(8,128)} %get-tuple-element.143.refs_2_.refs_3_), custom_call_target="tpu_custom_call" | custom-call | tf_op jit(solution)/shard_map/boundary/pallas_call | solution.py:1346
  374.2 2.2 keep.1
  377.3 16.0 %collect.1 = (f32[32,5,128]{2,1,0:T(8,128)}, f32[8,11,128]{2,1,0:T(8,128)}, bf16[32,4096]{1,0:T(8,128)(2,1)}, bf16[32,3072]{1,0:T(8,128)(2,1)}, bf16[32,2048]{1,0:T(8,128)(2,1)}) custom-call(f32[32,5,128]{2,1,0:T(8,128)} %reshape.364.refs_0_, f32[8,11,128]{2,1,0:T(8,128)} %reshape.367.refs_1_, bf16[8,32,1024]{2,1,0:T(8,128)(2,1)} %reduce-scatter.5.cloned.1.call-done.refs_2_, ...), custom_call_target="tpu_custom_call" | custom-call | tf_op jit(solution)/shard_map/collect/pallas_call | solution.py:1091
  406.7 6.3 %giveback.1 = bf16[32,4096]{1,0:T(8,128)(2,1)} custom-call(bf16[8,32,1024]{2,1,0:T(8,128)(2,1)} %reduce-scatter.11.cloned.1.call-done.refs_0_), custom_call_target="tpu_custom_call" | custom-call | tf_op jit(solution)/shard_map/giveback/pallas_call | solution.py:1016
  (195 shorter events, 62.6 us)
Async XLA Ops:
  7.2 89.1 %all-gather.5.cloned.1.call-start = ((), (), s32[]{:S(2)}) async-start(), calls=%async_computation.4 | async-start | bytes 2359296 | tf_op jit(solution)/shard_map/all_gather | solution.py:1767
  59.3 77.1 %all-gather.7.cloned.1.call-start = ((), (), s32[]{:S(2)}) async-start(), calls=%async_computation.5 | async-start | bytes 1769472 | tf_op jit(solution)/shard_map/all_gather | solution.py:1768
  60.1 120.1 %all-gather.9.cloned.1.call-start = ((), (), s32[]{:S(2)}) async-start(), calls=%async_computation.6 | async-start | bytes 2359296 | tf_op jit(solution)/shard_map/all_gather | solution.py:1682
  60.8 119.4 %all-gather.11.cloned.1.call-start = ((), (), s32[]{:S(2)}) async-start(), calls=%async_computation.7 | async-start | bytes 2359296 | tf_op jit(solution)/shard_map/all_gather | solution.py:1678
  61.4 256.6 %reduce-scatter.5.cloned.1.call-start = ((), (), s32[]{:S(2)}) async-start(), calls=%async_computation.8 | async-start | bytes 4718592 | tf_op jit(solution)/shard_map/reduce_scatter | solution.py:1828
  64.0 3.6 copy-start.18
  67.5 2.3 copy-start.30
  97.8 4.8 %copy-start.2 = (bf16[4,256,768]{2,1,0:T(8,128)(2,1)}, bf16[4,256,768]{2,1,0:T(8,128)(2,1)S(1)}, u32[]{:S(2)}) copy-start(bf16[4,256,768]{2,1,0:T(8,128)(2,1)S(1)} %slice.164) | copy-start | bytes 4718596
  136.5 3.0 copy-start.29
  137.8 4.6 %copy-start.6 = (bf16[4,256,512]{2,1,0:T(8,128)(2,1)}, bf16[4,256,512]{2,1,0:T(8,128)(2,1)S(1)}, u32[]{:S(2)}) copy-start(bf16[4,256,512]{2,1,0:T(8,128)(2,1)S(1)} %slice.168) | copy-start | bytes 3145732
  180.2 3.3 copy-start.20
  183.5 2.3 copy-start.33
  210.6 4.5 %copy-start.26 = (bf16[4,128,1024]{2,1,0:T(8,128)(2,1)S(1)}, bf16[4,128,1024]{2,1,0:T(8,128)(2,1)}, u32[]{:S(2)}) copy-start(bf16[4,128,1024]{2,1,0:T(8,128)(2,1)} %get-tuple-element.171) | copy-start | bytes 3145732
  210.6 4.5 %copy-start.34 = (f32[512,1024]{1,0:T(8,128)S(1)}, f32[512,1024]{1,0:T(8,128)}, u32[]{:S(2)}) copy-start(f32[512,1024]{1,0:T(8,128)} %copy-done.33) | copy-start | bytes 6291460
  220.5 129.9 %reduce-scatter.9.cloned.1.call-start = ((), (), s32[]{:S(2)}) async-start(), calls=%async_computation.10 | async-start | bytes 1769472 | tf_op jit(solution)/shard_map/reduce_scatter | solution.py:1846
  225.6 22.6 %copy-start.4 = (bf16[4,128,256]{2,1,0:T(8,128)(2,1)S(1)}, bf16[4,128,256]{2,1,0:T(8,128)(2,1)}, u32[]{:S(2)}) copy-start(bf16[4,128,256]{2,1,0:T(8,128)(2,1)} %get-tuple-element.161) | copy-start | bytes 786436
  253.0 15.1 %copy-start.23 = (bf16[4,128,1024]{2,1,0:T(8,128)(2,1)S(1)}, bf16[4,128,1024]{2,1,0:T(8,128)(2,1)}, u32[]{:S(2)}) copy-start(bf16[4,128,1024]{2,1,0:T(8,128)(2,1)} %get-tuple-element.155) | copy-start | bytes 3145732
  273.6 103.7 %reduce-scatter.7.cloned.1.call-start = ((), (), s32[]{:S(2)}) async-start(), calls=%async_computation.9 | async-start | bytes 2359296 | tf_op jit(solution)/shard_map/reduce_scatter | solution.py:1860
  295.9 14.5 %copy-start = (bf16[4,128,256]{2,1,0:T(8,128)(2,1)S(1)}, bf16[4,128,256]{2,1,0:T(8,128)(2,1)}, u32[]{:S(2)}) copy-start(bf16[4,128,256]{2,1,0:T(8,128)(2,1)} %attend.1) | copy-start | bytes 786436
  295.9 14.4 %copy-start.5 = (bf16[4,128,1024]{2,1,0:T(8,128)(2,1)S(1)}, bf16[4,128,1024]{2,1,0:T(8,128)(2,1)}, u32[]{:S(2)}) copy-start(bf16[4,128,1024]{2,1,0:T(8,128)(2,1)} %get-tuple-element.180) | copy-start | bytes 3145732
  313.7 2.4 copy-start.27
  318.0 22.2 %copy-start.31 = (f32[512,1024]{1,0:T(8,128)S(1)}, f32[512,1024]{1,0:T(8,128)}, u32[]{:S(2)}) copy-start(f32[512,1024]{1,0:T(8,128)} %copy-done.30) | copy-start | bytes 6291460
  318.1 87.6 %reduce-scatter.11.cloned.1.call-start = ((), (), s32[]{:S(2)}) async-start(), calls=%async_computation.11 | async-start | bytes 4718592 | tf_op jit(solution)/shard_map/reduce_scatter | solution.py:1868
  340.3 2.9 copy-start.32
  350.3 2.6 copy-start.16
  350.3 4.6 %copy-start.17 = (bf16[32,32,1024]{2,1,0:T(8,128)(2,1)S(1)}, bf16[32,32,1024]{2,1,0:T(8,128)(2,1)}, u32[]{:S(2)}) copy-start(bf16[32,32,1024]{2,1,0:T(8,128)(2,1)} %get-tuple-element.140) | copy-start | bytes 6291460
  354.9 15.7 %copy-start.10 = (f32[3,1024]{1,0:T(4,128)S(1)}, f32[3,1024]{1,0:T(4,128)}, u32[]{:S(2)}) copy-start(f32[3,1024]{1,0:T(4,128)} %get-tuple-element.191) | copy-start | bytes 36868
  354.9 15.7 %copy-start.11 = (f32[3,1024]{1,0:T(4,128)S(1)}, f32[3,1024]{1,0:T(4,128)}, u32[]{:S(2)}) copy-start(f32[3,1024]{1,0:T(4,128)} %get-tuple-element.192) | copy-start | bytes 36868
  354.9 15.7 %copy-start.12 = (f32[3,1024]{1,0:T(4,128)S(1)}, f32[3,1024]{1,0:T(4,128)}, u32[]{:S(2)}) copy-start(f32[3,1024]{1,0:T(4,128)} %get-tuple-element.193) | copy-start | bytes 36868
  354.9 15.7 %copy-start.13 = (f32[3,1024]{1,0:T(4,128)S(1)}, f32[3,1024]{1,0:T(4,128)}, u32[]{:S(2)}) copy-start(f32[3,1024]{1,0:T(4,128)} %get-tuple-element.194) | copy-start | bytes 36868
  370.6 5.8 %slice-start = ((bf16[8,32,1024]{2,1,0:T(8,128)(2,1)}), bf16[4,32,1024]{2,1,0:T(8,128)(2,1)S(1)}, s32[]{:S(2)}) async-start(bf16[8,32,1024]{2,1,0:T(8,128)(2,1)} %reduce-scatter.5.cloned.1.call-done.refs_2_), calls=%async_computation.12 | async-start | bytes 524288 | tf_op jit(solution)/shard_map/slice | solution.py:1947
  393.3 7.2 %copy-start.8 = (f32[8,11,128]{2,1,0:T(8,128)S(1)}, f32[8,11,128]{2,1,0:T(8,128)}, u32[]{:S(2)}) copy-start(f32[8,11,128]{2,1,0:T(8,128)} %get-tuple-element.206) | copy-start | bytes 135172
  (15 other events, 22.3 us)
Sparse Core Ops, SparseCore 0:
  59.5 27.0 all-gather.4
  88.2 24.6 all-gather.6
  114.5 28.3 all-gather.8
  144.4 28.5 all-gather.10
  220.6 48.4 reduce-scatter.4
  273.7 32.8 reduce-scatter.8
  318.2 34.7 reduce-scatter.6
  355.3 50.3 reduce-scatter.10
